TPU v7x, 256 devices: a whole 4x4x8 slice. The times are simulated.
256 devices in a mesh: node: 64 (over z, x, core), site: 4 (over y).
Axes of the slice: x: 4, y: 4, z: 8, core: 2. Of those that a mesh axis runs over, the one named last changes fastest.
Arguments:
- leaf_partials: float32 [4096, 4, 4096], P('node', None, 'site'), may hold values from 0.05 to 1
- dag_edges: int32 [3, 12288, 3], P(None, 'node'), may hold values from 0 to 4095, as said below
- weights: float32 [3, 12288], P(None, 'node'), may hold values from 0.25 to 4
- lengths: float32 [3, 12288], P(None, 'node'), may hold values from 0.02 to 2
- counts: int32 [4096], P('site'), may hold values from 1 to 9
- topo_nodes: int32 [256, 8], P('node'), may hold values from 0 to 4095
Outputs:
- topology_loglik: float32 [256], P('node')
- edge_gradient: float32 [12288], P('node')
Inputs may be any that keep to these rules, and one draw needn't show every extreme that they name: `dag_edges`: in every level each subsplit is the child of exactly 3 edges, listed on the index of node that owns the child; subsplit n is owned by index n // 64. Column 1 is the parent in the next level, column 2 the rotation (0 or 1). Every parent has at least one edge of each rotation. Among the edges of one index of node, at most 4 have parents owned by any one index, and some index receives exactly 4 from every index.
All inputs are finite; a program needn't handle non-finite values.
Results may differ from a plain program's by a relative error of at most 0.0003.
Values sent between devices are 32-bit elements; how exact they have to be, the bound alone decides.
No kernel may reach another device: no remote copies, remote signals or barrier semaphores. Data moves between devices by JAX's collectives and lax.ppermute only.
A program may use at most 192 MiB of HBM per device.

v0:
```python
import jax
import jax.numpy as jnp
from jax import lax
from jax.sharding import PartitionSpec as P


def transit(child_rows, branch):
    survival = jnp.exp(branch * (-4.0 / 3.0))[:, None, None]
    return survival * child_rows + (1.0 - survival) * 0.25 * jnp.sum(
        child_rows, axis=1, keepdims=True
    )


def on_device(leaf_partials, dag_edges, weights, lengths, counts, topo_nodes):
    node_dev, states, site_dev = leaf_partials.shape
    level_count, edge_dev = (dag_edges.shape[0], dag_edges.shape[1])
    owners = lax.axis_size("node")
    device = lax.axis_index("node")
    nodes_all = node_dev * owners
    sites_all = site_dev * lax.axis_size("site")
    scaled = counts.astype(jnp.float32) / sites_all
    incidence = lax.all_gather(topo_nodes, "node", axis=0, tiled=True)
    multiplicity = jax.ops.segment_sum(
        jnp.ones((incidence.size,), jnp.float32), incidence.reshape(-1), num_segments=nodes_all
    )
    capacity = 4 * node_dev // owners
    slots_all = owners * capacity
    current = leaf_partials
    for level_index in range(level_count):
        child_index = dag_edges[level_index, :, 0] - device * node_dev
        parents = dag_edges[level_index, :, 1]
        rotation = dag_edges[level_index, :, 2]
        message = transit(current[child_index], lengths[level_index])
        owner_dev = parents // node_dev
        one_hot = (owner_dev[:, None] == jnp.arange(owners)[None, :]).astype(jnp.int32)
        slot_rank = jnp.sum((jnp.cumsum(one_hot, axis=0) - one_hot) * one_hot, axis=1)
        slot_index = owner_dev * capacity + slot_rank
        pair_code = ((parents - owner_dev * node_dev) * 2 + rotation).astype(jnp.float32)
        buffer = jnp.zeros((slots_all, states, site_dev), jnp.float32).at[slot_index].set(message)
        code_buffer = jnp.full((slots_all,), -1.0, jnp.float32).at[slot_index].set(pair_code)
        weight_buffer = (
            jnp.zeros((slots_all,), jnp.float32).at[slot_index].set(weights[level_index])
        )
        received, received_codes, received_weights = (
            lax.all_to_all(
                buffer.reshape(owners, capacity, states, site_dev),
                "node",
                split_axis=0,
                concat_axis=0,
                tiled=True,
            ),
            lax.all_to_all(
                code_buffer.reshape(owners, capacity),
                "node",
                split_axis=0,
                concat_axis=0,
                tiled=True,
            ),
            lax.all_to_all(
                weight_buffer.reshape(owners, capacity),
                "node",
                split_axis=0,
                concat_axis=0,
                tiled=True,
            ),
        )
        flat_rows = received.reshape(slots_all, states * site_dev)
        selector = (
            received_codes.reshape(-1).astype(jnp.int32)[None, :]
            == jnp.arange(2 * node_dev)[:, None]
        ).astype(jnp.float32)
        summed = jnp.dot(
            selector * received_weights.reshape(-1)[None, :],
            flat_rows,
            precision=lax.Precision.HIGHEST,
            preferred_element_type=jnp.float32,
        )
        pair_sums = summed.reshape(node_dev, 2, states, site_dev)
        current = pair_sums[:, 0] * pair_sums[:, 1]
    denominator = 0.25 * jnp.sum(current, axis=1)
    node_part = jnp.sum(scaled[None, :] * jnp.log(denominator), axis=1)
    adjoint = pair_sums[:, ::-1] * (scaled[None, :] * 0.25 / denominator)[:, None, None, :]
    adjoint_slots = jnp.dot(
        selector.T,
        adjoint.reshape(2 * node_dev, states * site_dev),
        precision=lax.Precision.HIGHEST,
        preferred_element_type=jnp.float32,
    )
    grad_part = jnp.sum(flat_rows * adjoint_slots, axis=1)
    node_scores, slot_grads = lax.psum((node_part, grad_part), "site")
    own_mult = lax.dynamic_slice_in_dim(multiplicity, device * node_dev, node_dev)
    pair_mult = jnp.repeat(own_mult, 2)
    slot_mult = jnp.dot(
        selector.T, pair_mult, precision=lax.Precision.HIGHEST, preferred_element_type=jnp.float32
    )
    returned = lax.all_to_all(
        (slot_grads * slot_mult).reshape(owners, capacity),
        "node",
        split_axis=0,
        concat_axis=0,
        tiled=True,
    )
    edge_gradient = returned.reshape(-1)[slot_index]
    score_table = lax.all_gather(node_scores, "node", axis=0, tiled=True)
    topology_loglik = jnp.sum(score_table[topo_nodes], axis=1)
    return (topology_loglik, edge_gradient)


def solution(mesh):
    return jax.shard_map(
        on_device,
        mesh=mesh,
        in_specs=(
            P("node", None, "site"),
            P(None, "node", None),
            P(None, "node"),
            P(None, "node"),
            P("site"),
            P("node", None),
        ),
        out_specs=(P("node"), P("node")),
        check_vma=False,
    )
```

profile of v0, /device:TPU:2, one launch (start us, length us, event | category | flops | bytes accessed | tf_op | source)
XLA Modules:
  0.0 900.4 jit_solution(11495351797183941422)
XLA Ops:
  7.3 12.0 %all-to-all-start.4 = ((f32[64,1,4]{2,1,0:T(1,128)}), f32[64,1,4]{2,1,0:T(1,128)S(1)}, u32[]{:S(2)}, u32[]{:S(2)}) async-start(f32[64,1,4]{2,1,0:T(1,128)} %bitcast.30), calls=%async_computation.4 | async-start | bytes 65536 | tf_op jit(solution)/shard_map/all_to_all | solution.py:52
  20.2 4.1 gather_fusion
  30.2 10.3 %all-to-all-start.5 = ((f32[64,1,4]{2,1,0:T(1,128)}), f32[64,1,4]{2,1,0:T(1,128)S(1)}, u32[]{:S(2)}, u32[]{:S(2)}) async-start(f32[64,1,4]{2,1,0:T(1,128)} %bitcast.32), calls=%async_computation.5 | async-start | bytes 65536 | tf_op jit(solution)/shard_map/all_to_all | solution.py:59
  47.3 26.2 %scatter_fusion = f32[256,4,1024]{2,1,0:T(4,128)} fusion(f32[256,4,1024]{2,1,0:T(4,128)} %broadcast.594.clone.1, s32[192]{0:T(256)S(1)} %bitcast.186, f32[192,4,1024]{2,1,0:T(4,128)} %multiply_add_fusion.2), kind=kCustom, calls=%fused_computation.11 | custom fusion | bytes 9437952 | tf_op jit(solution)/shard_map/scatter | solution.py:39
  73.5 10.8 %all-to-all-start.6 = ((f32[64,4,4,1024]{3,2,1,0:T(4,128)}), f32[64,4,4,1024]{3,2,1,0:T(4,128)}, u32[]{:S(2)}, u32[]{:S(2)}) async-start(f32[64,4,4,1024]{3,2,1,0:T(4,128)} %bitcast.159), calls=%async_computation.6 | async-start | bytes 8388608 | tf_op jit(solution)/shard_map/all_to_all | solution.py:45
  89.7 90.5 %all-to-all-done.6 = f32[64,4,4,1024]{3,2,1,0:T(4,128)} async-done(((f32[64,4,4,1024]{3,2,1,0:T(4,128)}), f32[64,4,4,1024]{3,2,1,0:T(4,128)}, u32[]{:S(2)}, u32[]{:S(2)}) %all-to-all-start.6) | async-done | bytes 4194336 | tf_op jit(solution)/shard_map/all_to_all | solution.py:45
  180.2 5.4 all-to-all-start.2
  185.7 8.0 copy.51
  193.6 5.8 copy.35
  199.4 6.6 fusion.4
  206.8 4.1 gather_fusion.1
  214.9 10.3 %all-to-all-start.3 = ((f32[64,1,4]{2,1,0:T(1,128)}), f32[64,1,4]{2,1,0:T(1,128)S(1)}, u32[]{:S(2)}, u32[]{:S(2)}) async-start(f32[64,1,4]{2,1,0:T(1,128)} %bitcast.20), calls=%async_computation.3 | async-start | bytes 65536 | tf_op jit(solution)/shard_map/all_to_all | solution.py:59
  232.0 26.1 %scatter_fusion.1 = f32[256,4,1024]{2,1,0:T(4,128)} fusion(f32[256,4,1024]{2,1,0:T(4,128)} %broadcast.594.clone, s32[192]{0:T(256)S(1)} %bitcast.182, f32[192,4,1024]{2,1,0:T(4,128)} %multiply_add_fusion.1), kind=kCustom, calls=%fused_computation.12 | custom fusion | bytes 9437952 | tf_op jit(solution)/shard_map/scatter | solution.py:39
  258.1 11.1 %all-to-all-start.7 = ((f32[64,4,4,1024]{3,2,1,0:T(4,128)}), f32[64,4,4,1024]{3,2,1,0:T(4,128)}, u32[]{:S(2)}, u32[]{:S(2)}) async-start(f32[64,4,4,1024]{3,2,1,0:T(4,128)} %bitcast.160), calls=%async_computation.7 | async-start | bytes 8388608 | tf_op jit(solution)/shard_map/all_to_all | solution.py:45
  274.1 91.0 %all-to-all-done.7 = f32[64,4,4,1024]{3,2,1,0:T(4,128)} async-done(((f32[64,4,4,1024]{3,2,1,0:T(4,128)}), f32[64,4,4,1024]{3,2,1,0:T(4,128)}, u32[]{:S(2)}, u32[]{:S(2)}) %all-to-all-start.7) | async-done | bytes 4194336 | tf_op jit(solution)/shard_map/all_to_all | solution.py:45
  365.2 5.4 all-to-all-start
  370.6 8.0 copy.52
  378.6 5.7 copy.37
  384.3 6.6 fusion.6
  391.7 4.1 gather_fusion.2
  399.8 10.3 %all-to-all-start.1 = ((f32[64,1,4]{2,1,0:T(1,128)}), f32[64,1,4]{2,1,0:T(1,128)S(1)}, u32[]{:S(2)}, u32[]{:S(2)}) async-start(f32[64,1,4]{2,1,0:T(1,128)} %bitcast.8), calls=%async_computation.1 | async-start | bytes 65536 | tf_op jit(solution)/shard_map/all_to_all | solution.py:59
  410.1 3.8 multiply_add_fusion
  416.9 26.2 %scatter_fusion.2 = f32[256,4,1024]{2,1,0:T(4,128)} fusion(f32[256,4,1024]{2,1,0:T(4,128)} %broadcast.594, s32[192]{0:T(256)S(1)} %bitcast.171, f32[192,4,1024]{2,1,0:T(4,128)} %multiply_add_fusion), kind=kCustom, calls=%fused_computation.13 | custom fusion | bytes 9437952 | tf_op jit(solution)/shard_map/scatter | solution.py:39
  443.1 10.6 %all-to-all-start.8 = ((f32[64,4,4,1024]{3,2,1,0:T(4,128)}), f32[64,4,4,1024]{3,2,1,0:T(4,128)}, u32[]{:S(2)}, u32[]{:S(2)}) async-start(f32[64,4,4,1024]{3,2,1,0:T(4,128)} %bitcast.161), calls=%async_computation.8 | async-start | bytes 8388608 | tf_op jit(solution)/shard_map/all_to_all | solution.py:45
  453.7 135.0 %all-gather = s32[64,4,8]{2,1,0:T(4,128)S(1)} all-gather(s32[1,4,8]{2,1,0:T(4,128)S(1)} %bitcast.179), channel_id=1, replica_groups=mesh['node'=64,'site'=4] {'node'}, dimensions={0}, use_global_device_ids=true | all-gather | bytes 8320 | tf_op jit(solution)/shard_map/all_gather | solution.py:22
  588.8 11.2 %scatter_custom_fusion.9 = f32[4096]{0:T(1024)S(1)} fusion(s32[2048]{0:T(1024)S(1)} %reshape.800, f32[2048]{0:T(1024)S(1)} %broadcast.600, f32[]{:T(128)} %constant.79.clone.1), kind=kCustom, calls=%fused_computation.94 | custom fusion | flops 2048 | bytes 16388 | tf_op jit(solution)/shard_map/scatter-add | solution.py:23
  603.0 8.0 copy.53
  611.0 5.6 copy.39
  616.6 6.6 fusion.8
  629.8 10.7 %all-reduce.4 = (f32[64]{0:T(128)S(1)}, f32[256]{0:T(256)S(1)}) all-reduce(f32[64]{0:T(128)S(1)} %get-tuple-element.11, f32[256]{0:T(256)S(1)} %fusion), channel_id=1, replica_groups=mesh['node'=64,'site'=4] {'site'}, use_global_device_ids=true, to_apply=%region_23.24 | all-reduce | flops 320 | bytes 2560 | tf_op jit(solution)/shard_map/psum | solution.py:90
  641.3 8.1 all-to-all-start.9
  649.7 245.9 %all-reduce.3 = f32[4096]{0:T(1024)S(1)} all-reduce(f32[4096]{0:T(1024)S(1)} %dynamic-update-slice), channel_id=1, replica_groups=mesh['node'=64,'site'=4] {'node'}, use_global_device_ids=true, to_apply=%add.3 | all-reduce | flops 4096 | bytes 32768
  (128 shorter events, 63.9 us)
Async XLA Ops:
  0.6 19.6 %copy-start = (f32[64,4,1024]{2,1,0:T(4,128)S(1)}, f32[64,4,1024]{2,1,0:T(4,128)}, u32[]{:S(2)}) copy-start(f32[64,4,1024]{2,1,0:T(4,128)} %param.6) | copy-start | bytes 3145732
  7.3 22.8 %all-to-all-start.4 = ((f32[64,1,4]{2,1,0:T(1,128)}), f32[64,1,4]{2,1,0:T(1,128)S(1)}, u32[]{:S(2)}, u32[]{:S(2)}) async-start(f32[64,1,4]{2,1,0:T(1,128)} %bitcast.30), calls=%async_computation.4 | async-start | bytes 65536 | tf_op jit(solution)/shard_map/all_to_all | solution.py:52
  24.3 3.9 copy-start.5
  30.2 43.3 %all-to-all-start.5 = ((f32[64,1,4]{2,1,0:T(1,128)}), f32[64,1,4]{2,1,0:T(1,128)S(1)}, u32[]{:S(2)}, u32[]{:S(2)}) async-start(f32[64,1,4]{2,1,0:T(1,128)} %bitcast.32), calls=%async_computation.5 | async-start | bytes 65536 | tf_op jit(solution)/shard_map/all_to_all | solution.py:59
  73.5 106.8 %all-to-all-start.6 = ((f32[64,4,4,1024]{3,2,1,0:T(4,128)}), f32[64,4,4,1024]{3,2,1,0:T(4,128)}, u32[]{:S(2)}, u32[]{:S(2)}) async-start(f32[64,4,4,1024]{3,2,1,0:T(4,128)} %bitcast.159), calls=%async_computation.6 | async-start | bytes 8388608 | tf_op jit(solution)/shard_map/all_to_all | solution.py:45
  180.2 34.6 %all-to-all-start.2 = ((f32[64,1,4]{2,1,0:T(1,128)}), f32[64,1,4]{2,1,0:T(1,128)S(1)}, u32[]{:S(2)}, u32[]{:S(2)}) async-start(f32[64,1,4]{2,1,0:T(1,128)} %bitcast.18), calls=%async_computation.2 | async-start | bytes 65536 | tf_op jit(solution)/shard_map/all_to_all | solution.py:52
  214.9 43.3 %all-to-all-start.3 = ((f32[64,1,4]{2,1,0:T(1,128)}), f32[64,1,4]{2,1,0:T(1,128)S(1)}, u32[]{:S(2)}, u32[]{:S(2)}) async-start(f32[64,1,4]{2,1,0:T(1,128)} %bitcast.20), calls=%async_computation.3 | async-start | bytes 65536 | tf_op jit(solution)/shard_map/all_to_all | solution.py:59
  258.1 107.0 %all-to-all-start.7 = ((f32[64,4,4,1024]{3,2,1,0:T(4,128)}), f32[64,4,4,1024]{3,2,1,0:T(4,128)}, u32[]{:S(2)}, u32[]{:S(2)}) async-start(f32[64,4,4,1024]{3,2,1,0:T(4,128)} %bitcast.160), calls=%async_computation.7 | async-start | bytes 8388608 | tf_op jit(solution)/shard_map/all_to_all | solution.py:45
  365.2 34.6 %all-to-all-start = ((f32[64,1,4]{2,1,0:T(1,128)}), f32[64,1,4]{2,1,0:T(1,128)S(1)}, u32[]{:S(2)}, u32[]{:S(2)}) async-start(f32[64,1,4]{2,1,0:T(1,128)} %bitcast.6), calls=%async_computation | async-start | bytes 65536 | tf_op jit(solution)/shard_map/all_to_all | solution.py:52
  399.8 43.4 %all-to-all-start.1 = ((f32[64,1,4]{2,1,0:T(1,128)}), f32[64,1,4]{2,1,0:T(1,128)S(1)}, u32[]{:S(2)}, u32[]{:S(2)}) async-start(f32[64,1,4]{2,1,0:T(1,128)} %bitcast.8), calls=%async_computation.1 | async-start | bytes 65536 | tf_op jit(solution)/shard_map/all_to_all | solution.py:59
  443.1 10.6 %copy-start.3 = (s32[4,8]{1,0:T(4,128)S(1)}, s32[4,8]{1,0:T(4,128)}, u32[]{:S(2)}) copy-start(s32[4,8]{1,0:T(4,128)} %param.11) | copy-start | bytes 388
  443.1 157.4 %copy-start.6 = (u32[256]{0:T(256)S(1)}, u32[256]{0:T(256)}, u32[]{:S(2)}) copy-start(u32[256]{0:T(256)} %constant.96) | copy-start | bytes 3076
  443.1 158.7 %copy-start.4 = (s32[1024]{0:T(1024)S(1)}, s32[1024]{0:T(1024)}, u32[]{:S(2)}) copy-start(s32[1024]{0:T(1024)} %param.10) | copy-start | bytes 12292
  443.1 159.9 %all-to-all-start.8 = ((f32[64,4,4,1024]{3,2,1,0:T(4,128)}), f32[64,4,4,1024]{3,2,1,0:T(4,128)}, u32[]{:S(2)}, u32[]{:S(2)}) async-start(f32[64,4,4,1024]{3,2,1,0:T(4,128)} %bitcast.161), calls=%async_computation.8 | async-start | bytes 8388608 | tf_op jit(solution)/shard_map/all_to_all | solution.py:45
  625.2 2.2 copy-start.2
  627.4 272.6 %copy-start.1 = (f32[64,4,1024]{2,1,0:T(4,128)S(1)}, f32[64,4,1024]{2,1,0:T(4,128)}, u32[]{:S(2)}) copy-start(f32[64,4,1024]{2,1,0:T(4,128)} %param.6) | copy-start | bytes 3145732
  641.3 255.7 %all-to-all-start.9 = ((f32[64,1,4]{2,1,0:T(1,128)}), f32[64,1,4]{2,1,0:T(1,128)S(1)}, u32[]{:S(2)}, u32[]{:S(2)}) async-start(f32[64,1,4]{2,1,0:T(1,128)} %bitcast.59), calls=%async_computation.9 | async-start | bytes 65536 | tf_op jit(solution)/shard_map/all_to_all | solution.py:96
where the time goes:
time: 914 us; the launch traced here: 900 us
  blocking collectives  392 us (43%)
  waiting for transfers between devices  182 us (20%)
  local copies, waits for them, and re-layouts  165 us (18%)
  starting transfers between devices  94.5 us (10%)
  other arithmetic  43.2 us (5%)
  matrix products  22.3 us (2%)
    unnamed x1, blocking collectives  246 us
    all_to_all x3, waiting for transfers between devices, on_device(): lax.all_to_all(buffer.reshape(owners, capacity, states, site_dev), 'node'...  182 us
    all_gather x1, blocking collectives, on_device(): incidence = lax.all_gather(topo_nodes, 'node', axis=0, tiled=True)  135 us
    scatter x3, local copies, waits for them, and re-layouts, on_device(): jnp.zeros((slots_all, states, site_dev), jnp.float32).at[slot_index]  78.6 us
    all_to_all x3, starting transfers between devices, on_device(): lax.all_to_all(buffer.reshape(owners, capacity, states, site_dev), 'node'...  32.5 us
    all_to_all x3, starting transfers between devices, on_device(): lax.all_to_all(weight_buffer.reshape(owners, capacity), 'node', split_axi...  30.9 us
    unnamed x21, local copies, waits for them, and re-layouts  26.9 us
    all_to_all x3, starting transfers between devices, on_device(): lax.all_to_all(code_buffer.reshape(owners, capacity), 'node', split_axis=...  22.9 us
  transfers between devices with their start and end apart: 10, of which 2 were waited for; matrix products, arithmetic and copies ran while one was open for 21% of the time, Pallas kernels for 0%

commit v1 on v0

v1 whole, which is shorter than its diff:
```python
import functools

import jax
import jax.numpy as jnp
from jax import lax
from jax.experimental import pallas as pl
from jax.experimental.pallas import tpu as pltpu
from jax.sharding import PartitionSpec as P

F32 = jnp.float32
BF16 = jnp.bfloat16
LANES = 128


def spread_kernel(leaf_ref, out_ref):
    states = leaf_ref.shape[1]
    for pair in range(states // 2):
        rows = jnp.concatenate([leaf_ref[:, 2 * pair, :], leaf_ref[:, 2 * pair + 1, :]], axis=0)
        out_ref[:, pair * LANES : (pair + 1) * LANES] = rows.T


def two_parts(value):
    high = value.astype(BF16)
    return high, (value - high.astype(F32)).astype(BF16)


def state_sum(value):
    value = value + pltpu.roll(value, 16, 1)
    return value + pltpu.roll(value, 32, 1)


def dag_kernel(
    leaf_ref, meta_ref, topo_ref, scaled_ref, out_ref,
    current_ref, slot_ref, table_ref, score_ref, mult_ref, term_ref,
    *, levels, owners, node_dev, site_own, states, fields,
):
    half = 2 * node_dev
    slots = 4 * owners
    meta_rows = fields * levels * 2
    left = lax.broadcasted_iota(jnp.int32, (LANES, LANES), 1) < LANES // 2
    left_nodes = left[:node_dev]

    def store_current(start, value, mask):
        high = value.astype(BF16).astype(F32)
        current_ref[pl.ds(start, value.shape[0]), :] = jnp.where(
            mask, high, value - high
        ).astype(BF16)

    for level in range(levels):
        for field in range(1, fields):
            for part in range(2):
                row = (field * levels + level) * 2 + part
                block = meta_ref[pl.ds(row, owners, stride=meta_rows), :].T
                table_ref[
                    pl.ds((level * (fields - 1) + field - 1) * owners, owners),
                    part * LANES : (part + 1) * LANES,
                ] = jnp.concatenate([block[:owners], block[owners:]], axis=1)

    def count_uses(chunk, total):
        entry = topo_ref[pl.ds(chunk, 1), :]
        owner_of = entry // node_dev
        local_of = entry - owner_of * node_dev
        owner_hot = (lax.broadcasted_iota(jnp.int32, (LANES, LANES), 0) == owner_of).astype(F32)
        local_hot = (lax.broadcasted_iota(jnp.int32, (node_dev, LANES), 0) == local_of).astype(F32)
        return total + lax.dot_general(
            local_hot.astype(BF16), owner_hot.astype(BF16), (((1,), (1,)), ((), ())),
            preferred_element_type=F32,
        )

    mult_ref[...] = lax.fori_loop(
        0, topo_ref.shape[0], count_uses, jnp.zeros((node_dev, LANES), F32)
    )

    def load_leaves(pair, carry):
        first = leaf_ref[pl.ds(pl.multiple_of(pair * 2 * site_own, 2 * site_own), site_own), :]
        second = leaf_ref[
            pl.ds(pl.multiple_of(pair * 2 * site_own, 2 * site_own) + site_own, site_own), :
        ]
        pieces = []
        for block in range(states // 2):
            a = first[:, block * LANES : (block + 1) * LANES]
            b = second[:, block * LANES : (block + 1) * LANES]
            pieces.append(jnp.where(left[:site_own], a, pltpu.roll(b, LANES // 2, 1)))
            pieces.append(jnp.where(left[:site_own], pltpu.roll(a, LANES // 2, 1), b))
        stacked = jnp.concatenate(pieces + pieces, axis=0)
        store_current(pl.multiple_of(pair * LANES, LANES), stacked.T, left)
        return carry

    lax.fori_loop(0, owners // 2, load_leaves, 0)

    node_row = lax.broadcasted_iota(jnp.int32, (node_dev, LANES), 0).astype(F32) + 1.0
    pair_row = lax.broadcasted_iota(jnp.int32, (half, slots), 0).astype(F32) + 1.0

    def spread(level):
        def body(source, carry):
            rows = current_ref[pl.ds(pl.multiple_of(source * node_dev, node_dev), node_dev), :]
            for part in range(2):
                child = meta_ref[pl.ds(source * meta_rows + level * 2 + part, 1), :]
                hot = (node_row == child).astype(F32).astype(BF16)
                picked = lax.dot_general(
                    hot, rows, (((0,), (0,)), ((), ())), preferred_element_type=F32
                )
                slot_ref[pl.ds(part * half * owners + source, half, stride=owners), :] = picked
            return carry

        lax.fori_loop(0, owners, body, 0, unroll=4)

    def gather(level, last):
        def body(dest, carry):
            pieces = [
                slot_ref[pl.ds(pl.multiple_of((rank * owners + dest) * owners, owners), owners), :]
                for rank in range(4)
            ]
            rows = jnp.concatenate(pieces, axis=0).astype(BF16)
            base = level * (fields - 1) * owners + dest
            code = table_ref[pl.ds(base, 1), :]
            weight = table_ref[pl.ds(base + owners, 1), :]
            survival = table_ref[pl.ds(base + 2 * owners, 1), :]
            spread_out = (1.0 - survival) * 0.25
            hit = pair_row == code

            def weighted(scale):
                high = scale.astype(BF16).astype(F32)
                low = scale - high
                return sum(
                    jnp.dot(
                        jnp.where(hit, piece, 0.0).astype(BF16), rows, preferred_element_type=F32
                    )
                    for piece in (high, low)
                )

            sums = weighted(weight * survival) + state_sum(weighted(weight * spread_out))
            sums = sums + pltpu.roll(sums, LANES // 2, 1)
            value = sums[:node_dev] * sums[node_dev:]
            if not last:
                store_current(pl.multiple_of(dest * node_dev, node_dev), value, left_nodes)
                return carry
            scaled = scaled_ref[...]
            likelihood = 0.25 * state_sum(value)
            lane = lax.broadcasted_iota(jnp.int32, (node_dev, LANES), 1)
            logs = scaled * jnp.log(likelihood)
            high = logs.astype(BF16).astype(F32)
            middle = (logs - high).astype(BF16).astype(F32)
            packed = jnp.where(
                lane < site_own, high,
                jnp.where(
                    lane < 2 * site_own, middle,
                    jnp.where(lane < 3 * site_own, logs - high - middle, 0.0),
                ),
            )
            score_ref[pl.ds(dest, 1), :] = lax.dot_general(
                jnp.ones((8, LANES), BF16), packed.astype(BF16), (((1,), (1,)), ((), ())),
                preferred_element_type=F32,
            )[:1]
            times = jnp.sum(jnp.where(lane == dest, mult_ref[...], 0.0), axis=1, keepdims=True)
            factor = scaled * 0.25 / likelihood * times
            adjoint = jnp.concatenate([sums[node_dev:] * factor, sums[:node_dev] * factor], axis=0)

            def against(value):
                return sum(
                    lax.dot_general(
                        piece, rows, (((1,), (1,)), ((), ())), preferred_element_type=F32
                    )
                    for piece in two_parts(value)
                )

            terms = survival * against(adjoint) + spread_out * against(state_sum(adjoint))
            edge = jnp.sum(jnp.where(hit, terms, 0.0), axis=0, keepdims=True)
            for part in range(2):
                piece = edge[:, part * LANES : (part + 1) * LANES]
                term_ref[pl.ds(2 * part * owners + dest, 1), :] = piece
                term_ref[pl.ds((2 * part + 1) * owners + dest, 1), :] = pltpu.roll(
                    piece, LANES // 2, 1
                )
            return carry

        lax.fori_loop(0, owners, body, 0, unroll=2)

    term_ref[pl.ds(slots, LANES), :] = jnp.zeros((LANES, LANES), F32)
    for level in range(levels):
        spread(level)
        gather(level, level == levels - 1)

    score = score_ref[...]
    score_high = score.astype(BF16)
    score_rest = score - score_high.astype(F32)
    score_middle = score_rest.astype(BF16)
    score_low = (score_rest - score_middle.astype(F32)).astype(BF16)
    totals = [jnp.zeros((1, LANES), F32), jnp.zeros((1, LANES), F32)]
    for chunk in range(topo_ref.shape[0]):
        entry = topo_ref[chunk : chunk + 1, :]
        owner_of = entry // node_dev
        local_of = entry - owner_of * node_dev
        row = lax.broadcasted_iota(jnp.int32, (node_dev, LANES), 0)
        owner_hot = (row == owner_of).astype(F32).astype(BF16)
        found = sum(
            lax.dot_general(piece, owner_hot, (((0,), (0,)), ((), ())), preferred_element_type=F32)
            for piece in (score_high, score_middle, score_low)
        )
        totals[chunk % 2] = totals[chunk % 2] + jnp.sum(
            jnp.where(row == local_of, found, 0.0), axis=0, keepdims=True
        )
    for part in range(2):
        term_ref[slots + 2 * part : slots + 2 * part + 1, :] = totals[part]
        term_ref[slots + 2 * part + 1 : slots + 2 * part + 2, :] = pltpu.roll(
            totals[part], LANES // 2, 1
        )
    for block in range(slots // LANES + 1):
        out_ref[:, block * LANES : (block + 1) * LANES] = term_ref[
            block * LANES : (block + 1) * LANES, :
        ].T[:owners]


def on_device(leaf_partials, dag_edges, weights, lengths, counts, topo_nodes):
    node_dev, states, site_dev = leaf_partials.shape
    levels, edge_dev, _ = dag_edges.shape
    owners = lax.axis_size("node")
    device = lax.axis_index("node")
    sites_all = site_dev * lax.axis_size("site")
    site_own = site_dev // owners
    ranks = 4
    slots = ranks * owners
    fields = 4
    topo_dev, use = topo_nodes.shape

    turned = pl.pallas_call(
        spread_kernel,
        grid=(site_dev // LANES,),
        in_specs=[pl.BlockSpec((node_dev, states, LANES), lambda step: (0, 0, step))],
        out_specs=pl.BlockSpec((LANES, states * node_dev), lambda step: (step, 0)),
        out_shape=jax.ShapeDtypeStruct((site_dev, states * node_dev), F32),
    )(leaf_partials)
    leaves = lax.all_to_all(
        turned.reshape(owners, site_own, states * node_dev), "node",
        split_axis=0, concat_axis=0, tiled=True,
    ).reshape(owners * site_own, states * node_dev)

    child = dag_edges[:, :, 0] - device * node_dev
    parents = dag_edges[:, :, 1]
    owner_of = parents // node_dev
    code = dag_edges[:, :, 2] * node_dev + parents - owner_of * node_dev
    earlier = jnp.arange(edge_dev)[:, None] < jnp.arange(edge_dev)[None, :]
    rank = jnp.sum(
        ((owner_of[:, :, None] == owner_of[:, None, :]) & earlier[None]).astype(jnp.int32), axis=1
    )
    slot = rank * owners + owner_of
    chosen = slot[:, None, :] == jnp.arange(slots)[None, :, None]
    values = jnp.stack(
        [
            (child + 1).astype(F32), (code + 1).astype(F32), weights,
            jnp.exp(lengths * (-4.0 / 3.0)),
        ]
    )
    by_slot = jnp.sum(jnp.where(chosen[None], values[:, :, None, :], 0.0), axis=3)
    meta = lax.all_gather(by_slot.reshape(fields * levels * 2, LANES), "node", axis=0, tiled=True)
    topo = lax.all_gather(topo_nodes, "node", axis=0, tiled=True)
    topo = topo.reshape(owners, topo_dev, use).transpose(2, 1, 0).reshape(-1, LANES)
    own_counts = lax.dynamic_slice_in_dim(counts, device * site_own, site_own)
    scaled = jnp.tile(own_counts.astype(F32) / sites_all, LANES // site_own)[None, :]

    partial = pl.pallas_call(
        functools.partial(
            dag_kernel, levels=levels, owners=owners, node_dev=node_dev, site_own=site_own,
            states=states, fields=fields,
        ),
        out_shape=jax.ShapeDtypeStruct((owners, slots + LANES), F32),
        scratch_shapes=[
            pltpu.VMEM((owners * node_dev, LANES), BF16),
            pltpu.VMEM((slots * owners, LANES), F32),
            pltpu.VMEM((levels * (fields - 1) * owners, slots), F32),
            pltpu.VMEM((owners, node_dev), F32),
            pltpu.VMEM((node_dev, LANES), F32),
            pltpu.VMEM((slots + LANES, LANES), F32),
        ],
        compiler_params=pltpu.CompilerParams(vmem_limit_bytes=48 * 1024 * 1024),
    )(leaves, meta, topo, scaled)
    mine = lax.psum_scatter(partial, "node", scatter_dimension=0, tiled=True)
    mine = lax.psum(mine[:, : slots + topo_dev], "site")[0]
    edge_gradient = jnp.sum(
        jnp.where(slot[levels - 1][:, None] == jnp.arange(slots)[None, :], mine[None, :slots], 0.0),
        axis=1,
    )
    return (mine[slots:], edge_gradient)


def solution(mesh):
    return jax.shard_map(
        on_device,
        mesh=mesh,
        in_specs=(
            P("node", None, "site"),
            P(None, "node", None),
            P(None, "node"),
            P(None, "node"),
            P("site"),
            P("node", None),
        ),
        out_specs=(P("node"), P("node")),
        check_vma=False,
    )
```

time: 914 us -> 467 us (0.51); the launches traced: 900 us -> 466 us
  blocking collectives: 392 us -> 126 us
  local copies, waits for them, and re-layouts: 165 us -> 2.76 us
  Pallas kernels: 0 us -> 141 us
  starting transfers between devices: 94.5 us -> 12.2 us
  other arithmetic: 43.2 us -> 2.33 us
  matrix products: 22.3 us -> 0 us
  waiting for transfers between devices: 182 us -> 168 us
  between operations: 2.3 us -> 14.2 us
    unnamed x1 -> x0, blocking collectives: 246 us -> none
    all_to_all x10 -> x1, waiting for transfers between devices: 182 us -> 0.01 us  [on_device(): lax.all_to_all(turned.reshape(owners, site_own, states * node_dev), 'node...]
    unnamed x0 -> x2, waiting for transfers between devices: none -> 168 us
    pallas_call x0 -> x2, Pallas kernels: none -> 141 us  [the longest x1 135 us: on_device(): pl.pallas_call(functools.partial(dag_kernel, levels=levels, owners=owners...]
    scatter x9 -> x0, local copies, waits for them, and re-layouts: 85.7 us -> none  [the longest x3 78.6 us: on_device(): jnp.zeros((slots_all, states, site_dev), jnp.float32).at[slot_index]]
    all_to_all x10 -> x1, starting transfers between devices: 94.5 us -> 12.2 us  [on_device(): lax.all_to_all(turned.reshape(owners, site_own, states * node_dev), 'node...]
    unnamed x21 -> x11, local copies, waits for them, and re-layouts: 26.9 us -> 0.6 us
    dot_general x5 -> x0, matrix products: 22.3 us -> none  [the longest x3 19.7 us: on_device(): jnp.dot(selector * received_weights.reshape(-1)[None, :], flat_rows, prec...]
  transfers between devices with their start and end apart: 10 -> 2, of which waited for: 2 -> 1; matrix products, arithmetic and copies ran while one was open for 21% -> 1% of each run, Pallas kernels for 0% -> 0%
where the time goes in v1:
time: 467 us; the launch traced here: 466 us
  waiting for transfers between devices  168 us (36%)
  Pallas kernels  141 us (30%)
  blocking collectives  126 us (27%)
  between operations  14.2 us (3%)
  starting transfers between devices  12.2 us (3%)
    unnamed x2, waiting for transfers between devices  168 us
    pallas_call x1, Pallas kernels, on_device(): pl.pallas_call(functools.partial(dag_kernel, levels=levels, owners=owners...  135 us
    all_gather x1, blocking collectives, on_device(): topo = lax.all_gather(topo_nodes, 'node', axis=0, tiled=True)  66.5 us
    all_gather x1, blocking collectives, on_device(): lax.all_gather(by_slot.reshape(fields * levels * 2, LANES), 'node', axis=...  48.6 us
    all_to_all x1, starting transfers between devices, on_device(): lax.all_to_all(turned.reshape(owners, site_own, states * node_dev), 'node...  12.2 us
    psum x1, blocking collectives, on_device(): mine = lax.psum(mine[:, :slots + topo_dev], 'site')[0]  10.4 us
  transfers between devices with their start and end apart: 2, of which 1 were waited for; matrix products, arithmetic and copies ran while one was open for 1% of the time, Pallas kernels for 0%

profile of v1, /device:TPU:2, one launch (start us, length us, event | category | flops | bytes accessed | tf_op | source)
XLA Modules:
  0.0 465.6 jit_solution(10074179536012421255)
XLA Ops:
  7.2 5.7 %shard_map.77 = f32[1024,256]{1,0:T(8,128)} custom-call(f32[64,4,1024]{2,1,0:T(4,128)} %leaf_ref.1), custom_call_target="tpu_custom_call" | custom-call | tf_op jit(solution)/shard_map/pallas_call | solution.py:226
  12.8 0.0 copy-start.1
  12.8 0.0 copy-start
  12.8 0.0 copy-start.2
  12.8 0.0 copy-start.3
  12.8 12.2 %all-to-all-start = ((f32[64,16,256]{2,1,0:T(8,128)}), f32[64,16,256]{2,1,0:T(8,128)S(1)}, u32[]{:S(2)}, u32[]{:S(2)}) async-start(f32[64,16,256]{2,1,0:T(8,128)} %bitcast.71), calls=%async_computation | async-start | bytes 2097152 | tf_op jit(solution)/shard_map/all_to_all | solution.py:233
  25.0 0.0 all-reduce.3.cloned.1.call-start
  25.0 0.0 copy-done.1
  25.1 0.0 copy-done
  25.1 0.0 copy-done.2
  25.2 0.2 convert_reduce_fusion
  25.4 0.1 iota_compare_fusion
  25.6 0.4 select_reduce_fusion
  26.0 0.0 copy-done.3
  26.0 66.5 %all-gather = s32[64,4,8]{2,1,0:T(4,128)S(1)} all-gather(s32[1,4,8]{2,1,0:T(4,128)S(1)} %bitcast.76), channel_id=1, replica_groups=mesh['node'=64,'site'=4] {'node'}, dimensions={0}, use_global_device_ids=true | all-gather | bytes 8320 | tf_op jit(solution)/shard_map/all_gather | solution.py:256
  92.5 0.1 copy.23
  92.6 0.1 reshape.209.topo_ref
  92.7 0.8 convert_multiply_fusion
  93.5 0.1 broadcast_in_dim_tile.3.scaled_ref
  93.6 48.6 %all_gather.6.meta_ref = f32[1536,128]{1,0:T(8,128)S(1)} all-gather(f32[24,128]{1,0:T(8,128)S(1)} %reshape.207), channel_id=1, replica_groups=mesh['node'=64,'site'=4] {'node'}, dimensions={0}, use_global_device_ids=true | all-gather | bytes 798720 | tf_op jit(solution)/shard_map/all_gather | solution.py:255
  142.2 0.0 copy-start.4
  142.2 0.0 all-to-all-done
  142.2 135.0 %shard_map.78 = f32[64,384]{1,0:T(8,128)} custom-call(f32[1024,256]{1,0:T(8,128)S(1)} %bitcast.70, f32[1536,128]{1,0:T(8,128)S(1)} %all_gather.6.meta_ref, s32[16,128]{1,0:T(8,128)S(1)} %reshape.209.topo_ref, f32[1,128]{1,0:T(1,128)S(1)} %broadcast_in_dim_tile.3.scaled_ref), custom_call_target="tpu_custom_call" | custom-call | tf_op jit(solution)/shard_map/pallas_call | solution.py:261
  277.1 0.0 all-reduce.3.cloned.1.call-update
  277.2 0.0 copy-done.4
  277.2 0.6 dynamic-slice
  277.8 167.9 %all-reduce.3.cloned.1.call-done = f32[64,384]{1,0:T(8,128)} async-done(((f32[64,384]{1,0:T(8,128)}), f32[64,384]{1,0:T(8,128)}) %all-reduce.3.cloned.1.call-update) | async-done | bytes 98320
  445.6 1.4 constant_dynamic-slice_fusion
  447.0 10.4 %psum.7 = f32[1,260]{1,0:T(1,128)S(1)} all-reduce(f32[1,260]{1,0:T(1,128)S(1)} %constant_dynamic-slice_fusion), channel_id=1, replica_groups=mesh['node'=64,'site'=4] {'site'}, use_global_device_ids=true, to_apply=%region_3.4 | all-reduce | flops 260 | bytes 2080 | tf_op jit(solution)/shard_map/psum | solution.py:278
  457.4 0.5 slice_bitcast_fusion
  458.0 0.8 select_reduce_fusion.1
  (13 shorter events, 0.1 us)
Async XLA Ops:
  12.8 12.2 %copy-start.1 = (f32[3,192]{1,0:T(4,128)S(1)}, f32[3,192]{1,0:T(4,128)}, u32[]{:S(2)}) copy-start(f32[3,192]{1,0:T(4,128)} %param.9) | copy-start | bytes 6916
  12.8 12.3 %copy-start = (s32[3,192,3]{1,2,0:T(4,128)S(1)}, s32[3,192,3]{1,2,0:T(4,128)}, u32[]{:S(2)}) copy-start(s32[3,192,3]{1,2,0:T(4,128)} %param.7) | copy-start | bytes 20740
  12.8 12.3 %copy-start.2 = (f32[3,192]{1,0:T(4,128)S(1)}, f32[3,192]{1,0:T(4,128)}, u32[]{:S(2)}) copy-start(f32[3,192]{1,0:T(4,128)} %param.8) | copy-start | bytes 6916
  12.8 13.2 %copy-start.3 = (s32[4,8]{1,0:T(4,128)S(1)}, s32[4,8]{1,0:T(4,128)}, u32[]{:S(2)}) copy-start(s32[4,8]{1,0:T(4,128)} %param.11) | copy-start | bytes 388
  12.8 129.3 %all-to-all-start = ((f32[64,16,256]{2,1,0:T(8,128)}), f32[64,16,256]{2,1,0:T(8,128)S(1)}, u32[]{:S(2)}, u32[]{:S(2)}) async-start(f32[64,16,256]{2,1,0:T(8,128)} %bitcast.71), calls=%async_computation | async-start | bytes 2097152 | tf_op jit(solution)/shard_map/all_to_all | solution.py:233
  25.0 420.6 %all-reduce.3.cloned.1.call-start = ((), (), s32[]{:S(2)}) async-start(), calls=%async_computation.1 | async-start | bytes 196608
  142.2 135.0 %copy-start.4 = (u32[256]{0:T(256)S(1)}, u32[256]{0:T(256)}, u32[]{:S(2)}) copy-start(u32[256]{0:T(256)} %constant.40) | copy-start | bytes 3076
Sparse Core Ops, SparseCore 0:
  277.3 168.3 all-reduce.2

commit v2 on v1

--- a/solution.py
+++ b/solution.py
@@ -9,14 +9,24 @@
 
 F32 = jnp.float32
 BF16 = jnp.bfloat16
+MASK = F32
+SPREAD_UNROLL = 8
+GATHER_UNROLL = 8
+LAST_UNROLL = 4
+LEAF_UNROLL = 4
 LANES = 128
 
 
-def spread_kernel(leaf_ref, out_ref):
+def pack_kernel(leaf_ref, tail_ref, out_ref, *, site_own, chunk):
     states = leaf_ref.shape[1]
     for pair in range(states // 2):
-        rows = jnp.concatenate([leaf_ref[:, 2 * pair, :], leaf_ref[:, 2 * pair + 1, :]], axis=0)
-        out_ref[:, pair * LANES : (pair + 1) * LANES] = rows.T
+        rows = jnp.concatenate([leaf_ref[:, 2 * pair, :], leaf_ref[:, 2 * pair + 1, :]], axis=0).T
+        for peer in range(LANES // site_own):
+            out_ref[peer * chunk + pair * site_own : peer * chunk + (pair + 1) * site_own, :] = (
+                rows[peer * site_own : (peer + 1) * site_own]
+            )
+    for peer in range(LANES // site_own):
+        out_ref[peer * chunk + 2 * site_own : (peer + 1) * chunk, :] = tail_ref[...]
 
 
 def two_parts(value):
@@ -30,13 +40,14 @@
 
 
 def dag_kernel(
-    leaf_ref, meta_ref, topo_ref, scaled_ref, out_ref,
-    current_ref, slot_ref, table_ref, score_ref, mult_ref, term_ref,
-    *, levels, owners, node_dev, site_own, states, fields,
+    input_ref, scaled_ref, out_ref,
+    current_ref, slot_ref, table_ref, topo_ref, score_ref, mult_ref, term_ref,
+    *, levels, owners, node_dev, site_own, states, fields, chunk, out_rows,
 ):
     half = 2 * node_dev
     slots = 4 * owners
     meta_rows = fields * levels * 2
+    meta_base = 2 * site_own
     left = lax.broadcasted_iota(jnp.int32, (LANES, LANES), 1) < LANES // 2
     left_nodes = left[:node_dev]
 
@@ -50,11 +61,17 @@
         for field in range(1, fields):
             for part in range(2):
                 row = (field * levels + level) * 2 + part
-                block = meta_ref[pl.ds(row, owners, stride=meta_rows), :].T
+                block = input_ref[pl.ds(meta_base + row, owners, stride=chunk), :].T
                 table_ref[
                     pl.ds((level * (fields - 1) + field - 1) * owners, owners),
                     part * LANES : (part + 1) * LANES,
                 ] = jnp.concatenate([block[:owners], block[owners:]], axis=1)
+
+    block = input_ref[pl.ds(meta_base + meta_rows, owners, stride=chunk), :].T
+    entries = topo_ref.shape[0]
+    topo_ref[...] = jnp.concatenate(
+        [block[:entries], block[entries : 2 * entries]], axis=1
+    ).astype(jnp.int32)
 
     def count_uses(chunk, total):
         entry = topo_ref[pl.ds(chunk, 1), :]
@@ -68,42 +85,59 @@
         )
 
     mult_ref[...] = lax.fori_loop(
-        0, topo_ref.shape[0], count_uses, jnp.zeros((node_dev, LANES), F32)
+        0, topo_ref.shape[0], count_uses, jnp.zeros((node_dev, LANES), F32), unroll=True
     )
 
     def load_leaves(pair, carry):
-        first = leaf_ref[pl.ds(pl.multiple_of(pair * 2 * site_own, 2 * site_own), site_own), :]
-        second = leaf_ref[
-            pl.ds(pl.multiple_of(pair * 2 * site_own, 2 * site_own) + site_own, site_own), :
-        ]
+        first = pl.multiple_of(pair * 2 * chunk, chunk)
         pieces = []
         for block in range(states // 2):
-            a = first[:, block * LANES : (block + 1) * LANES]
-            b = second[:, block * LANES : (block + 1) * LANES]
+            a = input_ref[pl.ds(first + block * site_own, site_own), :]
+            b = input_ref[pl.ds(first + chunk + block * site_own, site_own), :]
             pieces.append(jnp.where(left[:site_own], a, pltpu.roll(b, LANES // 2, 1)))
             pieces.append(jnp.where(left[:site_own], pltpu.roll(a, LANES // 2, 1), b))
         stacked = jnp.concatenate(pieces + pieces, axis=0)
         store_current(pl.multiple_of(pair * LANES, LANES), stacked.T, left)
         return carry
 
-    lax.fori_loop(0, owners // 2, load_leaves, 0)
+    lax.fori_loop(0, owners // 2, load_leaves, 0, unroll=LEAF_UNROLL)
 
     node_row = lax.broadcasted_iota(jnp.int32, (node_dev, LANES), 0).astype(F32) + 1.0
-    pair_row = lax.broadcasted_iota(jnp.int32, (half, slots), 0).astype(F32) + 1.0
+    pair_row = (lax.broadcasted_iota(jnp.int32, (half, slots), 0).astype(F32) + 1.0).astype(MASK)
+    blank = jnp.zeros((node_dev, LANES), BF16)
+    pair_wide = lax.broadcasted_iota(jnp.int32, (half, slots), 0).astype(F32) + 1.0
 
     def spread(level):
-        def body(source, carry):
-            rows = current_ref[pl.ds(pl.multiple_of(source * node_dev, node_dev), node_dev), :]
+        def body(pair, carry):
+            rows = current_ref[pl.ds(pl.multiple_of(pair * LANES, LANES), LANES), :]
+            both = jnp.concatenate(
+                [
+                    jnp.concatenate([rows[:node_dev], blank], axis=0),
+                    jnp.concatenate([blank, rows[node_dev:]], axis=0),
+                ],
+                axis=1,
+            )
             for part in range(2):
-                child = meta_ref[pl.ds(source * meta_rows + level * 2 + part, 1), :]
-                hot = (node_row == child).astype(F32).astype(BF16)
+                hot = jnp.concatenate(
+                    [
+                        node_row == input_ref[
+                            pl.ds((2 * pair + side) * chunk + meta_base + level * 2 + part, 1), :
+                        ]
+                        for side in range(2)
+                    ],
+                    axis=0,
+                )
                 picked = lax.dot_general(
-                    hot, rows, (((0,), (0,)), ((), ())), preferred_element_type=F32
+                    hot.astype(F32).astype(BF16), both, (((0,), (0,)), ((), ())),
+                    preferred_element_type=F32,
                 )
-                slot_ref[pl.ds(part * half * owners + source, half, stride=owners), :] = picked
+                for side in range(2):
+                    slot_ref[
+                        pl.ds(part * half * owners + 2 * pair + side, half, stride=owners), :
+                    ] = picked[:, side * LANES : (side + 1) * LANES]
             return carry
 
-        lax.fori_loop(0, owners, body, 0, unroll=4)
+        lax.fori_loop(0, owners // 2, body, 0, unroll=SPREAD_UNROLL)
 
     def gather(level, last):
         def body(dest, carry):
@@ -117,19 +151,23 @@
             weight = table_ref[pl.ds(base + owners, 1), :]
             survival = table_ref[pl.ds(base + 2 * owners, 1), :]
             spread_out = (1.0 - survival) * 0.25
-            hit = pair_row == code
-
-            def weighted(scale):
+            hit = pair_row == code.astype(MASK)
+            scales = []
+            for scale in (weight * survival, weight * spread_out):
                 high = scale.astype(BF16).astype(F32)
-                low = scale - high
-                return sum(
-                    jnp.dot(
-                        jnp.where(hit, piece, 0.0).astype(BF16), rows, preferred_element_type=F32
-                    )
-                    for piece in (high, low)
-                )
-
-            sums = weighted(weight * survival) + state_sum(weighted(weight * spread_out))
+                scales += [high, scale - high]
+            chosen = jnp.concatenate(
+                [
+                    jnp.where(hit, scale.astype(MASK), jnp.zeros((), MASK)).astype(BF16)
+                    for scale in scales
+                ],
+                axis=0,
+            )
+            product = jnp.dot(chosen, rows, preferred_element_type=F32)
+            sums = (
+                product[:half] + product[half : 2 * half]
+                + state_sum(product[2 * half : 3 * half] + product[3 * half :])
+            )
             sums = sums + pltpu.roll(sums, LANES // 2, 1)
             value = sums[:node_dev] * sums[node_dev:]
             if not last:
@@ -155,17 +193,21 @@
             times = jnp.sum(jnp.where(lane == dest, mult_ref[...], 0.0), axis=1, keepdims=True)
             factor = scaled * 0.25 / likelihood * times
             adjoint = jnp.concatenate([sums[node_dev:] * factor, sums[:node_dev] * factor], axis=0)
-
-            def against(value):
-                return sum(
-                    lax.dot_general(
-                        piece, rows, (((1,), (1,)), ((), ())), preferred_element_type=F32
-                    )
-                    for piece in two_parts(value)
-                )
-
-            terms = survival * against(adjoint) + spread_out * against(state_sum(adjoint))
-            edge = jnp.sum(jnp.where(hit, terms, 0.0), axis=0, keepdims=True)
+            against = lax.dot_general(
+                jnp.concatenate(
+                    [
+                        jnp.concatenate(two_parts(value), axis=1)
+                        for value in (adjoint, state_sum(adjoint))
+                    ],
+                    axis=0,
+                ),
+                jnp.concatenate([rows, rows], axis=1),
+                (((1,), (1,)), ((), ())), preferred_element_type=F32,
+            )
+            found = hit if MASK == F32 else pair_wide == code
+            edge = survival * jnp.sum(
+                jnp.where(found, against[:half], 0.0), axis=0, keepdims=True
+            ) + spread_out * jnp.sum(jnp.where(found, against[half:], 0.0), axis=0, keepdims=True)
             for part in range(2):
                 piece = edge[:, part * LANES : (part + 1) * LANES]
                 term_ref[pl.ds(2 * part * owners + dest, 1), :] = piece
@@ -174,7 +216,7 @@
                 )
             return carry
 
-        lax.fori_loop(0, owners, body, 0, unroll=2)
+        lax.fori_loop(0, owners, body, 0, unroll=LAST_UNROLL if last else GATHER_UNROLL)
 
     term_ref[pl.ds(slots, LANES), :] = jnp.zeros((LANES, LANES), F32)
     for level in range(levels):
@@ -206,7 +248,7 @@
             totals[part], LANES // 2, 1
         )
     for block in range(slots // LANES + 1):
-        out_ref[:, block * LANES : (block + 1) * LANES] = term_ref[
+        out_ref[pl.ds(block, owners, stride=out_rows), :] = term_ref[
             block * LANES : (block + 1) * LANES, :
         ].T[:owners]
 
@@ -223,18 +265,6 @@
     fields = 4
     topo_dev, use = topo_nodes.shape
 
-    turned = pl.pallas_call(
-        spread_kernel,
-        grid=(site_dev // LANES,),
-        in_specs=[pl.BlockSpec((node_dev, states, LANES), lambda step: (0, 0, step))],
-        out_specs=pl.BlockSpec((LANES, states * node_dev), lambda step: (step, 0)),
-        out_shape=jax.ShapeDtypeStruct((site_dev, states * node_dev), F32),
-    )(leaf_partials)
-    leaves = lax.all_to_all(
-        turned.reshape(owners, site_own, states * node_dev), "node",
-        split_axis=0, concat_axis=0, tiled=True,
-    ).reshape(owners * site_own, states * node_dev)
-
     child = dag_edges[:, :, 0] - device * node_dev
     parents = dag_edges[:, :, 1]
     owner_of = parents // node_dev
@@ -252,35 +282,58 @@
         ]
     )
     by_slot = jnp.sum(jnp.where(chosen[None], values[:, :, None, :], 0.0), axis=3)
-    meta = lax.all_gather(by_slot.reshape(fields * levels * 2, LANES), "node", axis=0, tiled=True)
-    topo = lax.all_gather(topo_nodes, "node", axis=0, tiled=True)
-    topo = topo.reshape(owners, topo_dev, use).transpose(2, 1, 0).reshape(-1, LANES)
+    halves = topo_dev // 2
+    topo = topo_nodes.reshape(halves, 2, use).transpose(1, 2, 0).reshape(1, -1).astype(F32)
+    meta = by_slot.reshape(fields * levels * 2, LANES)
+    tail = -(-(meta.shape[0] + 1) // 8) * 8
+    tail = jnp.concatenate(
+        [meta, jnp.pad(topo, ((0, tail - meta.shape[0] - 1), (0, LANES - topo.shape[1])))], axis=0
+    )
+    chunk = 2 * site_own + tail.shape[0]
+    peers = LANES // site_own
+    packed = pl.pallas_call(
+        functools.partial(pack_kernel, site_own=site_own, chunk=chunk),
+        grid=(site_dev // LANES,),
+        in_specs=[
+            pl.BlockSpec((node_dev, states, LANES), lambda step: (0, 0, step)),
+            pl.BlockSpec(tail.shape, lambda step: (0, 0)),
+        ],
+        out_specs=pl.BlockSpec((peers * chunk, LANES), lambda step: (step, 0)),
+        out_shape=jax.ShapeDtypeStruct((owners * chunk, LANES), F32),
+    )(leaf_partials, tail)
+    received = lax.all_to_all(
+        packed.reshape(owners, chunk, LANES), "node", split_axis=0, concat_axis=0, tiled=True
+    ).reshape(owners * chunk, LANES)
     own_counts = lax.dynamic_slice_in_dim(counts, device * site_own, site_own)
     scaled = jnp.tile(own_counts.astype(F32) / sites_all, LANES // site_own)[None, :]
 
+    out_rows = 8
     partial = pl.pallas_call(
         functools.partial(
             dag_kernel, levels=levels, owners=owners, node_dev=node_dev, site_own=site_own,
-            states=states, fields=fields,
+            states=states, fields=fields, chunk=chunk, out_rows=out_rows,
         ),
-        out_shape=jax.ShapeDtypeStruct((owners, slots + LANES), F32),
+        out_shape=jax.ShapeDtypeStruct((owners * out_rows, LANES), F32),
         scratch_shapes=[
             pltpu.VMEM((owners * node_dev, LANES), BF16),
             pltpu.VMEM((slots * owners, LANES), F32),
             pltpu.VMEM((levels * (fields - 1) * owners, slots), F32),
+            pltpu.VMEM((use * halves, LANES), jnp.int32),
             pltpu.VMEM((owners, node_dev), F32),
             pltpu.VMEM((node_dev, LANES), F32),
             pltpu.VMEM((slots + LANES, LANES), F32),
         ],
         compiler_params=pltpu.CompilerParams(vmem_limit_bytes=48 * 1024 * 1024),
-    )(leaves, meta, topo, scaled)
-    mine = lax.psum_scatter(partial, "node", scatter_dimension=0, tiled=True)
-    mine = lax.psum(mine[:, : slots + topo_dev], "site")[0]
+    )(received, scaled)
+    shares = lax.all_to_all(
+        partial.reshape(owners, out_rows, LANES), "node", split_axis=0, concat_axis=0, tiled=True
+    )
+    mine = lax.psum(jnp.sum(shares[:, : slots // LANES + 1], axis=0), "site").reshape(-1)
     edge_gradient = jnp.sum(
         jnp.where(slot[levels - 1][:, None] == jnp.arange(slots)[None, :], mine[None, :slots], 0.0),
         axis=1,
     )
-    return (mine[slots:], edge_gradient)
+    return (mine[slots : slots + topo_dev], edge_gradient)
 
 
 def solution(mesh):

time: 467 us -> 183 us (0.39)
  blocking collectives: 126 us -> 10.7 us
  waiting for transfers between devices: 168 us -> 62.6 us
  Pallas kernels: 141 us -> 84.6 us
  between operations: 14.2 us -> 0.74 us
  starting transfers between devices: 12.2 us -> 17.4 us
    unnamed x2 -> x0, waiting for transfers between devices: 168 us -> none
    all_gather x2 -> x0, blocking collectives: 115 us -> none  [the longest x1 66.5 us: on_device(): topo = lax.all_gather(topo_nodes, 'node', axis=0, tiled=True)]
    all_to_all x1 -> x2, waiting for transfers between devices: 0.01 us -> 62.6 us  [the longest x1 50.4 us: on_device(): lax.all_to_all(packed.reshape(owners, chunk, LANES), 'node', split_axis=0...]
    pallas_call x1, Pallas kernels: 135 us -> 78.8 us  [on_device(): pl.pallas_call(functools.partial(dag_kernel, levels=levels, owners=owners...]
    all_to_all x1 -> x2, starting transfers between devices: 12.2 us -> 17.4 us  [the longest x1 12 us: on_device(): lax.all_to_all(packed.reshape(owners, chunk, LANES), 'node', split_axis=0...]
  transfers between devices with their start and end apart: 2 -> 2, of which waited for: 1 -> 2; matrix products, arithmetic and copies ran while one was open for 1% -> 0% of each run, Pallas kernels for 0% -> 0%
where the time goes in v2:
time: 183 us
  Pallas kernels  84.6 us (46%)
  waiting for transfers between devices  62.6 us (34%)
  starting transfers between devices  17.4 us (10%)
  blocking collectives  10.7 us (6%)
  other arithmetic  5.06 us (3%)
    pallas_call x1, Pallas kernels, on_device(): pl.pallas_call(functools.partial(dag_kernel, levels=levels, owners=owners...  78.8 us
    all_to_all x1, waiting for transfers between devices, on_device(): lax.all_to_all(packed.reshape(owners, chunk, LANES), 'node', split_axis=0...  50.4 us
    all_to_all x1, waiting for transfers between devices, on_device(): lax.all_to_all(partial.reshape(owners, out_rows, LANES), 'node', split_ax...  12.2 us
    all_to_all x1, starting transfers between devices, on_device(): lax.all_to_all(packed.reshape(owners, chunk, LANES), 'node', split_axis=0...  12 us
    psum x1, blocking collectives, on_device(): lax.psum(jnp.sum(shares[:, :slots // LANES + 1], axis=0), 'site')  10.7 us
    pallas_call x1, Pallas kernels, on_device(): pl.pallas_call(functools.partial(pack_kernel, site_own=site_own, chunk=ch...  5.84 us
    all_to_all x1, starting transfers between devices, on_device(): lax.all_to_all(partial.reshape(owners, out_rows, LANES), 'node', split_ax...  5.43 us
  transfers between devices with their start and end apart: 2, of which 2 were waited for; matrix products, arithmetic and copies ran while one was open for 0% of the time, Pallas kernels for 0%

profile of v2, /device:TPU:2, one launch (start us, length us, event | category | flops | bytes accessed | tf_op | source)
XLA Modules:
  0.0 182.8 jit_solution(12272146534127148742)
XLA Ops:
  0.6 0.8 fusion.23
  1.5 0.7 convert_element_type.55
  2.2 0.7 exponential_bitcast_fusion
  2.9 0.1 copy.19
  3.0 0.1 convert_element_type.58
  3.1 0.2 convert_reduce_fusion
  3.3 0.1 iota_compare_fusion
  3.5 0.7 pad_maximum_fusion
  4.2 0.4 select_reduce_fusion
  4.6 0.6 select_maximum_fusion.tail_ref
  5.2 5.8 %shard_map.77 = f32[4096,128]{1,0:T(8,128)} custom-call(f32[64,4,1024]{2,1,0:T(4,128)} %leaf_ref.1, f32[32,128]{1,0:T(8,128)} %select_maximum_fusion.tail_ref), custom_call_target="tpu_custom_call" | custom-call | tf_op jit(solution)/shard_map/pallas_call | solution.py:294
  11.0 12.0 %all-to-all-start = ((f32[64,64,128]{2,1,0:T(8,128)}), f32[64,64,128]{2,1,0:T(8,128)S(1)}, u32[]{:S(2)}, u32[]{:S(2)}) async-start(f32[64,64,128]{2,1,0:T(8,128)} %bitcast.72), calls=%async_computation | async-start | bytes 4194304 | tf_op jit(solution)/shard_map/all_to_all | solution.py:304
  23.1 0.8 convert_multiply_fusion
  23.8 0.1 broadcast_in_dim_tile.3.scaled_ref
  23.9 50.4 %all-to-all-done = f32[64,64,128]{2,1,0:T(8,128)S(1)} async-done(((f32[64,64,128]{2,1,0:T(8,128)}), f32[64,64,128]{2,1,0:T(8,128)S(1)}, u32[]{:S(2)}, u32[]{:S(2)}) %all-to-all-start) | async-done | bytes 2097184 | tf_op jit(solution)/shard_map/all_to_all | solution.py:304
  74.3 78.8 %shard_map.78 = f32[512,128]{1,0:T(8,128)} custom-call(f32[4096,128]{1,0:T(8,128)S(1)} %bitcast.71, f32[1,128]{1,0:T(1,128)S(1)} %broadcast_in_dim_tile.3.scaled_ref), custom_call_target="tpu_custom_call" | custom-call | tf_op jit(solution)/shard_map/pallas_call | solution.py:311
  153.1 5.4 %all-to-all-start.1 = ((f32[64,8,128]{2,1,0:T(8,128)}), f32[64,8,128]{2,1,0:T(8,128)S(1)}, u32[]{:S(2)}, u32[]{:S(2)}) async-start(f32[64,8,128]{2,1,0:T(8,128)} %bitcast.11), calls=%async_computation.1 | async-start | bytes 524288 | tf_op jit(solution)/shard_map/all_to_all | solution.py:328
  158.5 12.2 %all-to-all-done.1 = f32[64,8,128]{2,1,0:T(8,128)S(1)} async-done(((f32[64,8,128]{2,1,0:T(8,128)}), f32[64,8,128]{2,1,0:T(8,128)S(1)}, u32[]{:S(2)}, u32[]{:S(2)}) %all-to-all-start.1) | async-done | bytes 262176 | tf_op jit(solution)/shard_map/all_to_all | solution.py:328
  170.7 0.1 slice_reduce_fusion
  170.8 10.7 %psum.7 = f32[3,128]{1,0:T(4,128)S(1)} all-reduce(f32[3,128]{1,0:T(4,128)S(1)} %slice_reduce_fusion), channel_id=1, replica_groups=mesh['node'=64,'site'=4] {'site'}, use_global_device_ids=true, to_apply=%region_3.4 | all-reduce | flops 384 | bytes 3072 | tf_op jit(solution)/shard_map/psum | solution.py:331
  181.6 0.5 slice.26
  182.1 0.8 select_reduce_fusion.1
  (10 shorter events, 0.1 us)
Async XLA Ops:
  11.0 63.3 %all-to-all-start = ((f32[64,64,128]{2,1,0:T(8,128)}), f32[64,64,128]{2,1,0:T(8,128)S(1)}, u32[]{:S(2)}, u32[]{:S(2)}) async-start(f32[64,64,128]{2,1,0:T(8,128)} %bitcast.72), calls=%async_computation | async-start | bytes 4194304 | tf_op jit(solution)/shard_map/all_to_all | solution.py:304
  153.1 17.7 %all-to-all-start.1 = ((f32[64,8,128]{2,1,0:T(8,128)}), f32[64,8,128]{2,1,0:T(8,128)S(1)}, u32[]{:S(2)}, u32[]{:S(2)}) async-start(f32[64,8,128]{2,1,0:T(8,128)} %bitcast.11), calls=%async_computation.1 | async-start | bytes 524288 | tf_op jit(solution)/shard_map/all_to_all | solution.py:328

commit v3 on v2

--- a/solution.py
+++ b/solution.py
@@ -12,7 +12,8 @@
 MASK = F32
 SPREAD_UNROLL = 8
 GATHER_UNROLL = 8
-LAST_UNROLL = 4
+FINISH_UNROLL = 8
+EDGE_UNROLL = 8
 LEAF_UNROLL = 4
 LANES = 128
 
@@ -34,14 +35,13 @@
     return high, (value - high.astype(F32)).astype(BF16)
 
 
-def state_sum(value):
-    value = value + pltpu.roll(value, 16, 1)
-    return value + pltpu.roll(value, 32, 1)
+def both_parts(value):
+    return jnp.concatenate(two_parts(value), axis=1)
 
 
 def dag_kernel(
     input_ref, scaled_ref, out_ref,
-    current_ref, slot_ref, table_ref, topo_ref, score_ref, mult_ref, term_ref,
+    current_ref, slot_ref, table_ref, topo_ref, score_ref, term_ref, sums_ref, adjoint_ref,
     *, levels, owners, node_dev, site_own, states, fields, chunk, out_rows,
 ):
     half = 2 * node_dev
@@ -56,6 +56,15 @@
         current_ref[pl.ds(start, value.shape[0]), :] = jnp.where(
             mask, high, value - high
         ).astype(BF16)
+
+    apart = jnp.abs(
+        lax.broadcasted_iota(jnp.int32, (LANES, LANES), 0)
+        - lax.broadcasted_iota(jnp.int32, (LANES, LANES), 1)
+    )
+    fold = (apart % (site_own * states) == 0).astype(F32).astype(BF16)
+    over_states = (apart % site_own == 0).astype(F32).astype(BF16)
+    over_states_twice = jnp.concatenate([over_states, over_states], axis=0)
+    settle = jnp.concatenate([fold, fold, over_states_twice], axis=0)
 
     for level in range(levels):
         for field in range(1, fields):
@@ -72,21 +81,6 @@
     topo_ref[...] = jnp.concatenate(
         [block[:entries], block[entries : 2 * entries]], axis=1
     ).astype(jnp.int32)
-
-    def count_uses(chunk, total):
-        entry = topo_ref[pl.ds(chunk, 1), :]
-        owner_of = entry // node_dev
-        local_of = entry - owner_of * node_dev
-        owner_hot = (lax.broadcasted_iota(jnp.int32, (LANES, LANES), 0) == owner_of).astype(F32)
-        local_hot = (lax.broadcasted_iota(jnp.int32, (node_dev, LANES), 0) == local_of).astype(F32)
-        return total + lax.dot_general(
-            local_hot.astype(BF16), owner_hot.astype(BF16), (((1,), (1,)), ((), ())),
-            preferred_element_type=F32,
-        )
-
-    mult_ref[...] = lax.fori_loop(
-        0, topo_ref.shape[0], count_uses, jnp.zeros((node_dev, LANES), F32), unroll=True
-    )
 
     def load_leaves(pair, carry):
         first = pl.multiple_of(pair * 2 * chunk, chunk)
@@ -139,21 +133,22 @@
 
         lax.fori_loop(0, owners // 2, body, 0, unroll=SPREAD_UNROLL)
 
-    def gather(level, last):
+    def slot_rows(dest):
+        pieces = [
+            slot_ref[pl.ds(pl.multiple_of((rank * owners + dest) * owners, owners), owners), :]
+            for rank in range(4)
+        ]
+        return jnp.concatenate(pieces, axis=0).astype(BF16)
+
+    def gather(level):
         def body(dest, carry):
-            pieces = [
-                slot_ref[pl.ds(pl.multiple_of((rank * owners + dest) * owners, owners), owners), :]
-                for rank in range(4)
-            ]
-            rows = jnp.concatenate(pieces, axis=0).astype(BF16)
             base = level * (fields - 1) * owners + dest
             code = table_ref[pl.ds(base, 1), :]
             weight = table_ref[pl.ds(base + owners, 1), :]
             survival = table_ref[pl.ds(base + 2 * owners, 1), :]
-            spread_out = (1.0 - survival) * 0.25
             hit = pair_row == code.astype(MASK)
             scales = []
-            for scale in (weight * survival, weight * spread_out):
+            for scale in (weight * survival, weight * ((1.0 - survival) * 0.25)):
                 high = scale.astype(BF16).astype(F32)
                 scales += [high, scale - high]
             chosen = jnp.concatenate(
@@ -163,19 +158,43 @@
                 ],
                 axis=0,
             )
-            product = jnp.dot(chosen, rows, preferred_element_type=F32)
-            sums = (
+            product = jnp.dot(chosen, slot_rows(dest), preferred_element_type=F32)
+            start = pl.multiple_of(dest * half, half)
+            sums_ref[pl.ds(start, half), : 2 * LANES] = both_parts(
                 product[:half] + product[half : 2 * half]
-                + state_sum(product[2 * half : 3 * half] + product[3 * half :])
-            )
-            sums = sums + pltpu.roll(sums, LANES // 2, 1)
-            value = sums[:node_dev] * sums[node_dev:]
-            if not last:
-                store_current(pl.multiple_of(dest * node_dev, node_dev), value, left_nodes)
-                return carry
+            )
+            sums_ref[pl.ds(start, half), 2 * LANES :] = both_parts(
+                product[2 * half : 3 * half] + product[3 * half :]
+            )
+            return carry
+
+        lax.fori_loop(0, owners, body, 0, unroll=GATHER_UNROLL)
+
+    def pair_sums(dest):
+        start = pl.multiple_of(dest * half, half)
+        return jnp.dot(sums_ref[pl.ds(start, half), :], settle, preferred_element_type=F32)
+
+    def finish():
+        def body(dest, carry):
+            sums = pair_sums(dest)
+            store_current(
+                pl.multiple_of(dest * node_dev, node_dev), sums[:node_dev] * sums[node_dev:],
+                left_nodes,
+            )
+            return carry
+
+        lax.fori_loop(0, owners, body, 0, unroll=FINISH_UNROLL)
+
+    def finish_last():
+        lane = lax.broadcasted_iota(jnp.int32, (node_dev, LANES), 1)
+
+        def body(dest, carry):
+            sums = pair_sums(dest)
             scaled = scaled_ref[...]
-            likelihood = 0.25 * state_sum(value)
-            lane = lax.broadcasted_iota(jnp.int32, (node_dev, LANES), 1)
+            likelihood = 0.125 * jnp.dot(
+                both_parts(sums[:node_dev] * sums[node_dev:]), over_states_twice,
+                preferred_element_type=F32,
+            )
             logs = scaled * jnp.log(likelihood)
             high = logs.astype(BF16).astype(F32)
             middle = (logs - high).astype(BF16).astype(F32)
@@ -190,38 +209,50 @@
                 jnp.ones((8, LANES), BF16), packed.astype(BF16), (((1,), (1,)), ((), ())),
                 preferred_element_type=F32,
             )[:1]
-            times = jnp.sum(jnp.where(lane == dest, mult_ref[...], 0.0), axis=1, keepdims=True)
-            factor = scaled * 0.25 / likelihood * times
+            factor = scaled * 0.25 / likelihood
             adjoint = jnp.concatenate([sums[node_dev:] * factor, sums[:node_dev] * factor], axis=0)
+            start = pl.multiple_of(dest * 2 * half, 2 * half)
+            parts = both_parts(adjoint)
+            adjoint_ref[pl.ds(start, half), :] = parts
+            adjoint_ref[pl.ds(start + half, half), :] = both_parts(
+                0.5 * jnp.dot(parts, over_states_twice, preferred_element_type=F32)
+            )
+            return carry
+
+        lax.fori_loop(0, owners, body, 0, unroll=FINISH_UNROLL)
+
+    def edges(level):
+        def body(dest, carry):
+            base = level * (fields - 1) * owners + dest
+            code = table_ref[pl.ds(base, 1), :]
+            survival = table_ref[pl.ds(base + 2 * owners, 1), :]
+            rows = slot_rows(dest)
             against = lax.dot_general(
-                jnp.concatenate(
-                    [
-                        jnp.concatenate(two_parts(value), axis=1)
-                        for value in (adjoint, state_sum(adjoint))
-                    ],
-                    axis=0,
-                ),
+                adjoint_ref[pl.ds(pl.multiple_of(dest * 2 * half, 2 * half), 2 * half), :],
                 jnp.concatenate([rows, rows], axis=1),
                 (((1,), (1,)), ((), ())), preferred_element_type=F32,
             )
-            found = hit if MASK == F32 else pair_wide == code
+            found = pair_wide == code
             edge = survival * jnp.sum(
                 jnp.where(found, against[:half], 0.0), axis=0, keepdims=True
-            ) + spread_out * jnp.sum(jnp.where(found, against[half:], 0.0), axis=0, keepdims=True)
+            ) + ((1.0 - survival) * 0.25) * jnp.sum(
+                jnp.where(found, against[half:], 0.0), axis=0, keepdims=True
+            )
             for part in range(2):
-                piece = edge[:, part * LANES : (part + 1) * LANES]
-                term_ref[pl.ds(2 * part * owners + dest, 1), :] = piece
-                term_ref[pl.ds((2 * part + 1) * owners + dest, 1), :] = pltpu.roll(
-                    piece, LANES // 2, 1
-                )
-            return carry
-
-        lax.fori_loop(0, owners, body, 0, unroll=LAST_UNROLL if last else GATHER_UNROLL)
-
-    term_ref[pl.ds(slots, LANES), :] = jnp.zeros((LANES, LANES), F32)
+                term_ref[pl.ds(part * owners + dest, 1), :] = edge[
+                    :, part * LANES : (part + 1) * LANES
+                ]
+            return carry
+
+        lax.fori_loop(0, owners, body, 0, unroll=EDGE_UNROLL)
+
     for level in range(levels):
         spread(level)
-        gather(level, level == levels - 1)
+        gather(level)
+        if level < levels - 1:
+            finish()
+    finish_last()
+    edges(levels - 1)
 
     score = score_ref[...]
     score_high = score.astype(BF16)
@@ -242,15 +273,15 @@
         totals[chunk % 2] = totals[chunk % 2] + jnp.sum(
             jnp.where(row == local_of, found, 0.0), axis=0, keepdims=True
         )
+    def place(row, block):
+        turned = block.T
+        out_ref[pl.ds(row, owners, stride=out_rows), : 2 * block.shape[0]] = jnp.concatenate(
+            [turned[:owners], turned[owners:]], axis=1
+        )
+
     for part in range(2):
-        term_ref[slots + 2 * part : slots + 2 * part + 1, :] = totals[part]
-        term_ref[slots + 2 * part + 1 : slots + 2 * part + 2, :] = pltpu.roll(
-            totals[part], LANES // 2, 1
-        )
-    for block in range(slots // LANES + 1):
-        out_ref[pl.ds(block, owners, stride=out_rows), :] = term_ref[
-            block * LANES : (block + 1) * LANES, :
-        ].T[:owners]
+        place(part, term_ref[part * owners : (part + 1) * owners, :])
+    place(2, jnp.concatenate(totals + [jnp.zeros((6, LANES), F32)], axis=0))
 
 
 def on_device(leaf_partials, dag_edges, weights, lengths, counts, topo_nodes):
@@ -320,20 +351,26 @@
             pltpu.VMEM((levels * (fields - 1) * owners, slots), F32),
             pltpu.VMEM((use * halves, LANES), jnp.int32),
             pltpu.VMEM((owners, node_dev), F32),
-            pltpu.VMEM((node_dev, LANES), F32),
-            pltpu.VMEM((slots + LANES, LANES), F32),
+            pltpu.VMEM((2 * owners, LANES), F32),
+            pltpu.VMEM((2 * owners * node_dev, 4 * LANES), BF16),
+            pltpu.VMEM((4 * owners * node_dev, 2 * LANES), BF16),
         ],
-        compiler_params=pltpu.CompilerParams(vmem_limit_bytes=48 * 1024 * 1024),
+        compiler_params=pltpu.CompilerParams(vmem_limit_bytes=56 * 1024 * 1024),
     )(received, scaled)
     shares = lax.all_to_all(
         partial.reshape(owners, out_rows, LANES), "node", split_axis=0, concat_axis=0, tiled=True
     )
     mine = lax.psum(jnp.sum(shares[:, : slots // LANES + 1], axis=0), "site").reshape(-1)
-    edge_gradient = jnp.sum(
+    uses = received.reshape(owners, chunk, LANES)[:, 2 * site_own + meta.shape[0], : topo_dev * use]
+    multiplicity = jnp.sum(
+        (uses.reshape(-1)[None, :] == parents[levels - 1].astype(F32)[:, None]).astype(F32), axis=1
+    )
+    edge_gradient = multiplicity * jnp.sum(
         jnp.where(slot[levels - 1][:, None] == jnp.arange(slots)[None, :], mine[None, :slots], 0.0),
         axis=1,
     )
-    return (mine[slots : slots + topo_dev], edge_gradient)
+    topology = mine[slots : slots + 16].reshape(2, 8)[:, :halves].T.reshape(-1)
+    return (topology, edge_gradient)
 
 
 def solution(mesh):

time: 183 us -> 185 us (1.011)
  local copies, waits for them, and re-layouts: 1.63 us -> 4.86 us
  waiting for transfers between devices: 62.6 us -> 60 us
    all_to_all x1, waiting for transfers between devices: 12.2 us -> 10.1 us  [on_device(): lax.all_to_all(partial.reshape(owners, out_rows, LANES), 'node', split_ax...]
  transfers between devices with their start and end apart: 2 -> 2, of which waited for: 2 -> 2; matrix products, arithmetic and copies ran while one was open for 0% -> 2% of each run, Pallas kernels for 0% -> 0%
where the time goes in v3:
time: 185 us
  Pallas kernels  84.9 us (46%)
  waiting for transfers between devices  60 us (32%)
  starting transfers between devices  17.4 us (9%)
  blocking collectives  10.7 us (6%)
  other arithmetic  6.06 us (3%)
  local copies, waits for them, and re-layouts  4.86 us (3%)
    pallas_call x1, Pallas kernels, on_device(): pl.pallas_call(functools.partial(dag_kernel, levels=levels, owners=owners...  79.1 us
    all_to_all x1, waiting for transfers between devices, on_device(): lax.all_to_all(packed.reshape(owners, chunk, LANES), 'node', split_axis=0...  49.9 us
    all_to_all x1, starting transfers between devices, on_device(): lax.all_to_all(packed.reshape(owners, chunk, LANES), 'node', split_axis=0...  12 us
    psum x1, blocking collectives, on_device(): lax.psum(jnp.sum(shares[:, :slots // LANES + 1], axis=0), 'site')  10.7 us
    all_to_all x1, waiting for transfers between devices, on_device(): lax.all_to_all(partial.reshape(owners, out_rows, LANES), 'node', split_ax...  10.1 us
    pallas_call x1, Pallas kernels, on_device(): pl.pallas_call(functools.partial(pack_kernel, site_own=site_own, chunk=ch...  5.84 us
    all_to_all x1, starting transfers between devices, on_device(): lax.all_to_all(partial.reshape(owners, out_rows, LANES), 'node', split_ax...  5.43 us
  transfers between devices with their start and end apart: 2, of which 2 were waited for; matrix products, arithmetic and copies ran while one was open for 2% of the time, Pallas kernels for 0%

profile of v3, /device:TPU:2, one launch (start us, length us, event | category | flops | bytes accessed | tf_op | source)
XLA Modules:
  0.0 184.8 jit_solution(12773027044034307203)
XLA Ops:
  0.6 0.8 fusion.23
  1.5 0.7 convert_element_type.68
  2.2 0.7 exponential_bitcast_fusion
  2.9 0.1 copy.27
  3.0 0.1 convert_element_type.71
  3.1 0.2 convert_reduce_fusion.1
  3.3 0.1 iota_compare_fusion
  3.5 0.7 pad_maximum_fusion
  4.2 0.4 select_reduce_fusion
  4.6 0.6 select_maximum_fusion.tail_ref
  5.2 5.8 %shard_map.77 = f32[4096,128]{1,0:T(8,128)} custom-call(f32[64,4,1024]{2,1,0:T(4,128)} %leaf_ref.1, f32[32,128]{1,0:T(8,128)} %select_maximum_fusion.tail_ref), custom_call_target="tpu_custom_call" | custom-call | tf_op jit(solution)/shard_map/pallas_call | solution.py:325
  11.0 12.0 %all-to-all-start = ((f32[64,64,128]{2,1,0:T(8,128)}), f32[64,64,128]{2,1,0:T(8,128)S(1)}, u32[]{:S(2)}, u32[]{:S(2)}) async-start(f32[64,64,128]{2,1,0:T(8,128)} %bitcast.74), calls=%async_computation | async-start | bytes 4194304 | tf_op jit(solution)/shard_map/all_to_all | solution.py:335
  23.1 0.8 convert_multiply_fusion
  23.8 0.6 broadcast_in_dim_tile.3.scaled_ref
  24.4 49.9 %all-to-all-done = f32[64,64,128]{2,1,0:T(8,128)S(1)} async-done(((f32[64,64,128]{2,1,0:T(8,128)}), f32[64,64,128]{2,1,0:T(8,128)S(1)}, u32[]{:S(2)}, u32[]{:S(2)}) %all-to-all-start) | async-done | bytes 2097184 | tf_op jit(solution)/shard_map/all_to_all | solution.py:335
  74.3 0.0 copy-start
  74.3 1.3 copy-done
  75.7 79.1 %shard_map.78 = f32[512,128]{1,0:T(8,128)} custom-call(f32[4096,128]{1,0:T(8,128)} %bitcast.73, f32[1,128]{1,0:T(1,128)} %broadcast_in_dim_tile.3.scaled_ref), custom_call_target="tpu_custom_call" | custom-call | tf_op jit(solution)/shard_map/pallas_call | solution.py:342
  154.7 5.4 %all-to-all-start.1 = ((f32[64,8,128]{2,1,0:T(8,128)}), f32[64,8,128]{2,1,0:T(8,128)S(1)}, u32[]{:S(2)}, u32[]{:S(2)}) async-start(f32[64,8,128]{2,1,0:T(8,128)} %bitcast.75), calls=%async_computation.1 | async-start | bytes 524288 | tf_op jit(solution)/shard_map/all_to_all | solution.py:360
  160.2 0.7 slice_convert_fusion
  160.9 1.0 slice_reduce_fusion.1
  161.9 0.1 eq.69
  162.0 0.3 convert_reduce_fusion
  162.3 10.1 %all-to-all-done.1 = f32[64,8,128]{2,1,0:T(8,128)S(1)} async-done(((f32[64,8,128]{2,1,0:T(8,128)}), f32[64,8,128]{2,1,0:T(8,128)S(1)}, u32[]{:S(2)}, u32[]{:S(2)}) %all-to-all-start.1) | async-done | bytes 262176 | tf_op jit(solution)/shard_map/all_to_all | solution.py:360
  172.4 0.1 slice_reduce_fusion
  172.5 10.7 %psum.7 = f32[3,128]{1,0:T(4,128)S(1)} all-reduce(f32[3,128]{1,0:T(4,128)S(1)} %slice_reduce_fusion), channel_id=1, replica_groups=mesh['node'=64,'site'=4] {'site'}, use_global_device_ids=true, to_apply=%region_3.4 | all-reduce | flops 384 | bytes 3072 | tf_op jit(solution)/shard_map/psum | solution.py:363
  183.2 0.1 slice.39
  183.3 0.1 copy.28
  183.4 0.6 reshape.238
  184.0 0.2 select_reduce_fusion.1
  184.2 0.6 mul.53
  (11 shorter events, 0.1 us)
Async XLA Ops:
  11.0 63.3 %all-to-all-start = ((f32[64,64,128]{2,1,0:T(8,128)}), f32[64,64,128]{2,1,0:T(8,128)S(1)}, u32[]{:S(2)}, u32[]{:S(2)}) async-start(f32[64,64,128]{2,1,0:T(8,128)} %bitcast.74), calls=%async_computation | async-start | bytes 4194304 | tf_op jit(solution)/shard_map/all_to_all | solution.py:335
  74.3 1.4 copy-start
  154.7 17.7 %all-to-all-start.1 = ((f32[64,8,128]{2,1,0:T(8,128)}), f32[64,8,128]{2,1,0:T(8,128)S(1)}, u32[]{:S(2)}, u32[]{:S(2)}) async-start(f32[64,8,128]{2,1,0:T(8,128)} %bitcast.75), calls=%async_computation.1 | async-start | bytes 524288 | tf_op jit(solution)/shard_map/all_to_all | solution.py:360

commit v4 on v3

--- a/solution.py
+++ b/solution.py
@@ -12,10 +12,12 @@
 MASK = F32
 SPREAD_UNROLL = 8
 GATHER_UNROLL = 8
-FINISH_UNROLL = 8
+FINISH_UNROLL = 2
+LAST_UNROLL = 2
 EDGE_UNROLL = 8
 LEAF_UNROLL = 4
 LANES = 128
+GROUP = 4
 
 
 def pack_kernel(leaf_ref, tail_ref, out_ref, *, site_own, chunk):
@@ -48,6 +50,7 @@
     slots = 4 * owners
     meta_rows = fields * levels * 2
     meta_base = 2 * site_own
+    pitch = slot_ref.shape[0] // slots
     left = lax.broadcasted_iota(jnp.int32, (LANES, LANES), 1) < LANES // 2
     left_nodes = left[:node_dev]
 
@@ -127,7 +130,7 @@
                 )
                 for side in range(2):
                     slot_ref[
-                        pl.ds(part * half * owners + 2 * pair + side, half, stride=owners), :
+                        pl.ds(part * half * pitch + 2 * pair + side, half, stride=pitch), :
                     ] = picked[:, side * LANES : (side + 1) * LANES]
             return carry
 
@@ -135,7 +138,7 @@
 
     def slot_rows(dest):
         pieces = [
-            slot_ref[pl.ds(pl.multiple_of((rank * owners + dest) * owners, owners), owners), :]
+            slot_ref[pl.ds((rank * owners + dest) * pitch, owners), :]
             for rank in range(4)
         ]
         return jnp.concatenate(pieces, axis=0).astype(BF16)
@@ -170,30 +173,34 @@
 
         lax.fori_loop(0, owners, body, 0, unroll=GATHER_UNROLL)
 
-    def pair_sums(dest):
-        start = pl.multiple_of(dest * half, half)
-        return jnp.dot(sums_ref[pl.ds(start, half), :], settle, preferred_element_type=F32)
+    def pair_sums(group):
+        rows = GROUP * half
+        start = pl.multiple_of(group * rows, rows)
+        sums = jnp.dot(sums_ref[pl.ds(start, rows), :], settle, preferred_element_type=F32)
+        first = [sums[item * half : item * half + node_dev] for item in range(GROUP)]
+        second = [sums[item * half + node_dev : (item + 1) * half] for item in range(GROUP)]
+        return jnp.concatenate(first, axis=0), jnp.concatenate(second, axis=0)
+
+    group_nodes = GROUP * node_dev
 
     def finish():
-        def body(dest, carry):
-            sums = pair_sums(dest)
-            store_current(
-                pl.multiple_of(dest * node_dev, node_dev), sums[:node_dev] * sums[node_dev:],
-                left_nodes,
-            )
+        mask = lax.broadcasted_iota(jnp.int32, (group_nodes, LANES), 1) < LANES // 2
+
+        def body(group, carry):
+            first, second = pair_sums(group)
+            store_current(pl.multiple_of(group * group_nodes, group_nodes), first * second, mask)
             return carry
 
-        lax.fori_loop(0, owners, body, 0, unroll=FINISH_UNROLL)
+        lax.fori_loop(0, owners // GROUP, body, 0, unroll=FINISH_UNROLL)
 
     def finish_last():
-        lane = lax.broadcasted_iota(jnp.int32, (node_dev, LANES), 1)
-
-        def body(dest, carry):
-            sums = pair_sums(dest)
+        lane = lax.broadcasted_iota(jnp.int32, (group_nodes, LANES), 1)
+
+        def body(group, carry):
+            first, second = pair_sums(group)
             scaled = scaled_ref[...]
             likelihood = 0.125 * jnp.dot(
-                both_parts(sums[:node_dev] * sums[node_dev:]), over_states_twice,
-                preferred_element_type=F32,
+                both_parts(first * second), over_states_twice, preferred_element_type=F32
             )
             logs = scaled * jnp.log(likelihood)
             high = logs.astype(BF16).astype(F32)
@@ -205,21 +212,31 @@
                     jnp.where(lane < 3 * site_own, logs - high - middle, 0.0),
                 ),
             )
-            score_ref[pl.ds(dest, 1), :] = lax.dot_general(
+            score_ref[pl.ds(group, 1), :] = lax.dot_general(
                 jnp.ones((8, LANES), BF16), packed.astype(BF16), (((1,), (1,)), ((), ())),
                 preferred_element_type=F32,
             )[:1]
             factor = scaled * 0.25 / likelihood
-            adjoint = jnp.concatenate([sums[node_dev:] * factor, sums[:node_dev] * factor], axis=0)
-            start = pl.multiple_of(dest * 2 * half, 2 * half)
+            first, second = second * factor, first * factor
+            adjoint = jnp.concatenate(
+                [
+                    value[item * node_dev : (item + 1) * node_dev]
+                    for item in range(GROUP)
+                    for value in (first, second)
+                ],
+                axis=0,
+            )
             parts = both_parts(adjoint)
-            adjoint_ref[pl.ds(start, half), :] = parts
-            adjoint_ref[pl.ds(start + half, half), :] = both_parts(
+            summed = both_parts(
                 0.5 * jnp.dot(parts, over_states_twice, preferred_element_type=F32)
             )
+            for item in range(GROUP):
+                start = pl.multiple_of((group * GROUP + item) * 2 * half, 2 * half)
+                adjoint_ref[pl.ds(start, half), :] = parts[item * half : (item + 1) * half]
+                adjoint_ref[pl.ds(start + half, half), :] = summed[item * half : (item + 1) * half]
             return carry
 
-        lax.fori_loop(0, owners, body, 0, unroll=FINISH_UNROLL)
+        lax.fori_loop(0, owners // GROUP, body, 0, unroll=LAST_UNROLL)
 
     def edges(level):
         def body(dest, carry):
@@ -262,14 +279,15 @@
     totals = [jnp.zeros((1, LANES), F32), jnp.zeros((1, LANES), F32)]
     for chunk in range(topo_ref.shape[0]):
         entry = topo_ref[chunk : chunk + 1, :]
-        owner_of = entry // node_dev
-        local_of = entry - owner_of * node_dev
-        row = lax.broadcasted_iota(jnp.int32, (node_dev, LANES), 0)
-        owner_hot = (row == owner_of).astype(F32).astype(BF16)
+        group_of = entry // group_nodes
+        local_of = entry - group_of * group_nodes
+        group_row = lax.broadcasted_iota(jnp.int32, (owners // GROUP, LANES), 0)
+        group_hot = (group_row == group_of).astype(F32).astype(BF16)
         found = sum(
-            lax.dot_general(piece, owner_hot, (((0,), (0,)), ((), ())), preferred_element_type=F32)
+            lax.dot_general(piece, group_hot, (((0,), (0,)), ((), ())), preferred_element_type=F32)
             for piece in (score_high, score_middle, score_low)
         )
+        row = lax.broadcasted_iota(jnp.int32, (group_nodes, LANES), 0)
         totals[chunk % 2] = totals[chunk % 2] + jnp.sum(
             jnp.where(row == local_of, found, 0.0), axis=0, keepdims=True
         )
@@ -347,10 +365,10 @@
         out_shape=jax.ShapeDtypeStruct((owners * out_rows, LANES), F32),
         scratch_shapes=[
             pltpu.VMEM((owners * node_dev, LANES), BF16),
-            pltpu.VMEM((slots * owners, LANES), F32),
+            pltpu.VMEM((slots * (owners + 1), LANES), F32),
             pltpu.VMEM((levels * (fields - 1) * owners, slots), F32),
             pltpu.VMEM((use * halves, LANES), jnp.int32),
-            pltpu.VMEM((owners, node_dev), F32),
+            pltpu.VMEM((owners // GROUP, GROUP * node_dev), F32),
             pltpu.VMEM((2 * owners, LANES), F32),
             pltpu.VMEM((2 * owners * node_dev, 4 * LANES), BF16),
             pltpu.VMEM((4 * owners * node_dev, 2 * LANES), BF16),

time: 185 us -> 157 us (0.85)
  Pallas kernels: 84.9 us -> 56.5 us
    pallas_call x1, Pallas kernels: 79.1 us -> 50.7 us  [on_device(): pl.pallas_call(functools.partial(dag_kernel, levels=levels, owners=owners...]
where the time goes in v4:
time: 157 us; the launch traced here: 156 us
  waiting for transfers between devices  60 us (38%)
  Pallas kernels  56.5 us (36%)
  starting transfers between devices  17.4 us (11%)
  blocking collectives  10.7 us (7%)
  other arithmetic  6.06 us (4%)
  local copies, waits for them, and re-layouts  4.86 us (3%)
    pallas_call x1, Pallas kernels, on_device(): pl.pallas_call(functools.partial(dag_kernel, levels=levels, owners=owners...  50.7 us
    all_to_all x1, waiting for transfers between devices, on_device(): lax.all_to_all(packed.reshape(owners, chunk, LANES), 'node', split_axis=0...  49.9 us
    all_to_all x1, starting transfers between devices, on_device(): lax.all_to_all(packed.reshape(owners, chunk, LANES), 'node', split_axis=0...  12 us
    psum x1, blocking collectives, on_device(): lax.psum(jnp.sum(shares[:, :slots // LANES + 1], axis=0), 'site')  10.7 us
    all_to_all x1, waiting for transfers between devices, on_device(): lax.all_to_all(partial.reshape(owners, out_rows, LANES), 'node', split_ax...  10.1 us
    pallas_call x1, Pallas kernels, on_device(): pl.pallas_call(functools.partial(pack_kernel, site_own=site_own, chunk=ch...  5.84 us
    all_to_all x1, starting transfers between devices, on_device(): lax.all_to_all(partial.reshape(owners, out_rows, LANES), 'node', split_ax...  5.43 us
  transfers between devices with their start and end apart: 2, of which 2 were waited for; matrix products, arithmetic and copies ran while one was open for 2% of the time, Pallas kernels for 0%

profile of v4, /device:TPU:2, one launch (start us, length us, event | category | flops | bytes accessed | tf_op | source)
XLA Modules:
  0.0 156.4 jit_solution(14147599431810280363)
XLA Ops:
  0.6 0.8 fusion.23
  1.5 0.7 convert_element_type.68
  2.2 0.7 exponential_bitcast_fusion
  2.9 0.1 copy.27
  3.0 0.1 convert_element_type.71
  3.1 0.2 convert_reduce_fusion.1
  3.3 0.1 iota_compare_fusion
  3.5 0.7 pad_maximum_fusion
  4.2 0.4 select_reduce_fusion
  4.6 0.6 select_maximum_fusion.tail_ref
  5.2 5.8 %shard_map.77 = f32[4096,128]{1,0:T(8,128)} custom-call(f32[64,4,1024]{2,1,0:T(4,128)} %leaf_ref.1, f32[32,128]{1,0:T(8,128)} %select_maximum_fusion.tail_ref), custom_call_target="tpu_custom_call" | custom-call | tf_op jit(solution)/shard_map/pallas_call | solution.py:343
  11.0 12.0 %all-to-all-start = ((f32[64,64,128]{2,1,0:T(8,128)}), f32[64,64,128]{2,1,0:T(8,128)S(1)}, u32[]{:S(2)}, u32[]{:S(2)}) async-start(f32[64,64,128]{2,1,0:T(8,128)} %bitcast.74), calls=%async_computation | async-start | bytes 4194304 | tf_op jit(solution)/shard_map/all_to_all | solution.py:353
  23.1 0.8 convert_multiply_fusion
  23.8 0.6 broadcast_in_dim_tile.3.scaled_ref
  24.4 49.9 %all-to-all-done = f32[64,64,128]{2,1,0:T(8,128)S(1)} async-done(((f32[64,64,128]{2,1,0:T(8,128)}), f32[64,64,128]{2,1,0:T(8,128)S(1)}, u32[]{:S(2)}, u32[]{:S(2)}) %all-to-all-start) | async-done | bytes 2097184 | tf_op jit(solution)/shard_map/all_to_all | solution.py:353
  74.3 0.0 copy-start
  74.3 1.3 copy-done
  75.7 50.7 %shard_map.78 = f32[512,128]{1,0:T(8,128)} custom-call(f32[4096,128]{1,0:T(8,128)} %bitcast.73, f32[1,128]{1,0:T(1,128)} %broadcast_in_dim_tile.3.scaled_ref), custom_call_target="tpu_custom_call" | custom-call | tf_op jit(solution)/shard_map/pallas_call | solution.py:360
  126.4 5.4 %all-to-all-start.1 = ((f32[64,8,128]{2,1,0:T(8,128)}), f32[64,8,128]{2,1,0:T(8,128)S(1)}, u32[]{:S(2)}, u32[]{:S(2)}) async-start(f32[64,8,128]{2,1,0:T(8,128)} %bitcast.75), calls=%async_computation.1 | async-start | bytes 524288 | tf_op jit(solution)/shard_map/all_to_all | solution.py:378
  131.8 0.7 slice_convert_fusion
  132.5 1.0 slice_reduce_fusion.1
  133.5 0.1 eq.69
  133.6 0.3 convert_reduce_fusion
  133.9 10.1 %all-to-all-done.1 = f32[64,8,128]{2,1,0:T(8,128)S(1)} async-done(((f32[64,8,128]{2,1,0:T(8,128)}), f32[64,8,128]{2,1,0:T(8,128)S(1)}, u32[]{:S(2)}, u32[]{:S(2)}) %all-to-all-start.1) | async-done | bytes 262176 | tf_op jit(solution)/shard_map/all_to_all | solution.py:378
  144.0 0.1 slice_reduce_fusion
  144.1 10.7 %psum.7 = f32[3,128]{1,0:T(4,128)S(1)} all-reduce(f32[3,128]{1,0:T(4,128)S(1)} %slice_reduce_fusion), channel_id=1, replica_groups=mesh['node'=64,'site'=4] {'site'}, use_global_device_ids=true, to_apply=%region_3.4 | all-reduce | flops 384 | bytes 3072 | tf_op jit(solution)/shard_map/psum | solution.py:381
  154.8 0.1 slice.39
  154.9 0.1 copy.28
  155.0 0.6 reshape.238
  155.6 0.2 select_reduce_fusion.1
  155.8 0.6 mul.53
  (11 shorter events, 0.1 us)
Async XLA Ops:
  11.0 63.3 %all-to-all-start = ((f32[64,64,128]{2,1,0:T(8,128)}), f32[64,64,128]{2,1,0:T(8,128)S(1)}, u32[]{:S(2)}, u32[]{:S(2)}) async-start(f32[64,64,128]{2,1,0:T(8,128)} %bitcast.74), calls=%async_computation | async-start | bytes 4194304 | tf_op jit(solution)/shard_map/all_to_all | solution.py:353
  74.3 1.4 copy-start
  126.4 17.7 %all-to-all-start.1 = ((f32[64,8,128]{2,1,0:T(8,128)}), f32[64,8,128]{2,1,0:T(8,128)S(1)}, u32[]{:S(2)}, u32[]{:S(2)}) async-start(f32[64,8,128]{2,1,0:T(8,128)} %bitcast.75), calls=%async_computation.1 | async-start | bytes 524288 | tf_op jit(solution)/shard_map/all_to_all | solution.py:378

commit v5 on v4

--- a/solution.py
+++ b/solution.py
@@ -20,16 +20,44 @@
 GROUP = 4
 
 
-def pack_kernel(leaf_ref, tail_ref, out_ref, *, site_own, chunk):
+def pack_kernel(leaf_ref, out_ref, *, site_own):
     states = leaf_ref.shape[1]
+    chunk = states // 2 * site_own
     for pair in range(states // 2):
         rows = jnp.concatenate([leaf_ref[:, 2 * pair, :], leaf_ref[:, 2 * pair + 1, :]], axis=0).T
         for peer in range(LANES // site_own):
             out_ref[peer * chunk + pair * site_own : peer * chunk + (pair + 1) * site_own, :] = (
                 rows[peer * site_own : (peer + 1) * site_own]
             )
-    for peer in range(LANES // site_own):
-        out_ref[peer * chunk + 2 * site_own : (peer + 1) * chunk, :] = tail_ref[...]
+
+
+def table_kernel(
+    place_ref, *refs, levels, owners, fields, shares, share_rows, entries,
+):
+    share_refs, (child_ref, table_ref, topo_ref, meta_ref) = refs[:shares], refs[shares:]
+    size = owners * share_rows
+    for step in range(shares):
+        origin = lax.rem(place_ref[0] + (shares - step), shares)
+        meta_ref[pl.ds(pl.multiple_of(origin * size, size), size), :] = share_refs[step][...]
+
+    def rows_of(row):
+        return meta_ref[
+            pl.ds(row // share_rows * size + row % share_rows, owners, stride=share_rows), :
+        ]
+
+    child_ref[...] = meta_ref[:size, :]
+    for level in range(levels):
+        for field in range(1, fields):
+            for part in range(2):
+                block = rows_of((field * levels + level) * 2 + part).T
+                table_ref[
+                    pl.ds((level * (fields - 1) + field - 1) * owners, owners),
+                    part * LANES : (part + 1) * LANES,
+                ] = jnp.concatenate([block[:owners], block[owners:]], axis=1)
+    block = rows_of(fields * levels * 2).T
+    topo_ref[...] = jnp.concatenate(
+        [block[:entries], block[entries : 2 * entries]], axis=1
+    ).astype(jnp.int32)
 
 
 def two_parts(value):
@@ -42,14 +70,14 @@
 
 
 def dag_kernel(
-    input_ref, scaled_ref, out_ref,
-    current_ref, slot_ref, table_ref, topo_ref, score_ref, term_ref, sums_ref, adjoint_ref,
-    *, levels, owners, node_dev, site_own, states, fields, chunk, out_rows,
+    input_ref, child_ref, table_ref, topo_ref, scaled_ref, out_ref,
+    current_ref, slot_ref, score_ref, term_ref, sums_ref, adjoint_ref,
+    *, levels, owners, node_dev, site_own, states, fields, out_rows,
 ):
     half = 2 * node_dev
     slots = 4 * owners
-    meta_rows = fields * levels * 2
-    meta_base = 2 * site_own
+    chunk = states // 2 * site_own
+    child_rows = child_ref.shape[0] // owners
     pitch = slot_ref.shape[0] // slots
     left = lax.broadcasted_iota(jnp.int32, (LANES, LANES), 1) < LANES // 2
     left_nodes = left[:node_dev]
@@ -68,22 +96,6 @@
     over_states = (apart % site_own == 0).astype(F32).astype(BF16)
     over_states_twice = jnp.concatenate([over_states, over_states], axis=0)
     settle = jnp.concatenate([fold, fold, over_states_twice], axis=0)
-
-    for level in range(levels):
-        for field in range(1, fields):
-            for part in range(2):
-                row = (field * levels + level) * 2 + part
-                block = input_ref[pl.ds(meta_base + row, owners, stride=chunk), :].T
-                table_ref[
-                    pl.ds((level * (fields - 1) + field - 1) * owners, owners),
-                    part * LANES : (part + 1) * LANES,
-                ] = jnp.concatenate([block[:owners], block[owners:]], axis=1)
-
-    block = input_ref[pl.ds(meta_base + meta_rows, owners, stride=chunk), :].T
-    entries = topo_ref.shape[0]
-    topo_ref[...] = jnp.concatenate(
-        [block[:entries], block[entries : 2 * entries]], axis=1
-    ).astype(jnp.int32)
 
     def load_leaves(pair, carry):
         first = pl.multiple_of(pair * 2 * chunk, chunk)
@@ -117,8 +129,8 @@
             for part in range(2):
                 hot = jnp.concatenate(
                     [
-                        node_row == input_ref[
-                            pl.ds((2 * pair + side) * chunk + meta_base + level * 2 + part, 1), :
+                        node_row == child_ref[
+                            pl.ds((2 * pair + side) * child_rows + level * 2 + part, 1), :
                         ]
                         for side in range(2)
                     ],
@@ -334,22 +346,53 @@
     halves = topo_dev // 2
     topo = topo_nodes.reshape(halves, 2, use).transpose(1, 2, 0).reshape(1, -1).astype(F32)
     meta = by_slot.reshape(fields * levels * 2, LANES)
-    tail = -(-(meta.shape[0] + 1) // 8) * 8
-    tail = jnp.concatenate(
-        [meta, jnp.pad(topo, ((0, tail - meta.shape[0] - 1), (0, LANES - topo.shape[1])))], axis=0
-    )
-    chunk = 2 * site_own + tail.shape[0]
+    shares = lax.axis_size("site")
+    share_rows = -(-(meta.shape[0] + 1) // (8 * shares)) * 8
+    place = lax.axis_index("site")
+    meta = jnp.concatenate(
+        [
+            meta,
+            jnp.pad(
+                topo,
+                ((0, share_rows * shares - meta.shape[0] - 1), (0, LANES - topo.shape[1])),
+            ),
+        ],
+        axis=0,
+    )
+    share = lax.dynamic_slice_in_dim(meta, place * share_rows, share_rows)
+    share = lax.all_to_all(
+        jnp.broadcast_to(share[None], (owners, share_rows, LANES)), "node",
+        split_axis=0, concat_axis=0, tiled=True,
+    ).reshape(owners * share_rows, LANES)
+    met = [share] + [
+        lax.ppermute(share, "site", [(k, (k + step) % shares) for k in range(shares)])
+        for step in range(1, shares)
+    ]
+    vmem = pl.BlockSpec(memory_space=pltpu.VMEM)
+    entries = use * halves
+    child_table, edge_table, topologies = pl.pallas_call(
+        functools.partial(
+            table_kernel, levels=levels, owners=owners, fields=fields, shares=shares,
+            share_rows=share_rows, entries=entries,
+        ),
+        in_specs=[pl.BlockSpec(memory_space=pltpu.SMEM)] + [vmem] * shares,
+        out_shape=[
+            jax.ShapeDtypeStruct((owners * share_rows, LANES), F32),
+            jax.ShapeDtypeStruct((levels * (fields - 1) * owners, slots), F32),
+            jax.ShapeDtypeStruct((entries, LANES), jnp.int32),
+        ],
+        scratch_shapes=[pltpu.VMEM((owners * share_rows * shares, LANES), F32)],
+    )(place.astype(jnp.int32).reshape(1), *met)
+
+    chunk = states // 2 * site_own
     peers = LANES // site_own
     packed = pl.pallas_call(
-        functools.partial(pack_kernel, site_own=site_own, chunk=chunk),
+        functools.partial(pack_kernel, site_own=site_own),
         grid=(site_dev // LANES,),
-        in_specs=[
-            pl.BlockSpec((node_dev, states, LANES), lambda step: (0, 0, step)),
-            pl.BlockSpec(tail.shape, lambda step: (0, 0)),
-        ],
+        in_specs=[pl.BlockSpec((node_dev, states, LANES), lambda step: (0, 0, step))],
         out_specs=pl.BlockSpec((peers * chunk, LANES), lambda step: (step, 0)),
         out_shape=jax.ShapeDtypeStruct((owners * chunk, LANES), F32),
-    )(leaf_partials, tail)
+    )(leaf_partials)
     received = lax.all_to_all(
         packed.reshape(owners, chunk, LANES), "node", split_axis=0, concat_axis=0, tiled=True
     ).reshape(owners * chunk, LANES)
@@ -360,28 +403,25 @@
     partial = pl.pallas_call(
         functools.partial(
             dag_kernel, levels=levels, owners=owners, node_dev=node_dev, site_own=site_own,
-            states=states, fields=fields, chunk=chunk, out_rows=out_rows,
+            states=states, fields=fields, out_rows=out_rows,
         ),
         out_shape=jax.ShapeDtypeStruct((owners * out_rows, LANES), F32),
         scratch_shapes=[
             pltpu.VMEM((owners * node_dev, LANES), BF16),
             pltpu.VMEM((slots * (owners + 1), LANES), F32),
-            pltpu.VMEM((levels * (fields - 1) * owners, slots), F32),
-            pltpu.VMEM((use * halves, LANES), jnp.int32),
             pltpu.VMEM((owners // GROUP, GROUP * node_dev), F32),
             pltpu.VMEM((2 * owners, LANES), F32),
             pltpu.VMEM((2 * owners * node_dev, 4 * LANES), BF16),
             pltpu.VMEM((4 * owners * node_dev, 2 * LANES), BF16),
         ],
         compiler_params=pltpu.CompilerParams(vmem_limit_bytes=56 * 1024 * 1024),
-    )(received, scaled)
+    )(received, child_table, edge_table, topologies, scaled)
     shares = lax.all_to_all(
         partial.reshape(owners, out_rows, LANES), "node", split_axis=0, concat_axis=0, tiled=True
     )
     mine = lax.psum(jnp.sum(shares[:, : slots // LANES + 1], axis=0), "site").reshape(-1)
-    uses = received.reshape(owners, chunk, LANES)[:, 2 * site_own + meta.shape[0], : topo_dev * use]
     multiplicity = jnp.sum(
-        (uses.reshape(-1)[None, :] == parents[levels - 1].astype(F32)[:, None]).astype(F32), axis=1
+        (topologies.reshape(-1)[None, :] == parents[levels - 1][:, None]).astype(F32), axis=1
     )
     edge_gradient = multiplicity * jnp.sum(
         jnp.where(slot[levels - 1][:, None] == jnp.arange(slots)[None, :], mine[None, :slots], 0.0),

time: 157 us -> 146 us (0.930)
  waiting for transfers between devices: 60 us -> 35.8 us
  starting transfers between devices: 17.4 us -> 29.2 us
  Pallas kernels: 56.5 us -> 58.3 us
    all_to_all x1, waiting for transfers between devices: 49.9 us -> 8.79 us  [on_device(): lax.all_to_all(packed.reshape(owners, chunk, LANES), 'node', split_axis=0...]
    all_to_all x0 -> x1, starting transfers between devices: none -> 12 us  [on_device(): lax.all_to_all(jnp.broadcast_to(share[None], (owners, share_rows, LANES))...]
    ppermute x0 -> x3, waiting for transfers between devices: none -> 9.24 us  [on_device(): lax.ppermute(share, 'site', [(k, (k + step) % shares) for k in range(shar...]
    all_to_all x0 -> x1, waiting for transfers between devices: none -> 6.57 us  [on_device(): lax.all_to_all(jnp.broadcast_to(share[None], (owners, share_rows, LANES))...]
    all_to_all x1, starting transfers between devices: 12 us -> 5.65 us  [on_device(): lax.all_to_all(packed.reshape(owners, chunk, LANES), 'node', split_axis=0...]
    ppermute x0 -> x3, starting transfers between devices: none -> 5.9 us  [on_device(): lax.ppermute(share, 'site', [(k, (k + step) % shares) for k in range(shar...]
    pallas_call x1 -> x2, Pallas kernels: 5.84 us -> 8.35 us  [the longest x1 5.65 us: on_device(): pl.pallas_call(functools.partial(pack_kernel, site_own=site_own), grid=(s...]
  transfers between devices with their start and end apart: 2 -> 6, of which waited for: 2 -> 5; matrix products, arithmetic and copies ran while one was open for 2% -> 2% of each run, Pallas kernels for 0% -> 6%
where the time goes in v5:
time: 146 us; the launch traced here: 145 us
  Pallas kernels  58.3 us (40%)
  waiting for transfers between devices  35.8 us (25%)
  starting transfers between devices  29.2 us (20%)
  blocking collectives  10.7 us (7%)
  local copies, waits for them, and re-layouts  5.62 us (4%)
  other arithmetic  4.77 us (3%)
    pallas_call x1, Pallas kernels, on_device(): pl.pallas_call(functools.partial(dag_kernel, levels=levels, owners=owners...  49.9 us
    all_to_all x1, starting transfers between devices, on_device(): lax.all_to_all(jnp.broadcast_to(share[None], (owners, share_rows, LANES))...  12 us
    all_to_all x1, waiting for transfers between devices, on_device(): lax.all_to_all(partial.reshape(owners, out_rows, LANES), 'node', split_ax...  11.2 us
    psum x1, blocking collectives, on_device(): lax.psum(jnp.sum(shares[:, :slots // LANES + 1], axis=0), 'site')  10.7 us
    ppermute x3, waiting for transfers between devices, on_device(): lax.ppermute(share, 'site', [(k, (k + step) % shares) for k in range(shar...  9.24 us
    all_to_all x1, waiting for transfers between devices, on_device(): lax.all_to_all(packed.reshape(owners, chunk, LANES), 'node', split_axis=0...  8.79 us
    all_to_all x1, waiting for transfers between devices, on_device(): lax.all_to_all(jnp.broadcast_to(share[None], (owners, share_rows, LANES))...  6.57 us
    ppermute x3, starting transfers between devices, on_device(): lax.ppermute(share, 'site', [(k, (k + step) % shares) for k in range(shar...  5.9 us
  transfers between devices with their start and end apart: 6, of which 5 were waited for; matrix products, arithmetic and copies ran while one was open for 2% of the time, Pallas kernels for 6%

profile of v5, /device:TPU:2, one launch (start us, length us, event | category | flops | bytes accessed | tf_op | source)
XLA Modules:
  0.0 145.2 jit_solution(4620205463014781576)
XLA Ops:
  0.6 0.8 fusion.25
  1.5 0.7 exponential_bitcast_fusion
  2.3 0.2 convert_reduce_fusion.1
  2.4 0.1 iota_compare_fusion
  2.6 0.7 pad_maximum_fusion
  3.3 0.4 select_reduce_fusion
  3.7 0.7 convert_element_type.58
  4.6 0.7 broadcast_in_dim.54
  5.4 12.0 %all-to-all-start.1 = ((f32[64,8,128]{2,1,0:T(8,128)}), f32[64,8,128]{2,1,0:T(8,128)S(1)}, u32[]{:S(2)}, u32[]{:S(2)}) async-start(f32[64,8,128]{2,1,0:T(8,128)} %broadcast_in_dim.54), calls=%async_computation.1 | async-start | bytes 524288 | tf_op jit(solution)/shard_map/all_to_all | solution.py:363
  17.4 5.7 %shard_map.77 = f32[2048,128]{1,0:T(8,128)} custom-call(f32[64,4,1024]{2,1,0:T(4,128)} %leaf_ref.1), custom_call_target="tpu_custom_call" | custom-call | tf_op jit(solution)/shard_map/pallas_call | solution.py:389
  23.0 6.6 %all-to-all-done.1 = f32[64,8,128]{2,1,0:T(8,128)S(1)} async-done(((f32[64,8,128]{2,1,0:T(8,128)}), f32[64,8,128]{2,1,0:T(8,128)S(1)}, u32[]{:S(2)}, u32[]{:S(2)}) %all-to-all-start.1) | async-done | bytes 262176 | tf_op jit(solution)/shard_map/all_to_all | solution.py:363
  29.6 5.7 %all-to-all-start = ((f32[64,32,128]{2,1,0:T(8,128)}), f32[64,32,128]{2,1,0:T(8,128)S(1)}, u32[]{:S(2)}, u32[]{:S(2)}) async-start(f32[64,32,128]{2,1,0:T(8,128)} %bitcast.77), calls=%async_computation | async-start | bytes 2097152 | tf_op jit(solution)/shard_map/all_to_all | solution.py:396
  35.3 1.7 %collective-permute-start = (f32[512,128]{1,0:T(8,128)S(1)}, f32[512,128]{1,0:T(8,128)S(1)}, u32[]{:S(2)}, u32[]{:S(2)}) collective-permute-start(f32[512,128]{1,0:T(8,128)S(1)} %bitcast.79), channel_id=1, source_target_pairs={{0,1},{1,2},{2,3},{3,0},{4,5},{5,6},{6,7},{7,4},{8,9},{9,10},{10,1... | collective-permute-start | bytes 786440 | tf_op jit(solution)/shard_map/ppermute | solution.py:368
  36.9 2.9 %collective-permute-start.1 = (f32[512,128]{1,0:T(8,128)S(1)}, f32[512,128]{1,0:T(8,128)S(1)}, u32[]{:S(2)}, u32[]{:S(2)}) collective-permute-start(f32[512,128]{1,0:T(8,128)S(1)} %bitcast.80), channel_id=1, source_target_pairs={{0,2},{1,3},{2,0},{3,1},{4,6},{5,7},{6,4},{7,5},{8,10},{9,11},{10,... | collective-permute-start | bytes 786440 | tf_op jit(solution)/shard_map/ppermute | solution.py:368
  39.8 1.3 collective-permute-start.2
  41.2 0.8 convert_multiply_fusion
  41.9 0.6 broadcast_in_dim_tile.3.scaled_ref
  42.5 2.4 %collective-permute-done.refs_1_ = f32[512,128]{1,0:T(8,128)S(1)} collective-permute-done((f32[512,128]{1,0:T(8,128)S(1)}, f32[512,128]{1,0:T(8,128)S(1)}, u32[]{:S(2)}, u32[]{:S(2)}) %collective-permute-start) | collective-permute-done | bytes 262176 | tf_op jit(solution)/shard_map/ppermute | solution.py:368
  45.0 6.8 %collective-permute-done.1.refs_2_ = f32[512,128]{1,0:T(8,128)S(1)} collective-permute-done((f32[512,128]{1,0:T(8,128)S(1)}, f32[512,128]{1,0:T(8,128)S(1)}, u32[]{:S(2)}, u32[]{:S(2)}) %collective-permute-start.1) | collective-permute-done | bytes 262176 | tf_op jit(solution)/shard_map/ppermute | solution.py:368
  51.8 0.7 copy-done.3
  52.6 2.7 %shard_map.78 = (f32[512,128]{1,0:T(8,128)}, f32[576,256]{1,0:T(8,128)}, s32[16,128]{1,0:T(8,128)}) custom-call(s32[1]{0:T(128)} %bitcast.2.place_ref, f32[512,128]{1,0:T(8,128)} %bitcast.82, f32[512,128]{1,0:T(8,128)} %copy-done.2, f32[512,128]{1,0:T(8,128)} %copy-done.3, f32[512,128]{1,0:T(8,128)} %copy-done.4), custom_call_target="tpu_custom_call" | custom-call | tf_op jit(solution)/shard_map/pallas_call | solution.py:373
  55.3 8.8 %all-to-all-done = f32[64,32,128]{2,1,0:T(8,128)S(1)} async-done(((f32[64,32,128]{2,1,0:T(8,128)}), f32[64,32,128]{2,1,0:T(8,128)S(1)}, u32[]{:S(2)}, u32[]{:S(2)}) %all-to-all-start) | async-done | bytes 1048608 | tf_op jit(solution)/shard_map/all_to_all | solution.py:396
  64.1 1.0 copy-done
  65.1 49.9 %shard_map.79 = f32[512,128]{1,0:T(8,128)} custom-call(f32[2048,128]{1,0:T(8,128)} %bitcast.76, f32[512,128]{1,0:T(8,128)} %get-tuple-element.5.child_ref, f32[576,256]{1,0:T(8,128)} %get-tuple-element.6.table_ref, s32[16,128]{1,0:T(8,128)} %get-tuple-element.7.topo_ref, f32[1,128]{1,0:T(1,128)} %broadcast_in_dim_tile.3.scaled_ref), custom_call_target="tpu_custom_call" | custom-call | tf_op jit(solution)/shard_map/pallas_call | solution.py:403
  115.0 5.7 %all-to-all-start.2 = ((f32[64,8,128]{2,1,0:T(8,128)}), f32[64,8,128]{2,1,0:T(8,128)S(1)}, u32[]{:S(2)}, u32[]{:S(2)}) async-start(f32[64,8,128]{2,1,0:T(8,128)} %bitcast.78), calls=%async_computation.2 | async-start | bytes 524288 | tf_op jit(solution)/shard_map/all_to_all | solution.py:419
  120.6 0.7 slice.38
  121.3 0.3 convert_reduce_fusion
  121.6 11.2 %all-to-all-done.2 = f32[64,8,128]{2,1,0:T(8,128)S(1)} async-done(((f32[64,8,128]{2,1,0:T(8,128)}), f32[64,8,128]{2,1,0:T(8,128)S(1)}, u32[]{:S(2)}, u32[]{:S(2)}) %all-to-all-start.2) | async-done | bytes 262176 | tf_op jit(solution)/shard_map/all_to_all | solution.py:419
  132.9 10.7 %psum.7 = f32[3,128]{1,0:T(4,128)S(1)} all-reduce(f32[3,128]{1,0:T(4,128)S(1)} %slice_reduce_fusion), channel_id=1, replica_groups=mesh['node'=64,'site'=4] {'site'}, use_global_device_ids=true, to_apply=%region_3.4 | all-reduce | flops 384 | bytes 3072 | tf_op jit(solution)/shard_map/psum | solution.py:422
  143.9 0.6 reshape.242
  144.5 0.2 select_reduce_fusion.1
  144.7 0.6 mul.57
  (28 shorter events, 0.7 us)
Async XLA Ops:
  5.4 24.2 %all-to-all-start.1 = ((f32[64,8,128]{2,1,0:T(8,128)}), f32[64,8,128]{2,1,0:T(8,128)S(1)}, u32[]{:S(2)}, u32[]{:S(2)}) async-start(f32[64,8,128]{2,1,0:T(8,128)} %broadcast_in_dim.54), calls=%async_computation.1 | async-start | bytes 524288 | tf_op jit(solution)/shard_map/all_to_all | solution.py:363
  29.6 10.2 %copy-start.1 = (f32[64,8,128]{2,1,0:T(8,128)}, f32[64,8,128]{2,1,0:T(8,128)S(1)}, u32[]{:S(2)}) copy-start(f32[64,8,128]{2,1,0:T(8,128)S(1)} %all-to-all-done.1) | copy-start | bytes 786436
  29.6 34.5 %all-to-all-start = ((f32[64,32,128]{2,1,0:T(8,128)}), f32[64,32,128]{2,1,0:T(8,128)S(1)}, u32[]{:S(2)}, u32[]{:S(2)}) async-start(f32[64,32,128]{2,1,0:T(8,128)} %bitcast.77), calls=%async_computation | async-start | bytes 2097152 | tf_op jit(solution)/shard_map/all_to_all | solution.py:396
  35.3 9.7 %collective-permute-start = (f32[512,128]{1,0:T(8,128)S(1)}, f32[512,128]{1,0:T(8,128)S(1)}, u32[]{:S(2)}, u32[]{:S(2)}) collective-permute-start(f32[512,128]{1,0:T(8,128)S(1)} %bitcast.79), channel_id=1, source_target_pairs={{0,1},{1,2},{2,3},{3,0},{4,5},{5,6},{6,7},{7,4},{8,9},{9,10},{10,1... | collective-permute-start | bytes 786440 | tf_op jit(solution)/shard_map/ppermute | solution.py:368
  36.9 14.9 %collective-permute-start.1 = (f32[512,128]{1,0:T(8,128)S(1)}, f32[512,128]{1,0:T(8,128)S(1)}, u32[]{:S(2)}, u32[]{:S(2)}) collective-permute-start(f32[512,128]{1,0:T(8,128)S(1)} %bitcast.80), channel_id=1, source_target_pairs={{0,2},{1,3},{2,0},{3,1},{4,6},{5,7},{6,4},{7,5},{8,10},{9,11},{10,... | collective-permute-start | bytes 786440 | tf_op jit(solution)/shard_map/ppermute | solution.py:368
  39.8 12.0 %collective-permute-start.2 = (f32[512,128]{1,0:T(8,128)S(1)}, f32[512,128]{1,0:T(8,128)S(1)}, u32[]{:S(2)}, u32[]{:S(2)}) collective-permute-start(f32[512,128]{1,0:T(8,128)S(1)} %bitcast.81), channel_id=1, source_target_pairs={{0,3},{1,0},{2,1},{3,2},{4,7},{5,4},{6,5},{7,6},{8,11},{9,8},{10,9... | collective-permute-start | bytes 786440 | tf_op jit(solution)/shard_map/ppermute | solution.py:368
  45.0 6.8 %copy-start.2 = (f32[512,128]{1,0:T(8,128)}, f32[512,128]{1,0:T(8,128)S(1)}, u32[]{:S(2)}) copy-start(f32[512,128]{1,0:T(8,128)S(1)} %collective-permute-done.refs_1_) | copy-start | bytes 786436
  51.8 0.7 copy-start.3
  51.8 0.8 copy-start.4
  64.1 1.0 copy-start
  65.1 56.3 %copy-start.5 = (s32[16,128]{1,0:T(8,128)S(1)}, s32[16,128]{1,0:T(8,128)}, u32[]{:S(2)}) copy-start(s32[16,128]{1,0:T(8,128)} %get-tuple-element.7.topo_ref) | copy-start | bytes 24580
  115.0 17.9 %all-to-all-start.2 = ((f32[64,8,128]{2,1,0:T(8,128)}), f32[64,8,128]{2,1,0:T(8,128)S(1)}, u32[]{:S(2)}, u32[]{:S(2)}) async-start(f32[64,8,128]{2,1,0:T(8,128)} %bitcast.78), calls=%async_computation.2 | async-start | bytes 524288 | tf_op jit(solution)/shard_map/all_to_all | solution.py:419

commit v6 on v5

--- a/solution.py
+++ b/solution.py
@@ -9,7 +9,6 @@
 
 F32 = jnp.float32
 BF16 = jnp.bfloat16
-MASK = F32
 SPREAD_UNROLL = 8
 GATHER_UNROLL = 8
 FINISH_UNROLL = 2
@@ -60,6 +59,31 @@
     ).astype(jnp.int32)
 
 
+def scale_kernel(table_ref, out_ref, *, owners, fields, per_step):
+    step = pl.program_id(0)
+    level = step * per_step // owners
+    slots = table_ref.shape[1]
+    row = lax.broadcasted_iota(jnp.int32, (8, slots), 0)
+    rank = lax.broadcasted_iota(jnp.int32, (8, LANES), 0)
+    left = lax.broadcasted_iota(jnp.int32, (8, LANES), 1) < LANES // 2
+    sides = jnp.where(
+        (left & (rank < 3)) | (~left & (rank >= 3) & (rank < 6)), 1.0, 0.0
+    ).astype(BF16)
+    for item in range(per_step):
+        base = level * (fields - 1) * owners + (step * per_step - level * owners) + item
+        weight = table_ref[pl.ds(base + owners, 1), :]
+        survival = table_ref[pl.ds(base + 2 * owners, 1), :]
+        stacked = jnp.zeros((8, slots), F32)
+        for side, scale in enumerate((weight * survival, weight * ((1.0 - survival) * 0.25))):
+            for part in range(3):
+                high = scale.astype(BF16).astype(F32)
+                stacked = jnp.where(row == 3 * side + part, high, stacked)
+                scale = scale - high
+        out_ref[item * slots : (item + 1) * slots, :] = lax.dot_general(
+            stacked.astype(BF16), sides, (((0,), (0,)), ((), ())), preferred_element_type=F32
+        )
+
+
 def two_parts(value):
     high = value.astype(BF16)
     return high, (value - high.astype(F32)).astype(BF16)
@@ -70,8 +94,9 @@
 
 
 def dag_kernel(
-    input_ref, child_ref, table_ref, topo_ref, scaled_ref, out_ref,
-    current_ref, slot_ref, score_ref, term_ref, sums_ref, adjoint_ref,
+    input_ref, child_ref, table_ref, topo_ref, scaled_ref, scale_ref, out_ref,
+    current_ref, slot_ref, score_ref, term_ref, sums_ref, adjoint_ref, weighted_ref, factor_ref,
+    arrived,
     *, levels, owners, node_dev, site_own, states, fields, out_rows,
 ):
     half = 2 * node_dev
@@ -79,23 +104,34 @@
     chunk = states // 2 * site_own
     child_rows = child_ref.shape[0] // owners
     pitch = slot_ref.shape[0] // slots
+    size = owners * slots
     left = lax.broadcasted_iota(jnp.int32, (LANES, LANES), 1) < LANES // 2
-    left_nodes = left[:node_dev]
-
-    def store_current(start, value, mask):
-        high = value.astype(BF16).astype(F32)
-        current_ref[pl.ds(start, value.shape[0]), :] = jnp.where(
-            mask, high, value - high
-        ).astype(BF16)
-
-    apart = jnp.abs(
-        lax.broadcasted_iota(jnp.int32, (LANES, LANES), 0)
-        - lax.broadcasted_iota(jnp.int32, (LANES, LANES), 1)
-    )
-    fold = (apart % (site_own * states) == 0).astype(F32).astype(BF16)
-    over_states = (apart % site_own == 0).astype(F32).astype(BF16)
+
+    def fetch(level):
+        return pltpu.make_async_copy(
+            scale_ref.at[pl.ds(level * size, size), :], factor_ref.at[level % 2],
+            arrived.at[level % 2],
+        )
+
+    for level in range(min(2, levels)):
+        fetch(level).start()
+
+    def store_current(source, value):
+        high, low = two_parts(value)
+        start = pl.multiple_of(source * half, half)
+        current_ref[pl.ds(start, node_dev), :] = high
+        current_ref[pl.ds(start + node_dev, node_dev), :] = low
+
+    from_lane = lax.broadcasted_iota(jnp.int32, (LANES, LANES), 0)
+    to_lane = lax.broadcasted_iota(jnp.int32, (LANES, LANES), 1)
+    apart = jnp.abs(from_lane - to_lane)
+    over_states = apart % site_own == 0
+    settle = (
+        (apart % (site_own * states) == 0) | (over_states & (from_lane >= LANES // 2))
+    ).astype(F32).astype(BF16)
+    settle = jnp.concatenate([settle, settle], axis=0)
+    over_states = over_states.astype(F32).astype(BF16)
     over_states_twice = jnp.concatenate([over_states, over_states], axis=0)
-    settle = jnp.concatenate([fold, fold, over_states_twice], axis=0)
 
     def load_leaves(pair, carry):
         first = pl.multiple_of(pair * 2 * chunk, chunk)
@@ -106,38 +142,36 @@
             pieces.append(jnp.where(left[:site_own], a, pltpu.roll(b, LANES // 2, 1)))
             pieces.append(jnp.where(left[:site_own], pltpu.roll(a, LANES // 2, 1), b))
         stacked = jnp.concatenate(pieces + pieces, axis=0)
-        store_current(pl.multiple_of(pair * LANES, LANES), stacked.T, left)
+        turned = stacked.T
+        store_current(2 * pair, turned[:node_dev])
+        store_current(2 * pair + 1, turned[node_dev:])
         return carry
 
     lax.fori_loop(0, owners // 2, load_leaves, 0, unroll=LEAF_UNROLL)
 
     node_row = lax.broadcasted_iota(jnp.int32, (node_dev, LANES), 0).astype(F32) + 1.0
-    pair_row = (lax.broadcasted_iota(jnp.int32, (half, slots), 0).astype(F32) + 1.0).astype(MASK)
-    blank = jnp.zeros((node_dev, LANES), BF16)
-    pair_wide = lax.broadcasted_iota(jnp.int32, (half, slots), 0).astype(F32) + 1.0
+    pair_row = lax.broadcasted_iota(jnp.int32, (half, slots), 0).astype(F32) + 1.0
+    blank = jnp.zeros((half, LANES), BF16)
 
     def spread(level):
         def body(pair, carry):
-            rows = current_ref[pl.ds(pl.multiple_of(pair * LANES, LANES), LANES), :]
+            rows = current_ref[pl.ds(pl.multiple_of(pair * 2 * half, 2 * half), 2 * half), :]
             both = jnp.concatenate(
                 [
-                    jnp.concatenate([rows[:node_dev], blank], axis=0),
-                    jnp.concatenate([blank, rows[node_dev:]], axis=0),
+                    jnp.concatenate([rows[:half], blank], axis=0),
+                    jnp.concatenate([blank, rows[half:]], axis=0),
                 ],
                 axis=1,
             )
             for part in range(2):
-                hot = jnp.concatenate(
-                    [
-                        node_row == child_ref[
-                            pl.ds((2 * pair + side) * child_rows + level * 2 + part, 1), :
-                        ]
-                        for side in range(2)
-                    ],
-                    axis=0,
-                )
+                hot = []
+                for side in range(2):
+                    child = child_ref[
+                        pl.ds((2 * pair + side) * child_rows + level * 2 + part, 1), :
+                    ]
+                    hot += [(node_row == child).astype(F32).astype(BF16)] * 2
                 picked = lax.dot_general(
-                    hot.astype(F32).astype(BF16), both, (((0,), (0,)), ((), ())),
+                    jnp.concatenate(hot, axis=0), both, (((0,), (0,)), ((), ())),
                     preferred_element_type=F32,
                 )
                 for side in range(2):
@@ -148,42 +182,36 @@
 
         lax.fori_loop(0, owners // 2, body, 0, unroll=SPREAD_UNROLL)
 
-    def slot_rows(dest):
-        pieces = [
-            slot_ref[pl.ds((rank * owners + dest) * pitch, owners), :]
-            for rank in range(4)
-        ]
-        return jnp.concatenate(pieces, axis=0).astype(BF16)
-
-    def gather(level):
+    def code_of(level, dest):
+        return table_ref[pl.ds(level * (fields - 1) * owners + dest, 1), :]
+
+    def gather(level, last):
+        fetch(level).wait()
+
         def body(dest, carry):
-            base = level * (fields - 1) * owners + dest
-            code = table_ref[pl.ds(base, 1), :]
-            weight = table_ref[pl.ds(base + owners, 1), :]
-            survival = table_ref[pl.ds(base + 2 * owners, 1), :]
-            hit = pair_row == code.astype(MASK)
-            scales = []
-            for scale in (weight * survival, weight * ((1.0 - survival) * 0.25)):
-                high = scale.astype(BF16).astype(F32)
-                scales += [high, scale - high]
-            chosen = jnp.concatenate(
+            rows = jnp.concatenate(
                 [
-                    jnp.where(hit, scale.astype(MASK), jnp.zeros((), MASK)).astype(BF16)
-                    for scale in scales
+                    slot_ref[pl.ds((rank * owners + dest) * pitch, owners), :]
+                    for rank in range(4)
                 ],
                 axis=0,
             )
-            product = jnp.dot(chosen, slot_rows(dest), preferred_element_type=F32)
-            start = pl.multiple_of(dest * half, half)
-            sums_ref[pl.ds(start, half), : 2 * LANES] = both_parts(
-                product[:half] + product[half : 2 * half]
-            )
-            sums_ref[pl.ds(start, half), 2 * LANES :] = both_parts(
-                product[2 * half : 3 * half] + product[3 * half :]
+            factor = factor_ref[
+                level % 2, pl.ds(pl.multiple_of(dest * slots, slots), slots), :
+            ]
+            weighted = both_parts(rows * factor)
+            if last:
+                weighted_ref[pl.ds(pl.multiple_of(dest * slots, slots), slots), :] = weighted
+            hit = (pair_row == code_of(level, dest)).astype(F32).astype(BF16)
+            product = jnp.dot(hit, weighted, preferred_element_type=F32)
+            sums_ref[pl.ds(pl.multiple_of(dest * half, half), half), :] = both_parts(
+                product[:, :LANES] + product[:, LANES:]
             )
             return carry
 
         lax.fori_loop(0, owners, body, 0, unroll=GATHER_UNROLL)
+        if level + 2 < levels:
+            fetch(level + 2).start()
 
     def pair_sums(group):
         rows = GROUP * half
@@ -196,17 +224,20 @@
     group_nodes = GROUP * node_dev
 
     def finish():
-        mask = lax.broadcasted_iota(jnp.int32, (group_nodes, LANES), 1) < LANES // 2
-
         def body(group, carry):
             first, second = pair_sums(group)
-            store_current(pl.multiple_of(group * group_nodes, group_nodes), first * second, mask)
+            value = first * second
+            for item in range(GROUP):
+                store_current(
+                    group * GROUP + item, value[item * node_dev : (item + 1) * node_dev]
+                )
             return carry
 
         lax.fori_loop(0, owners // GROUP, body, 0, unroll=FINISH_UNROLL)
 
     def finish_last():
         lane = lax.broadcasted_iota(jnp.int32, (group_nodes, LANES), 1)
+        wide_left = lax.broadcasted_iota(jnp.int32, (GROUP * half, LANES), 1) < LANES // 2
 
         def body(group, carry):
             first, second = pair_sums(group)
@@ -238,34 +269,37 @@
                 ],
                 axis=0,
             )
-            parts = both_parts(adjoint)
-            summed = both_parts(
-                0.5 * jnp.dot(parts, over_states_twice, preferred_element_type=F32)
-            )
-            for item in range(GROUP):
-                start = pl.multiple_of((group * GROUP + item) * 2 * half, 2 * half)
-                adjoint_ref[pl.ds(start, half), :] = parts[item * half : (item + 1) * half]
-                adjoint_ref[pl.ds(start + half, half), :] = summed[item * half : (item + 1) * half]
+            summed = 0.5 * jnp.dot(
+                both_parts(adjoint), over_states_twice, preferred_element_type=F32
+            )
+            start = pl.multiple_of(group * GROUP * half, GROUP * half)
+            adjoint_ref[pl.ds(start, GROUP * half), :] = both_parts(
+                jnp.where(wide_left, adjoint, summed)
+            )
             return carry
 
         lax.fori_loop(0, owners // GROUP, body, 0, unroll=LAST_UNROLL)
 
     def edges(level):
         def body(dest, carry):
-            base = level * (fields - 1) * owners + dest
-            code = table_ref[pl.ds(base, 1), :]
-            survival = table_ref[pl.ds(base + 2 * owners, 1), :]
-            rows = slot_rows(dest)
+            parts = adjoint_ref[pl.ds(pl.multiple_of(dest * half, half), half), :]
+            high = parts[:, :LANES]
             against = lax.dot_general(
-                adjoint_ref[pl.ds(pl.multiple_of(dest * 2 * half, 2 * half), 2 * half), :],
-                jnp.concatenate([rows, rows], axis=1),
+                jnp.concatenate(
+                    [
+                        jnp.concatenate([high, high], axis=1),
+                        jnp.concatenate([parts[:, LANES:], jnp.zeros_like(high)], axis=1),
+                    ],
+                    axis=0,
+                ),
+                weighted_ref[pl.ds(pl.multiple_of(dest * slots, slots), slots), :],
                 (((1,), (1,)), ((), ())), preferred_element_type=F32,
             )
-            found = pair_wide == code
-            edge = survival * jnp.sum(
-                jnp.where(found, against[:half], 0.0), axis=0, keepdims=True
-            ) + ((1.0 - survival) * 0.25) * jnp.sum(
-                jnp.where(found, against[half:], 0.0), axis=0, keepdims=True
+            edge = jnp.sum(
+                jnp.where(
+                    pair_row == code_of(level, dest), against[:half] + against[half:], 0.0
+                ),
+                axis=0, keepdims=True,
             )
             for part in range(2):
                 term_ref[pl.ds(part * owners + dest, 1), :] = edge[
@@ -277,7 +311,7 @@
 
     for level in range(levels):
         spread(level)
-        gather(level)
+        gather(level, level == levels - 1)
         if level < levels - 1:
             finish()
     finish_last()
@@ -399,23 +433,36 @@
     own_counts = lax.dynamic_slice_in_dim(counts, device * site_own, site_own)
     scaled = jnp.tile(own_counts.astype(F32) / sites_all, LANES // site_own)[None, :]
 
+    per_step = 8
+    scales = pl.pallas_call(
+        functools.partial(scale_kernel, owners=owners, fields=fields, per_step=per_step),
+        grid=(levels * owners // per_step,),
+        in_specs=[pl.BlockSpec(edge_table.shape, lambda step: (0, 0))],
+        out_specs=pl.BlockSpec((per_step * slots, LANES), lambda step: (step, 0)),
+        out_shape=jax.ShapeDtypeStruct((levels * owners * slots, LANES), F32),
+    )(edge_table)
+
     out_rows = 8
     partial = pl.pallas_call(
         functools.partial(
             dag_kernel, levels=levels, owners=owners, node_dev=node_dev, site_own=site_own,
             states=states, fields=fields, out_rows=out_rows,
         ),
+        in_specs=[vmem] * 5 + [pl.BlockSpec(memory_space=pl.ANY)],
         out_shape=jax.ShapeDtypeStruct((owners * out_rows, LANES), F32),
         scratch_shapes=[
-            pltpu.VMEM((owners * node_dev, LANES), BF16),
+            pltpu.VMEM((2 * owners * node_dev, LANES), BF16),
             pltpu.VMEM((slots * (owners + 1), LANES), F32),
             pltpu.VMEM((owners // GROUP, GROUP * node_dev), F32),
             pltpu.VMEM((2 * owners, LANES), F32),
-            pltpu.VMEM((2 * owners * node_dev, 4 * LANES), BF16),
-            pltpu.VMEM((4 * owners * node_dev, 2 * LANES), BF16),
+            pltpu.VMEM((2 * owners * node_dev, 2 * LANES), BF16),
+            pltpu.VMEM((2 * owners * node_dev, 2 * LANES), BF16),
+            pltpu.VMEM((owners * slots, 2 * LANES), BF16),
+            pltpu.VMEM((2, owners * slots, LANES), F32),
+            pltpu.SemaphoreType.DMA((2,)),
         ],
         compiler_params=pltpu.CompilerParams(vmem_limit_bytes=56 * 1024 * 1024),
-    )(received, child_table, edge_table, topologies, scaled)
+    )(received, child_table, edge_table, topologies, scaled, scales)
     shares = lax.all_to_all(
         partial.reshape(owners, out_rows, LANES), "node", split_axis=0, concat_axis=0, tiled=True
     )
@@ -423,7 +470,7 @@
     multiplicity = jnp.sum(
         (topologies.reshape(-1)[None, :] == parents[levels - 1][:, None]).astype(F32), axis=1
     )
-    edge_gradient = multiplicity * jnp.sum(
+    edge_gradient = multiplicity / weights[levels - 1] * jnp.sum(
         jnp.where(slot[levels - 1][:, None] == jnp.arange(slots)[None, :], mine[None, :slots], 0.0),
         axis=1,
     )

time: 146 us -> 147 us (level)
  waiting for transfers between devices: 35.8 us -> 29.3 us
  Pallas kernels: 58.3 us -> 63.7 us
  starting transfers between devices: 29.2 us -> 32.7 us
  blocking collectives: 10.7 us -> 8.32 us
    pallas_call x0 -> x1, Pallas kernels: none -> 17.8 us  [on_device(): pl.pallas_call(functools.partial(scale_kernel, owners=owners, fields=fiel...]
    pallas_call x1, Pallas kernels: 49.9 us -> 37.5 us  [on_device(): pl.pallas_call(functools.partial(dag_kernel, levels=levels, owners=owners...]
    all_to_all x1, waiting for transfers between devices: 8.79 us -> 0.01 us  [on_device(): lax.all_to_all(packed.reshape(owners, chunk, LANES), 'node', split_axis=0...]
    all_to_all x1, starting transfers between devices: 5.66 us -> 10.3 us  [on_device(): lax.all_to_all(partial.reshape(owners, out_rows, LANES), 'node', split_ax...]
    ppermute x3, waiting for transfers between devices: 9.24 us -> 12.2 us  [on_device(): lax.ppermute(share, 'site', [(k, (k + step) % shares) for k in range(shar...]
    psum x1, blocking collectives: 10.7 us -> 8.32 us  [on_device(): lax.psum(jnp.sum(shares[:, :slots // LANES + 1], axis=0), 'site')]
  transfers between devices with their start and end apart: 6 -> 6, of which waited for: 5 -> 4; matrix products, arithmetic and copies ran while one was open for 2% -> 2% of each run, Pallas kernels for 6% -> 18%
where the time goes in v6:
time: 147 us; the launch traced here: 146 us
  Pallas kernels  63.7 us (43%)
  starting transfers between devices  32.7 us (22%)
  waiting for transfers between devices  29.3 us (20%)
  blocking collectives  8.32 us (6%)
  local copies, waits for them, and re-layouts  6.26 us (4%)
  other arithmetic  4.78 us (3%)
    pallas_call x1, Pallas kernels, on_device(): pl.pallas_call(functools.partial(dag_kernel, levels=levels, owners=owners...  37.5 us
    pallas_call x1, Pallas kernels, on_device(): pl.pallas_call(functools.partial(scale_kernel, owners=owners, fields=fiel...  17.8 us
    ppermute x3, waiting for transfers between devices, on_device(): lax.ppermute(share, 'site', [(k, (k + step) % shares) for k in range(shar...  12.2 us
    all_to_all x1, starting transfers between devices, on_device(): lax.all_to_all(jnp.broadcast_to(share[None], (owners, share_rows, LANES))...  12 us
    all_to_all x1, waiting for transfers between devices, on_device(): lax.all_to_all(partial.reshape(owners, out_rows, LANES), 'node', split_ax...  10.5 us
    all_to_all x1, starting transfers between devices, on_device(): lax.all_to_all(partial.reshape(owners, out_rows, LANES), 'node', split_ax...  10.3 us
    psum x1, blocking collectives, on_device(): lax.psum(jnp.sum(shares[:, :slots // LANES + 1], axis=0), 'site')  8.32 us
    all_to_all x1, waiting for transfers between devices, on_device(): lax.all_to_all(jnp.broadcast_to(share[None], (owners, share_rows, LANES))...  6.56 us
  transfers between devices with their start and end apart: 6, of which 4 were waited for; matrix products, arithmetic and copies ran while one was open for 2% of the time, Pallas kernels for 18%

profile of v6, /device:TPU:2, one launch (start us, length us, event | category | flops | bytes accessed | tf_op | source)
XLA Modules:
  0.0 145.8 jit_solution(2892817267161480700)
XLA Ops:
  0.6 0.8 fusion.25
  1.5 0.7 convert_element_type.58
  2.2 0.7 exponential_bitcast_fusion
  3.1 0.2 convert_reduce_fusion.1
  3.5 0.7 pad_maximum_fusion
  4.2 0.4 select_reduce_fusion
  4.6 0.7 broadcast_in_dim.54
  5.3 12.0 %all-to-all-start.1 = ((f32[64,8,128]{2,1,0:T(8,128)}), f32[64,8,128]{2,1,0:T(8,128)S(1)}, u32[]{:S(2)}, u32[]{:S(2)}) async-start(f32[64,8,128]{2,1,0:T(8,128)} %broadcast_in_dim.54), calls=%async_computation.1 | async-start | bytes 524288 | tf_op jit(solution)/shard_map/all_to_all | solution.py:397
  17.4 5.7 %shard_map.77 = f32[2048,128]{1,0:T(8,128)} custom-call(f32[64,4,1024]{2,1,0:T(4,128)} %leaf_ref.1), custom_call_target="tpu_custom_call" | custom-call | tf_op jit(solution)/shard_map/pallas_call | solution.py:423
  23.0 6.6 %all-to-all-done.1 = f32[64,8,128]{2,1,0:T(8,128)S(1)} async-done(((f32[64,8,128]{2,1,0:T(8,128)}), f32[64,8,128]{2,1,0:T(8,128)S(1)}, u32[]{:S(2)}, u32[]{:S(2)}) %all-to-all-start.1) | async-done | bytes 262176 | tf_op jit(solution)/shard_map/all_to_all | solution.py:397
  29.6 5.7 %all-to-all-start = ((f32[64,32,128]{2,1,0:T(8,128)}), f32[64,32,128]{2,1,0:T(8,128)S(1)}, u32[]{:S(2)}, u32[]{:S(2)}) async-start(f32[64,32,128]{2,1,0:T(8,128)} %bitcast.78), calls=%async_computation | async-start | bytes 2097152 | tf_op jit(solution)/shard_map/all_to_all | solution.py:430
  35.2 3.1 %collective-permute-start.2 = (f32[512,128]{1,0:T(8,128)S(1)}, f32[512,128]{1,0:T(8,128)S(1)}, u32[]{:S(2)}, u32[]{:S(2)}) collective-permute-start(f32[512,128]{1,0:T(8,128)S(1)} %bitcast.80), channel_id=1, source_target_pairs={{0,3},{1,0},{2,1},{3,2},{4,7},{5,4},{6,5},{7,6},{8,11},{9,8},{10,9... | collective-permute-start | bytes 786440 | tf_op jit(solution)/shard_map/ppermute | solution.py:402
  38.3 0.6 collective-permute-start.1
  39.0 1.0 collective-permute-start
  39.9 0.8 convert_multiply_fusion
  40.7 0.6 broadcast_in_dim_tile.3.scaled_ref
  41.3 8.5 %collective-permute-done.2.refs_3_ = f32[512,128]{1,0:T(8,128)S(1)} collective-permute-done((f32[512,128]{1,0:T(8,128)S(1)}, f32[512,128]{1,0:T(8,128)S(1)}, u32[]{:S(2)}, u32[]{:S(2)}) %collective-permute-start.2) | collective-permute-done | bytes 262176 | tf_op jit(solution)/shard_map/ppermute | solution.py:402
  49.8 3.7 %collective-permute-done.refs_1_ = f32[512,128]{1,0:T(8,128)S(1)} collective-permute-done((f32[512,128]{1,0:T(8,128)S(1)}, f32[512,128]{1,0:T(8,128)S(1)}, u32[]{:S(2)}, u32[]{:S(2)}) %collective-permute-start) | collective-permute-done | bytes 262176 | tf_op jit(solution)/shard_map/ppermute | solution.py:402
  53.5 0.7 copy-done.4
  54.2 2.7 %shard_map.78 = (f32[512,128]{1,0:T(8,128)}, f32[576,256]{1,0:T(8,128)}, s32[16,128]{1,0:T(8,128)}) custom-call(s32[1]{0:T(128)} %bitcast.2.place_ref, f32[512,128]{1,0:T(8,128)} %bitcast.83, f32[512,128]{1,0:T(8,128)} %copy-done.4, f32[512,128]{1,0:T(8,128)} %copy-done.3, f32[512,128]{1,0:T(8,128)} %copy-done.2), custom_call_target="tpu_custom_call" | custom-call | tf_op jit(solution)/shard_map/pallas_call | solution.py:407
  56.9 17.8 %shard_map.79.scale_ref = f32[49152,128]{1,0:T(8,128)} custom-call(f32[576,256]{1,0:T(8,128)} %get-tuple-element.6.table_ref), custom_call_target="tpu_custom_call" | custom-call | tf_op jit(solution)/shard_map/pallas_call | solution.py:437
  74.8 1.1 copy-done
  75.8 37.5 %shard_map.80 = f32[512,128]{1,0:T(8,128)} custom-call(f32[2048,128]{1,0:T(8,128)} %bitcast.77, f32[512,128]{1,0:T(8,128)} %get-tuple-element.5.child_ref, f32[576,256]{1,0:T(8,128)} %get-tuple-element.6.table_ref, s32[16,128]{1,0:T(8,128)} %get-tuple-element.7.topo_ref, f32[1,128]{1,0:T(1,128)} %broadcast_in_dim_tile.3.scaled_ref, ...), custom_call_target="tpu_custom_call" | custom-call | tf_op jit(solution)/shard_map/pallas_call | solution.py:446
  113.3 10.3 %all-to-all-start.2 = ((f32[64,8,128]{2,1,0:T(8,128)}), f32[64,8,128]{2,1,0:T(8,128)S(1)}, u32[]{:S(2)}, u32[]{:S(2)}) async-start(f32[64,8,128]{2,1,0:T(8,128)} %bitcast.79), calls=%async_computation.2 | async-start | bytes 524288 | tf_op jit(solution)/shard_map/all_to_all | solution.py:466
  123.6 0.7 slice.41
  124.3 0.7 slice.42
  125.0 0.3 convert_reduce_fusion
  125.3 10.5 %all-to-all-done.2 = f32[64,8,128]{2,1,0:T(8,128)S(1)} async-done(((f32[64,8,128]{2,1,0:T(8,128)}), f32[64,8,128]{2,1,0:T(8,128)S(1)}, u32[]{:S(2)}, u32[]{:S(2)}) %all-to-all-start.2) | async-done | bytes 262176 | tf_op jit(solution)/shard_map/all_to_all | solution.py:466
  135.9 8.3 %psum.7 = f32[3,128]{1,0:T(4,128)S(1)} all-reduce(f32[3,128]{1,0:T(4,128)S(1)} %slice_reduce_fusion), channel_id=1, replica_groups=mesh['node'=64,'site'=4] {'site'}, use_global_device_ids=true, to_apply=%region_3.4 | all-reduce | flops 384 | bytes 3072 | tf_op jit(solution)/shard_map/psum | solution.py:469
  144.4 0.6 reshape.242
  145.0 0.2 select_reduce_fusion.1
  145.2 0.6 divide_multiply_fusion
  (30 shorter events, 0.7 us)
Async XLA Ops:
  5.3 24.2 %all-to-all-start.1 = ((f32[64,8,128]{2,1,0:T(8,128)}), f32[64,8,128]{2,1,0:T(8,128)S(1)}, u32[]{:S(2)}, u32[]{:S(2)}) async-start(f32[64,8,128]{2,1,0:T(8,128)} %broadcast_in_dim.54), calls=%async_computation.1 | async-start | bytes 524288 | tf_op jit(solution)/shard_map/all_to_all | solution.py:397
  29.6 24.0 %copy-start.1 = (f32[64,8,128]{2,1,0:T(8,128)}, f32[64,8,128]{2,1,0:T(8,128)S(1)}, u32[]{:S(2)}) copy-start(f32[64,8,128]{2,1,0:T(8,128)S(1)} %all-to-all-done.1) | copy-start | bytes 786436
  29.6 45.2 %all-to-all-start = ((f32[64,32,128]{2,1,0:T(8,128)}), f32[64,32,128]{2,1,0:T(8,128)S(1)}, u32[]{:S(2)}, u32[]{:S(2)}) async-start(f32[64,32,128]{2,1,0:T(8,128)} %bitcast.78), calls=%async_computation | async-start | bytes 2097152 | tf_op jit(solution)/shard_map/all_to_all | solution.py:430
  35.2 14.6 %collective-permute-start.2 = (f32[512,128]{1,0:T(8,128)S(1)}, f32[512,128]{1,0:T(8,128)S(1)}, u32[]{:S(2)}, u32[]{:S(2)}) collective-permute-start(f32[512,128]{1,0:T(8,128)S(1)} %bitcast.80), channel_id=1, source_target_pairs={{0,3},{1,0},{2,1},{3,2},{4,7},{5,4},{6,5},{7,6},{8,11},{9,8},{10,9... | collective-permute-start | bytes 786440 | tf_op jit(solution)/shard_map/ppermute | solution.py:402
  38.3 11.5 %collective-permute-start.1 = (f32[512,128]{1,0:T(8,128)S(1)}, f32[512,128]{1,0:T(8,128)S(1)}, u32[]{:S(2)}, u32[]{:S(2)}) collective-permute-start(f32[512,128]{1,0:T(8,128)S(1)} %bitcast.81), channel_id=1, source_target_pairs={{0,2},{1,3},{2,0},{3,1},{4,6},{5,7},{6,4},{7,5},{8,10},{9,11},{10,... | collective-permute-start | bytes 786440 | tf_op jit(solution)/shard_map/ppermute | solution.py:402
  39.0 14.6 %collective-permute-start = (f32[512,128]{1,0:T(8,128)S(1)}, f32[512,128]{1,0:T(8,128)S(1)}, u32[]{:S(2)}, u32[]{:S(2)}) collective-permute-start(f32[512,128]{1,0:T(8,128)S(1)} %bitcast.82), channel_id=1, source_target_pairs={{0,1},{1,2},{2,3},{3,0},{4,5},{5,6},{6,7},{7,4},{8,9},{9,10},{10,1... | collective-permute-start | bytes 786440 | tf_op jit(solution)/shard_map/ppermute | solution.py:402
  49.8 3.7 %copy-start.2 = (f32[512,128]{1,0:T(8,128)}, f32[512,128]{1,0:T(8,128)S(1)}, u32[]{:S(2)}) copy-start(f32[512,128]{1,0:T(8,128)S(1)} %collective-permute-done.2.refs_3_) | copy-start | bytes 786436
  49.8 3.7 %copy-start.3 = (f32[512,128]{1,0:T(8,128)}, f32[512,128]{1,0:T(8,128)S(1)}, u32[]{:S(2)}) copy-start(f32[512,128]{1,0:T(8,128)S(1)} %collective-permute-done.1.refs_2_) | copy-start | bytes 786436
  53.5 0.7 copy-start.4
  74.7 1.1 copy-start
  75.8 49.2 %copy-start.5 = (s32[16,128]{1,0:T(8,128)S(1)}, s32[16,128]{1,0:T(8,128)}, u32[]{:S(2)}) copy-start(s32[16,128]{1,0:T(8,128)} %get-tuple-element.7.topo_ref) | copy-start | bytes 24580
  113.3 22.5 %all-to-all-start.2 = ((f32[64,8,128]{2,1,0:T(8,128)}), f32[64,8,128]{2,1,0:T(8,128)S(1)}, u32[]{:S(2)}, u32[]{:S(2)}) async-start(f32[64,8,128]{2,1,0:T(8,128)} %bitcast.79), calls=%async_computation.2 | async-start | bytes 524288 | tf_op jit(solution)/shard_map/all_to_all | solution.py:466

commit v7 on v6

--- a/solution.py
+++ b/solution.py
@@ -11,8 +11,8 @@
 BF16 = jnp.bfloat16
 SPREAD_UNROLL = 8
 GATHER_UNROLL = 8
-FINISH_UNROLL = 2
-LAST_UNROLL = 2
+FINISH_UNROLL = 4
+LAST_UNROLL = 4
 EDGE_UNROLL = 8
 LEAF_UNROLL = 4
 LANES = 128
@@ -28,6 +28,62 @@
             out_ref[peer * chunk + pair * site_own : peer * chunk + (pair + 1) * site_own, :] = (
                 rows[peer * site_own : (peer + 1) * site_own]
             )
+
+
+def slot_kernel(
+    where_ref, dag_ref, weight_ref, length_ref, topo_ref, share_ref, slot_ref, meta_ref,
+    *, levels, owners, node_dev, fields, share_rows,
+):
+    edges = weight_ref.shape[1]
+    slots = 4 * owners
+
+    def rows(count):
+        return lax.broadcasted_iota(jnp.int32, (count, edges), 0)
+
+    earlier = rows(edges) < lax.broadcasted_iota(jnp.int32, (edges, edges), 1)
+    earlier = earlier.astype(F32).astype(BF16)
+    meta_ref[...] = jnp.zeros(meta_ref.shape, F32)
+    field_row = rows(8)
+    for level in range(levels):
+        child = dag_ref[level : level + 1, :] - where_ref[0] * node_dev
+        parent = dag_ref[levels + level : levels + level + 1, :]
+        rotation = dag_ref[2 * levels + level : 2 * levels + level + 1, :]
+        owner_of = parent // node_dev
+        code = rotation * node_dev + parent - owner_of * node_dev
+        goes = (rows(owners) == owner_of).astype(F32)
+        before = jnp.dot(goes.astype(BF16), earlier, preferred_element_type=F32)
+        rank = jnp.sum(goes * before, axis=0, keepdims=True)
+        slot = rank.astype(jnp.int32) * owners + owner_of
+        slot_ref[level : level + 1, :] = slot
+        values = jnp.zeros((8, edges), F32)
+        for field, value in enumerate(
+            (
+                (child + 1).astype(F32), (code + 1).astype(F32), weight_ref[level : level + 1, :],
+                jnp.exp(length_ref[level : level + 1, :] * (-4.0 / 3.0)),
+            )
+        ):
+            values = jnp.where(field_row == field, value, values)
+        parts = []
+        for _ in range(3):
+            parts.append(values.astype(BF16).astype(F32))
+            values = values - parts[-1]
+        found = lax.dot_general(
+            jnp.concatenate(parts, axis=0).astype(BF16),
+            (rows(slots) == slot).astype(F32).astype(BF16),
+            (((1,), (1,)), ((), ())), preferred_element_type=F32,
+        )
+        found = found[:8] + found[8:16] + found[16:]
+        for field in range(fields):
+            for part in range(2):
+                row = (field * levels + level) * 2 + part
+                meta_ref[row : row + 1, :] = found[
+                    field : field + 1, part * LANES : (part + 1) * LANES
+                ]
+    row = fields * levels * 2
+    meta_ref[row : row + 1, : topo_ref.shape[1]] = topo_ref[...].astype(F32)
+    share = meta_ref[pl.ds(pl.multiple_of(where_ref[1] * share_rows, share_rows), share_rows), :]
+    for owner in range(owners):
+        share_ref[owner * share_rows : (owner + 1) * share_rows, :] = share
 
 
 def table_kernel(
@@ -54,34 +110,12 @@
                     part * LANES : (part + 1) * LANES,
                 ] = jnp.concatenate([block[:owners], block[owners:]], axis=1)
     block = rows_of(fields * levels * 2).T
-    topo_ref[...] = jnp.concatenate(
-        [block[:entries], block[entries : 2 * entries]], axis=1
-    ).astype(jnp.int32)
-
-
-def scale_kernel(table_ref, out_ref, *, owners, fields, per_step):
-    step = pl.program_id(0)
-    level = step * per_step // owners
-    slots = table_ref.shape[1]
-    row = lax.broadcasted_iota(jnp.int32, (8, slots), 0)
-    rank = lax.broadcasted_iota(jnp.int32, (8, LANES), 0)
-    left = lax.broadcasted_iota(jnp.int32, (8, LANES), 1) < LANES // 2
-    sides = jnp.where(
-        (left & (rank < 3)) | (~left & (rank >= 3) & (rank < 6)), 1.0, 0.0
-    ).astype(BF16)
-    for item in range(per_step):
-        base = level * (fields - 1) * owners + (step * per_step - level * owners) + item
-        weight = table_ref[pl.ds(base + owners, 1), :]
-        survival = table_ref[pl.ds(base + 2 * owners, 1), :]
-        stacked = jnp.zeros((8, slots), F32)
-        for side, scale in enumerate((weight * survival, weight * ((1.0 - survival) * 0.25))):
-            for part in range(3):
-                high = scale.astype(BF16).astype(F32)
-                stacked = jnp.where(row == 3 * side + part, high, stacked)
-                scale = scale - high
-        out_ref[item * slots : (item + 1) * slots, :] = lax.dot_general(
-            stacked.astype(BF16), sides, (((0,), (0,)), ((), ())), preferred_element_type=F32
-        )
+    use = entries // 2
+    for part in range(2):
+        start = 2 * part * use
+        topo_ref[part * use : (part + 1) * use, :] = jnp.concatenate(
+            [block[start : start + use], block[start + use : start + 2 * use]], axis=1
+        ).astype(jnp.int32)
 
 
 def two_parts(value):
@@ -94,9 +128,8 @@
 
 
 def dag_kernel(
-    input_ref, child_ref, table_ref, topo_ref, scaled_ref, scale_ref, out_ref,
-    current_ref, slot_ref, score_ref, term_ref, sums_ref, adjoint_ref, weighted_ref, factor_ref,
-    arrived,
+    input_ref, child_ref, table_ref, topo_ref, scaled_ref, out_ref,
+    current_ref, slot_ref, score_ref, term_ref, sums_ref, adjoint_ref, weighted_ref,
     *, levels, owners, node_dev, site_own, states, fields, out_rows,
 ):
     half = 2 * node_dev
@@ -104,17 +137,7 @@
     chunk = states // 2 * site_own
     child_rows = child_ref.shape[0] // owners
     pitch = slot_ref.shape[0] // slots
-    size = owners * slots
     left = lax.broadcasted_iota(jnp.int32, (LANES, LANES), 1) < LANES // 2
-
-    def fetch(level):
-        return pltpu.make_async_copy(
-            scale_ref.at[pl.ds(level * size, size), :], factor_ref.at[level % 2],
-            arrived.at[level % 2],
-        )
-
-    for level in range(min(2, levels)):
-        fetch(level).start()
 
     def store_current(source, value):
         high, low = two_parts(value)
@@ -185,9 +208,28 @@
     def code_of(level, dest):
         return table_ref[pl.ds(level * (fields - 1) * owners + dest, 1), :]
 
+    part_row = lax.broadcasted_iota(jnp.int32, (8, slots), 0)
+    part_rank = lax.broadcasted_iota(jnp.int32, (8, LANES), 0)
+    part_left = lax.broadcasted_iota(jnp.int32, (8, LANES), 1) < LANES // 2
+    sides = jnp.where(
+        (part_left & (part_rank < 3)) | (~part_left & (part_rank >= 3) & (part_rank < 6)), 1.0, 0.0
+    ).astype(BF16)
+
+    def factor_of(level, dest):
+        base = level * (fields - 1) * owners + dest
+        weight = table_ref[pl.ds(base + owners, 1), :]
+        survival = table_ref[pl.ds(base + 2 * owners, 1), :]
+        stacked = jnp.zeros((8, slots), F32)
+        for side, scale in enumerate((weight * survival, weight * ((1.0 - survival) * 0.25))):
+            for part in range(3):
+                high = scale.astype(BF16).astype(F32)
+                stacked = jnp.where(part_row == 3 * side + part, high, stacked)
+                scale = scale - high
+        return lax.dot_general(
+            stacked.astype(BF16), sides, (((0,), (0,)), ((), ())), preferred_element_type=F32
+        )
+
     def gather(level, last):
-        fetch(level).wait()
-
         def body(dest, carry):
             rows = jnp.concatenate(
                 [
@@ -196,9 +238,7 @@
                 ],
                 axis=0,
             )
-            factor = factor_ref[
-                level % 2, pl.ds(pl.multiple_of(dest * slots, slots), slots), :
-            ]
+            factor = factor_of(level, dest)
             weighted = both_parts(rows * factor)
             if last:
                 weighted_ref[pl.ds(pl.multiple_of(dest * slots, slots), slots), :] = weighted
@@ -210,8 +250,6 @@
             return carry
 
         lax.fori_loop(0, owners, body, 0, unroll=GATHER_UNROLL)
-        if level + 2 < levels:
-            fetch(level + 2).start()
 
     def pair_sums(group):
         rows = GROUP * half
@@ -334,7 +372,7 @@
             for piece in (score_high, score_middle, score_low)
         )
         row = lax.broadcasted_iota(jnp.int32, (group_nodes, LANES), 0)
-        totals[chunk % 2] = totals[chunk % 2] + jnp.sum(
+        totals[chunk * 2 // topo_ref.shape[0]] = totals[chunk * 2 // topo_ref.shape[0]] + jnp.sum(
             jnp.where(row == local_of, found, 0.0), axis=0, keepdims=True
         )
     def place(row, block):
@@ -360,62 +398,50 @@
     fields = 4
     topo_dev, use = topo_nodes.shape
 
-    child = dag_edges[:, :, 0] - device * node_dev
-    parents = dag_edges[:, :, 1]
-    owner_of = parents // node_dev
-    code = dag_edges[:, :, 2] * node_dev + parents - owner_of * node_dev
-    earlier = jnp.arange(edge_dev)[:, None] < jnp.arange(edge_dev)[None, :]
-    rank = jnp.sum(
-        ((owner_of[:, :, None] == owner_of[:, None, :]) & earlier[None]).astype(jnp.int32), axis=1
+    halves = topo_dev // 2
+    vmem = pl.BlockSpec(memory_space=pltpu.VMEM)
+    smem = pl.BlockSpec(memory_space=pltpu.SMEM)
+    shares = lax.axis_size("site")
+    share_rows = -(-(fields * levels * 2 + 1) // (8 * shares)) * 8
+    place = lax.axis_index("site")
+    share, slot = pl.pallas_call(
+        functools.partial(
+            slot_kernel, levels=levels, owners=owners, node_dev=node_dev, fields=fields,
+            share_rows=share_rows,
+        ),
+        in_specs=[smem] + [vmem] * 4,
+        out_shape=[
+            jax.ShapeDtypeStruct((owners * share_rows, LANES), F32),
+            jax.ShapeDtypeStruct((levels, edge_dev), jnp.int32),
+        ],
+        scratch_shapes=[pltpu.VMEM((share_rows * shares, LANES), F32)],
+    )(
+        jnp.stack([device, place]).astype(jnp.int32),
+        dag_edges.transpose(2, 0, 1).reshape(3 * levels, edge_dev), weights, lengths,
+        topo_nodes.reshape(1, -1),
     )
-    slot = rank * owners + owner_of
-    chosen = slot[:, None, :] == jnp.arange(slots)[None, :, None]
-    values = jnp.stack(
-        [
-            (child + 1).astype(F32), (code + 1).astype(F32), weights,
-            jnp.exp(lengths * (-4.0 / 3.0)),
-        ]
-    )
-    by_slot = jnp.sum(jnp.where(chosen[None], values[:, :, None, :], 0.0), axis=3)
-    halves = topo_dev // 2
-    topo = topo_nodes.reshape(halves, 2, use).transpose(1, 2, 0).reshape(1, -1).astype(F32)
-    meta = by_slot.reshape(fields * levels * 2, LANES)
-    shares = lax.axis_size("site")
-    share_rows = -(-(meta.shape[0] + 1) // (8 * shares)) * 8
-    place = lax.axis_index("site")
-    meta = jnp.concatenate(
-        [
-            meta,
-            jnp.pad(
-                topo,
-                ((0, share_rows * shares - meta.shape[0] - 1), (0, LANES - topo.shape[1])),
-            ),
-        ],
-        axis=0,
-    )
-    share = lax.dynamic_slice_in_dim(meta, place * share_rows, share_rows)
     share = lax.all_to_all(
-        jnp.broadcast_to(share[None], (owners, share_rows, LANES)), "node",
+        share.reshape(owners, share_rows, LANES), "node",
         split_axis=0, concat_axis=0, tiled=True,
     ).reshape(owners * share_rows, LANES)
     met = [share] + [
         lax.ppermute(share, "site", [(k, (k + step) % shares) for k in range(shares)])
         for step in range(1, shares)
     ]
-    vmem = pl.BlockSpec(memory_space=pltpu.VMEM)
     entries = use * halves
     child_table, edge_table, topologies = pl.pallas_call(
         functools.partial(
             table_kernel, levels=levels, owners=owners, fields=fields, shares=shares,
             share_rows=share_rows, entries=entries,
         ),
-        in_specs=[pl.BlockSpec(memory_space=pltpu.SMEM)] + [vmem] * shares,
+        in_specs=[smem] + [vmem] * shares,
         out_shape=[
             jax.ShapeDtypeStruct((owners * share_rows, LANES), F32),
             jax.ShapeDtypeStruct((levels * (fields - 1) * owners, slots), F32),
             jax.ShapeDtypeStruct((entries, LANES), jnp.int32),
         ],
         scratch_shapes=[pltpu.VMEM((owners * share_rows * shares, LANES), F32)],
+        compiler_params=pltpu.CompilerParams(vmem_limit_bytes=8 * 1024 * 1024),
     )(place.astype(jnp.int32).reshape(1), *met)
 
     chunk = states // 2 * site_own
@@ -433,22 +459,13 @@
     own_counts = lax.dynamic_slice_in_dim(counts, device * site_own, site_own)
     scaled = jnp.tile(own_counts.astype(F32) / sites_all, LANES // site_own)[None, :]
 
-    per_step = 8
-    scales = pl.pallas_call(
-        functools.partial(scale_kernel, owners=owners, fields=fields, per_step=per_step),
-        grid=(levels * owners // per_step,),
-        in_specs=[pl.BlockSpec(edge_table.shape, lambda step: (0, 0))],
-        out_specs=pl.BlockSpec((per_step * slots, LANES), lambda step: (step, 0)),
-        out_shape=jax.ShapeDtypeStruct((levels * owners * slots, LANES), F32),
-    )(edge_table)
-
     out_rows = 8
     partial = pl.pallas_call(
         functools.partial(
             dag_kernel, levels=levels, owners=owners, node_dev=node_dev, site_own=site_own,
             states=states, fields=fields, out_rows=out_rows,
         ),
-        in_specs=[vmem] * 5 + [pl.BlockSpec(memory_space=pl.ANY)],
+        in_specs=[vmem] * 5,
         out_shape=jax.ShapeDtypeStruct((owners * out_rows, LANES), F32),
         scratch_shapes=[
             pltpu.VMEM((2 * owners * node_dev, LANES), BF16),
@@ -458,17 +475,15 @@
             pltpu.VMEM((2 * owners * node_dev, 2 * LANES), BF16),
             pltpu.VMEM((2 * owners * node_dev, 2 * LANES), BF16),
             pltpu.VMEM((owners * slots, 2 * LANES), BF16),
-            pltpu.VMEM((2, owners * slots, LANES), F32),
-            pltpu.SemaphoreType.DMA((2,)),
         ],
-        compiler_params=pltpu.CompilerParams(vmem_limit_bytes=56 * 1024 * 1024),
-    )(received, child_table, edge_table, topologies, scaled, scales)
+        compiler_params=pltpu.CompilerParams(vmem_limit_bytes=40 * 1024 * 1024),
+    )(received, child_table, edge_table, topologies, scaled)
     shares = lax.all_to_all(
         partial.reshape(owners, out_rows, LANES), "node", split_axis=0, concat_axis=0, tiled=True
     )
     mine = lax.psum(jnp.sum(shares[:, : slots // LANES + 1], axis=0), "site").reshape(-1)
     multiplicity = jnp.sum(
-        (topologies.reshape(-1)[None, :] == parents[levels - 1][:, None]).astype(F32), axis=1
+        (topologies.reshape(-1)[None, :] == dag_edges[levels - 1, :, 1][:, None]).astype(F32), axis=1
     )
     edge_gradient = multiplicity / weights[levels - 1] * jnp.sum(
         jnp.where(slot[levels - 1][:, None] == jnp.arange(slots)[None, :], mine[None, :slots], 0.0),

time: 147 us -> 136 us (0.925)
  Pallas kernels: 63.7 us -> 48.4 us
  waiting for transfers between devices: 29.3 us -> 37.8 us
  starting transfers between devices: 32.7 us -> 29.2 us
  blocking collectives: 8.32 us -> 10.7 us
  other arithmetic: 4.78 us -> 2.47 us
    pallas_call x1, Pallas kernels: 17.8 us -> 2.17 us  [on_device(): pl.pallas_call(functools.partial(slot_kernel, levels=levels, owners=owner...]
    all_to_all x1, waiting for transfers between devices: 0.01 us -> 11.6 us  [on_device(): lax.all_to_all(packed.reshape(owners, chunk, LANES), 'node', split_axis=0...]
    all_to_all x1, starting transfers between devices: 10.3 us -> 5.65 us  [on_device(): lax.all_to_all(partial.reshape(owners, out_rows, LANES), 'node', split_ax...]
    ppermute x3, waiting for transfers between devices: 12.2 us -> 9.75 us  [on_device(): lax.ppermute(share, 'site', [(k, (k + step) % shares) for k in range(shar...]
    pallas_call x1, Pallas kernels: 37.5 us -> 39.9 us  [on_device(): pl.pallas_call(functools.partial(dag_kernel, levels=levels, owners=owners...]
    psum x1, blocking collectives: 8.32 us -> 10.7 us  [on_device(): lax.psum(jnp.sum(shares[:, :slots // LANES + 1], axis=0), 'site')]
    pallas_call x1, Pallas kernels: 2.68 us -> 0.67 us  [on_device(): pl.pallas_call(functools.partial(table_kernel, levels=levels, owners=owne...]
    reshape x1 -> x2, local copies, waits for them, and re-layouts: 0.01 us -> 1.91 us  [the longest x1 1.3 us: on_device(): topo_nodes.reshape(1, -1)]
  transfers between devices with their start and end apart: 6 -> 6, of which waited for: 4 -> 5; matrix products, arithmetic and copies ran while one was open for 2% -> 2% of each run, Pallas kernels for 18% -> 5%
where the time goes in v7:
time: 136 us; the launch traced here: 135 us
  Pallas kernels  48.4 us (36%)
  waiting for transfers between devices  37.8 us (28%)
  starting transfers between devices  29.2 us (21%)
  blocking collectives  10.7 us (8%)
  local copies, waits for them, and re-layouts  5.55 us (4%)
  other arithmetic  2.47 us (2%)
    pallas_call x1, Pallas kernels, on_device(): pl.pallas_call(functools.partial(dag_kernel, levels=levels, owners=owners...  39.9 us
    all_to_all x1, starting transfers between devices, on_device(): lax.all_to_all(share.reshape(owners, share_rows, LANES), 'node', split_ax...  12 us
    all_to_all x1, waiting for transfers between devices, on_device(): lax.all_to_all(packed.reshape(owners, chunk, LANES), 'node', split_axis=0...  11.6 us
    psum x1, blocking collectives, on_device(): lax.psum(jnp.sum(shares[:, :slots // LANES + 1], axis=0), 'site')  10.7 us
    all_to_all x1, waiting for transfers between devices, on_device(): lax.all_to_all(partial.reshape(owners, out_rows, LANES), 'node', split_ax...  9.86 us
    ppermute x3, waiting for transfers between devices, on_device(): lax.ppermute(share, 'site', [(k, (k + step) % shares) for k in range(shar...  9.75 us
    all_to_all x1, waiting for transfers between devices, on_device(): lax.all_to_all(share.reshape(owners, share_rows, LANES), 'node', split_ax...  6.57 us
    ppermute x3, starting transfers between devices, on_device(): lax.ppermute(share, 'site', [(k, (k + step) % shares) for k in range(shar...  5.9 us
  transfers between devices with their start and end apart: 6, of which 5 were waited for; matrix products, arithmetic and copies ran while one was open for 2% of the time, Pallas kernels for 5%

profile of v7, /device:TPU:2, one launch (start us, length us, event | category | flops | bytes accessed | tf_op | source)
XLA Modules:
  0.0 134.9 jit_solution(6093557892371354815)
XLA Ops:
  0.6 0.7 copy.11
  1.3 0.6 reshape.45.dag_ref
  2.0 1.3 reshape.46.topo_ref
  3.3 0.6 pad_add_fusion.where_ref
  3.8 2.2 %shard_map.78 = (f32[512,128]{1,0:T(8,128)}, s32[3,192]{1,0:T(4,128)}) custom-call(s32[2]{0:T(128)} %pad_add_fusion.where_ref, s32[9,192]{1,0:T(8,128)} %reshape.45.dag_ref, f32[3,192]{1,0:T(4,128)} %weight_ref.1, f32[3,192]{1,0:T(4,128)} %length_ref.1, s32[1,32]{1,0:T(1,128)} %reshape.46.topo_ref), custom_call_target="tpu_custom_call" | custom-call | tf_op jit(solution)/shard_map/pallas_call | solution.py:407
  6.0 12.0 %all-to-all-start.1 = ((f32[64,8,128]{2,1,0:T(8,128)}), f32[64,8,128]{2,1,0:T(8,128)S(1)}, u32[]{:S(2)}, u32[]{:S(2)}) async-start(f32[64,8,128]{2,1,0:T(8,128)} %bitcast.23), calls=%async_computation.1 | async-start | bytes 524288 | tf_op jit(solution)/shard_map/all_to_all | solution.py:423
  18.0 5.7 %shard_map.77 = f32[2048,128]{1,0:T(8,128)} custom-call(f32[64,4,1024]{2,1,0:T(4,128)} %leaf_ref.1), custom_call_target="tpu_custom_call" | custom-call | tf_op jit(solution)/shard_map/pallas_call | solution.py:449
  23.7 6.6 %all-to-all-done.1 = f32[64,8,128]{2,1,0:T(8,128)S(1)} async-done(((f32[64,8,128]{2,1,0:T(8,128)}), f32[64,8,128]{2,1,0:T(8,128)S(1)}, u32[]{:S(2)}, u32[]{:S(2)}) %all-to-all-start.1) | async-done | bytes 262176 | tf_op jit(solution)/shard_map/all_to_all | solution.py:423
  30.2 5.7 %all-to-all-start = ((f32[64,32,128]{2,1,0:T(8,128)}), f32[64,32,128]{2,1,0:T(8,128)S(1)}, u32[]{:S(2)}, u32[]{:S(2)}) async-start(f32[64,32,128]{2,1,0:T(8,128)} %bitcast.22), calls=%async_computation | async-start | bytes 2097152 | tf_op jit(solution)/shard_map/all_to_all | solution.py:456
  35.9 1.7 %collective-permute-start = (f32[512,128]{1,0:T(8,128)S(1)}, f32[512,128]{1,0:T(8,128)S(1)}, u32[]{:S(2)}, u32[]{:S(2)}) collective-permute-start(f32[512,128]{1,0:T(8,128)S(1)} %bitcast.17), channel_id=1, source_target_pairs={{0,1},{1,2},{2,3},{3,0},{4,5},{5,6},{6,7},{7,4},{8,9},{9,10},{10,1... | collective-permute-start | bytes 786440 | tf_op jit(solution)/shard_map/ppermute | solution.py:428
  37.6 2.9 %collective-permute-start.1 = (f32[512,128]{1,0:T(8,128)S(1)}, f32[512,128]{1,0:T(8,128)S(1)}, u32[]{:S(2)}, u32[]{:S(2)}) collective-permute-start(f32[512,128]{1,0:T(8,128)S(1)} %bitcast.18), channel_id=1, source_target_pairs={{0,2},{1,3},{2,0},{3,1},{4,6},{5,7},{6,4},{7,5},{8,10},{9,11},{10,... | collective-permute-start | bytes 786440 | tf_op jit(solution)/shard_map/ppermute | solution.py:428
  40.5 1.4 %collective-permute-start.2 = (f32[512,128]{1,0:T(8,128)S(1)}, f32[512,128]{1,0:T(8,128)S(1)}, u32[]{:S(2)}, u32[]{:S(2)}) collective-permute-start(f32[512,128]{1,0:T(8,128)S(1)} %bitcast.19), channel_id=1, source_target_pairs={{0,3},{1,0},{2,1},{3,2},{4,7},{5,4},{6,5},{7,6},{8,11},{9,8},{10,9... | collective-permute-start | bytes 786440 | tf_op jit(solution)/shard_map/ppermute | solution.py:428
  41.8 0.8 convert_multiply_fusion
  42.6 0.1 broadcast_in_dim_tile.3.scaled_ref
  42.7 3.0 %collective-permute-done.refs_1_ = f32[512,128]{1,0:T(8,128)S(1)} collective-permute-done((f32[512,128]{1,0:T(8,128)S(1)}, f32[512,128]{1,0:T(8,128)S(1)}, u32[]{:S(2)}, u32[]{:S(2)}) %collective-permute-start) | collective-permute-done | bytes 262176 | tf_op jit(solution)/shard_map/ppermute | solution.py:428
  45.6 6.8 %collective-permute-done.1.refs_2_ = f32[512,128]{1,0:T(8,128)S(1)} collective-permute-done((f32[512,128]{1,0:T(8,128)S(1)}, f32[512,128]{1,0:T(8,128)S(1)}, u32[]{:S(2)}, u32[]{:S(2)}) %collective-permute-start.1) | collective-permute-done | bytes 262176 | tf_op jit(solution)/shard_map/ppermute | solution.py:428
  52.4 0.7 shard_map.79
  53.1 11.6 %all-to-all-done = f32[64,32,128]{2,1,0:T(8,128)S(1)} async-done(((f32[64,32,128]{2,1,0:T(8,128)}), f32[64,32,128]{2,1,0:T(8,128)S(1)}, u32[]{:S(2)}, u32[]{:S(2)}) %all-to-all-start) | async-done | bytes 1048608 | tf_op jit(solution)/shard_map/all_to_all | solution.py:456
  64.7 39.9 %shard_map.80 = f32[512,128]{1,0:T(8,128)} custom-call(f32[2048,128]{1,0:T(8,128)S(1)} %bitcast.16, f32[512,128]{1,0:T(8,128)S(1)} %get-tuple-element.8.child_ref, f32[576,256]{1,0:T(8,128)S(1)} %get-tuple-element.9.table_ref, s32[16,128]{1,0:T(8,128)S(1)} %get-tuple-element.10.topo_ref, f32[1,128]{1,0:T(1,128)S(1)} %broadcast_in_dim_tile.3.scaled_ref), custom_call_target="tpu_custom_call" | custom-call | tf_op jit(solution)/shard_map/pallas_call | solution.py:463
  104.6 5.7 %all-to-all-start.2 = ((f32[64,8,128]{2,1,0:T(8,128)}), f32[64,8,128]{2,1,0:T(8,128)S(1)}, u32[]{:S(2)}, u32[]{:S(2)}) async-start(f32[64,8,128]{2,1,0:T(8,128)} %bitcast.7), calls=%async_computation.2 | async-start | bytes 524288 | tf_op jit(solution)/shard_map/all_to_all | solution.py:481
  110.3 0.7 slice.27
  111.0 0.7 slice.28
  111.7 0.7 slice.29
  112.3 0.3 convert_reduce_fusion
  112.6 9.9 %all-to-all-done.2 = f32[64,8,128]{2,1,0:T(8,128)S(1)} async-done(((f32[64,8,128]{2,1,0:T(8,128)}), f32[64,8,128]{2,1,0:T(8,128)S(1)}, u32[]{:S(2)}, u32[]{:S(2)}) %all-to-all-start.2) | async-done | bytes 262176 | tf_op jit(solution)/shard_map/all_to_all | solution.py:481
  122.5 0.1 slice_reduce_fusion
  122.6 10.7 %psum.7 = f32[3,128]{1,0:T(4,128)S(1)} all-reduce(f32[3,128]{1,0:T(4,128)S(1)} %slice_reduce_fusion), channel_id=1, replica_groups=mesh['node'=64,'site'=4] {'site'}, use_global_device_ids=true, to_apply=%region_1.0 | all-reduce | flops 384 | bytes 3072 | tf_op jit(solution)/shard_map/psum | solution.py:484
  133.3 0.1 slice.25
  133.4 0.1 copy.12
  133.5 0.6 reshape.50
  134.1 0.2 select_reduce_fusion
  134.3 0.6 divide_multiply_fusion
  (4 shorter events, 0.0 us)
Async XLA Ops:
  6.0 24.2 %all-to-all-start.1 = ((f32[64,8,128]{2,1,0:T(8,128)}), f32[64,8,128]{2,1,0:T(8,128)S(1)}, u32[]{:S(2)}, u32[]{:S(2)}) async-start(f32[64,8,128]{2,1,0:T(8,128)} %bitcast.23), calls=%async_computation.1 | async-start | bytes 524288 | tf_op jit(solution)/shard_map/all_to_all | solution.py:423
  30.2 34.5 %all-to-all-start = ((f32[64,32,128]{2,1,0:T(8,128)}), f32[64,32,128]{2,1,0:T(8,128)S(1)}, u32[]{:S(2)}, u32[]{:S(2)}) async-start(f32[64,32,128]{2,1,0:T(8,128)} %bitcast.22), calls=%async_computation | async-start | bytes 2097152 | tf_op jit(solution)/shard_map/all_to_all | solution.py:456
  35.9 9.7 %collective-permute-start = (f32[512,128]{1,0:T(8,128)S(1)}, f32[512,128]{1,0:T(8,128)S(1)}, u32[]{:S(2)}, u32[]{:S(2)}) collective-permute-start(f32[512,128]{1,0:T(8,128)S(1)} %bitcast.17), channel_id=1, source_target_pairs={{0,1},{1,2},{2,3},{3,0},{4,5},{5,6},{6,7},{7,4},{8,9},{9,10},{10,1... | collective-permute-start | bytes 786440 | tf_op jit(solution)/shard_map/ppermute | solution.py:428
  37.6 14.8 %collective-permute-start.1 = (f32[512,128]{1,0:T(8,128)S(1)}, f32[512,128]{1,0:T(8,128)S(1)}, u32[]{:S(2)}, u32[]{:S(2)}) collective-permute-start(f32[512,128]{1,0:T(8,128)S(1)} %bitcast.18), channel_id=1, source_target_pairs={{0,2},{1,3},{2,0},{3,1},{4,6},{5,7},{6,4},{7,5},{8,10},{9,11},{10,... | collective-permute-start | bytes 786440 | tf_op jit(solution)/shard_map/ppermute | solution.py:428
  40.5 12.0 %collective-permute-start.2 = (f32[512,128]{1,0:T(8,128)S(1)}, f32[512,128]{1,0:T(8,128)S(1)}, u32[]{:S(2)}, u32[]{:S(2)}) collective-permute-start(f32[512,128]{1,0:T(8,128)S(1)} %bitcast.19), channel_id=1, source_target_pairs={{0,3},{1,0},{2,1},{3,2},{4,7},{5,4},{6,5},{7,6},{8,11},{9,8},{10,9... | collective-permute-start | bytes 786440 | tf_op jit(solution)/shard_map/ppermute | solution.py:428
  104.6 17.9 %all-to-all-start.2 = ((f32[64,8,128]{2,1,0:T(8,128)}), f32[64,8,128]{2,1,0:T(8,128)S(1)}, u32[]{:S(2)}, u32[]{:S(2)}) async-start(f32[64,8,128]{2,1,0:T(8,128)} %bitcast.7), calls=%async_computation.2 | async-start | bytes 524288 | tf_op jit(solution)/shard_map/all_to_all | solution.py:481

commit v8 on v7

--- a/solution.py
+++ b/solution.py
@@ -31,7 +31,7 @@
 
 
 def slot_kernel(
-    where_ref, dag_ref, weight_ref, length_ref, topo_ref, share_ref, slot_ref, meta_ref,
+    dag_ref, weight_ref, length_ref, topo_ref, share_ref, slot_ref, meta_ref,
     *, levels, owners, node_dev, fields, share_rows,
 ):
     edges = weight_ref.shape[1]
@@ -45,9 +45,9 @@
     meta_ref[...] = jnp.zeros(meta_ref.shape, F32)
     field_row = rows(8)
     for level in range(levels):
-        child = dag_ref[level : level + 1, :] - where_ref[0] * node_dev
-        parent = dag_ref[levels + level : levels + level + 1, :]
-        rotation = dag_ref[2 * levels + level : 2 * levels + level + 1, :]
+        child = dag_ref[0, level : level + 1, :] - lax.axis_index("node") * node_dev
+        parent = dag_ref[1, level : level + 1, :]
+        rotation = dag_ref[2, level : level + 1, :]
         owner_of = parent // node_dev
         code = rotation * node_dev + parent - owner_of * node_dev
         goes = (rows(owners) == owner_of).astype(F32)
@@ -80,19 +80,24 @@
                     field : field + 1, part * LANES : (part + 1) * LANES
                 ]
     row = fields * levels * 2
-    meta_ref[row : row + 1, : topo_ref.shape[1]] = topo_ref[...].astype(F32)
-    share = meta_ref[pl.ds(pl.multiple_of(where_ref[1] * share_rows, share_rows), share_rows), :]
+    use = topo_ref.shape[1]
+    for topology in range(topo_ref.shape[0]):
+        meta_ref[row : row + 1, topology * use : (topology + 1) * use] = topo_ref[
+            topology : topology + 1, :
+        ].astype(F32)
+    place = lax.axis_index("site")
+    share = meta_ref[pl.ds(pl.multiple_of(place * share_rows, share_rows), share_rows), :]
     for owner in range(owners):
         share_ref[owner * share_rows : (owner + 1) * share_rows, :] = share
 
 
 def table_kernel(
-    place_ref, *refs, levels, owners, fields, shares, share_rows, entries,
+    *refs, levels, owners, fields, shares, share_rows, entries,
 ):
     share_refs, (child_ref, table_ref, topo_ref, meta_ref) = refs[:shares], refs[shares:]
     size = owners * share_rows
     for step in range(shares):
-        origin = lax.rem(place_ref[0] + (shares - step), shares)
+        origin = lax.rem(lax.axis_index("site") + (shares - step), shares)
         meta_ref[pl.ds(pl.multiple_of(origin * size, size), size), :] = share_refs[step][...]
 
     def rows_of(row):
@@ -208,48 +213,62 @@
     def code_of(level, dest):
         return table_ref[pl.ds(level * (fields - 1) * owners + dest, 1), :]
 
-    part_row = lax.broadcasted_iota(jnp.int32, (8, slots), 0)
-    part_rank = lax.broadcasted_iota(jnp.int32, (8, LANES), 0)
-    part_left = lax.broadcasted_iota(jnp.int32, (8, LANES), 1) < LANES // 2
+    part_row = lax.broadcasted_iota(jnp.int32, (16, slots), 0)
+    part_rank = lax.broadcasted_iota(jnp.int32, (16, 2 * LANES), 0)
+    part_lane = lax.broadcasted_iota(jnp.int32, (16, 2 * LANES), 1)
+    part_within = part_rank % 8
+    part_left = part_lane % LANES < LANES // 2
     sides = jnp.where(
-        (part_left & (part_rank < 3)) | (~part_left & (part_rank >= 3) & (part_rank < 6)), 1.0, 0.0
+        (part_rank // 8 == part_lane // LANES)
+        & (
+            (part_left & (part_within < 3))
+            | (~part_left & (part_within >= 3) & (part_within < 6))
+        ),
+        1.0, 0.0,
     ).astype(BF16)
 
-    def factor_of(level, dest):
-        base = level * (fields - 1) * owners + dest
-        weight = table_ref[pl.ds(base + owners, 1), :]
-        survival = table_ref[pl.ds(base + 2 * owners, 1), :]
-        stacked = jnp.zeros((8, slots), F32)
-        for side, scale in enumerate((weight * survival, weight * ((1.0 - survival) * 0.25))):
-            for part in range(3):
-                high = scale.astype(BF16).astype(F32)
-                stacked = jnp.where(part_row == 3 * side + part, high, stacked)
-                scale = scale - high
+    def factors_of(level, pair):
+        stacked = jnp.zeros((16, slots), F32)
+        for item in range(2):
+            base = level * (fields - 1) * owners + 2 * pair + item
+            weight = table_ref[pl.ds(base + owners, 1), :]
+            survival = table_ref[pl.ds(base + 2 * owners, 1), :]
+            for side, scale in enumerate(
+                (weight * survival, weight * ((1.0 - survival) * 0.25))
+            ):
+                for part in range(3):
+                    high = scale.astype(BF16).astype(F32)
+                    stacked = jnp.where(part_row == 8 * item + 3 * side + part, high, stacked)
+                    scale = scale - high
         return lax.dot_general(
             stacked.astype(BF16), sides, (((0,), (0,)), ((), ())), preferred_element_type=F32
         )
 
     def gather(level, last):
-        def body(dest, carry):
-            rows = jnp.concatenate(
-                [
-                    slot_ref[pl.ds((rank * owners + dest) * pitch, owners), :]
-                    for rank in range(4)
-                ],
-                axis=0,
-            )
-            factor = factor_of(level, dest)
-            weighted = both_parts(rows * factor)
-            if last:
-                weighted_ref[pl.ds(pl.multiple_of(dest * slots, slots), slots), :] = weighted
-            hit = (pair_row == code_of(level, dest)).astype(F32).astype(BF16)
-            product = jnp.dot(hit, weighted, preferred_element_type=F32)
-            sums_ref[pl.ds(pl.multiple_of(dest * half, half), half), :] = both_parts(
-                product[:, :LANES] + product[:, LANES:]
-            )
+        def body(pair, carry):
+            factors = factors_of(level, pair)
+            for item in range(2):
+                dest = 2 * pair + item
+                rows = jnp.concatenate(
+                    [
+                        slot_ref[pl.ds((rank * owners + dest) * pitch, owners), :]
+                        for rank in range(4)
+                    ],
+                    axis=0,
+                )
+                weighted = both_parts(rows * factors[:, item * LANES : (item + 1) * LANES])
+                if last:
+                    weighted_ref[
+                        pl.ds(pl.multiple_of(dest * slots, slots), slots), :
+                    ] = weighted
+                hit = (pair_row == code_of(level, dest)).astype(F32).astype(BF16)
+                product = jnp.dot(hit, weighted, preferred_element_type=F32)
+                sums_ref[pl.ds(pl.multiple_of(dest * half, half), half), :] = both_parts(
+                    product[:, :LANES] + product[:, LANES:]
+                )
             return carry
 
-        lax.fori_loop(0, owners, body, 0, unroll=GATHER_UNROLL)
+        lax.fori_loop(0, owners // 2, body, 0, unroll=GATHER_UNROLL // 2)
 
     def pair_sums(group):
         rows = GROUP * half
@@ -400,25 +419,21 @@
 
     halves = topo_dev // 2
     vmem = pl.BlockSpec(memory_space=pltpu.VMEM)
-    smem = pl.BlockSpec(memory_space=pltpu.SMEM)
     shares = lax.axis_size("site")
     share_rows = -(-(fields * levels * 2 + 1) // (8 * shares)) * 8
-    place = lax.axis_index("site")
     share, slot = pl.pallas_call(
         functools.partial(
             slot_kernel, levels=levels, owners=owners, node_dev=node_dev, fields=fields,
             share_rows=share_rows,
         ),
-        in_specs=[smem] + [vmem] * 4,
+        in_specs=[vmem] * 4,
         out_shape=[
             jax.ShapeDtypeStruct((owners * share_rows, LANES), F32),
             jax.ShapeDtypeStruct((levels, edge_dev), jnp.int32),
         ],
         scratch_shapes=[pltpu.VMEM((share_rows * shares, LANES), F32)],
     )(
-        jnp.stack([device, place]).astype(jnp.int32),
-        dag_edges.transpose(2, 0, 1).reshape(3 * levels, edge_dev), weights, lengths,
-        topo_nodes.reshape(1, -1),
+        dag_edges.transpose(2, 0, 1), weights, lengths, topo_nodes
     )
     share = lax.all_to_all(
         share.reshape(owners, share_rows, LANES), "node",
@@ -434,7 +449,7 @@
             table_kernel, levels=levels, owners=owners, fields=fields, shares=shares,
             share_rows=share_rows, entries=entries,
         ),
-        in_specs=[smem] + [vmem] * shares,
+        in_specs=[vmem] * shares,
         out_shape=[
             jax.ShapeDtypeStruct((owners * share_rows, LANES), F32),
             jax.ShapeDtypeStruct((levels * (fields - 1) * owners, slots), F32),
@@ -442,7 +457,7 @@
         ],
         scratch_shapes=[pltpu.VMEM((owners * share_rows * shares, LANES), F32)],
         compiler_params=pltpu.CompilerParams(vmem_limit_bytes=8 * 1024 * 1024),
-    )(place.astype(jnp.int32).reshape(1), *met)
+    )(*met)
 
     chunk = states // 2 * site_own
     peers = LANES // site_own

time: 136 us -> 135 us (level)
    reshape x2 -> x0, local copies, waits for them, and re-layouts: 1.91 us -> none  [the longest x1 1.3 us: on_device(): topo_nodes.reshape(1, -1)]
where the time goes in v8:
time: 135 us; the launch traced here: 134 us
  Pallas kernels  49.3 us (37%)
  waiting for transfers between devices  37.8 us (28%)
  starting transfers between devices  29.2 us (22%)
  blocking collectives  10.8 us (8%)
  local copies, waits for them, and re-layouts  4.23 us (3%)
  other arithmetic  1.89 us (1%)
    pallas_call x1, Pallas kernels, on_device(): pl.pallas_call(functools.partial(dag_kernel, levels=levels, owners=owners...  40.9 us
    all_to_all x1, starting transfers between devices, on_device(): lax.all_to_all(share.reshape(owners, share_rows, LANES), 'node', split_ax...  12 us
    all_to_all x1, waiting for transfers between devices, on_device(): lax.all_to_all(packed.reshape(owners, chunk, LANES), 'node', split_axis=0...  11.6 us
    psum x1, blocking collectives, on_device(): lax.psum(jnp.sum(shares[:, :slots // LANES + 1], axis=0), 'site')  10.8 us
    all_to_all x1, waiting for transfers between devices, on_device(): lax.all_to_all(partial.reshape(owners, out_rows, LANES), 'node', split_ax...  9.86 us
    ppermute x3, waiting for transfers between devices, on_device(): lax.ppermute(share, 'site', [(k, (k + step) % shares) for k in range(shar...  9.75 us
    all_to_all x1, waiting for transfers between devices, on_device(): lax.all_to_all(share.reshape(owners, share_rows, LANES), 'node', split_ax...  6.57 us
    ppermute x3, starting transfers between devices, on_device(): lax.ppermute(share, 'site', [(k, (k + step) % shares) for k in range(shar...  5.9 us
  transfers between devices with their start and end apart: 6, of which 5 were waited for; matrix products, arithmetic and copies ran while one was open for 2% of the time, Pallas kernels for 5%

profile of v8, /device:TPU:2, one launch (start us, length us, event | category | flops | bytes accessed | tf_op | source)
XLA Modules:
  0.0 133.9 jit_solution(9179930913166603292)
XLA Ops:
  0.6 1.3 copy.14
  1.9 2.1 %shard_map.78 = (f32[512,128]{1,0:T(8,128)}, s32[3,192]{1,0:T(4,128)}) custom-call(s32[3,3,192]{2,1,0:T(4,128)} %bitcast.24, f32[3,192]{1,0:T(4,128)} %weight_ref.1, f32[3,192]{1,0:T(4,128)} %length_ref.1, s32[4,8]{1,0:T(4,128)} %topo_ref.1), custom_call_target="tpu_custom_call" | custom-call | tf_op jit(solution)/shard_map/pallas_call | solution.py:424
  4.0 12.0 %all-to-all-start.1 = ((f32[64,8,128]{2,1,0:T(8,128)}), f32[64,8,128]{2,1,0:T(8,128)S(1)}, u32[]{:S(2)}, u32[]{:S(2)}) async-start(f32[64,8,128]{2,1,0:T(8,128)} %bitcast.23), calls=%async_computation.1 | async-start | bytes 524288 | tf_op jit(solution)/shard_map/all_to_all | solution.py:438
  16.1 5.7 %shard_map.77 = f32[2048,128]{1,0:T(8,128)} custom-call(f32[64,4,1024]{2,1,0:T(4,128)} %leaf_ref.1), custom_call_target="tpu_custom_call" | custom-call | tf_op jit(solution)/shard_map/pallas_call | solution.py:464
  21.7 6.6 %all-to-all-done.1 = f32[64,8,128]{2,1,0:T(8,128)S(1)} async-done(((f32[64,8,128]{2,1,0:T(8,128)}), f32[64,8,128]{2,1,0:T(8,128)S(1)}, u32[]{:S(2)}, u32[]{:S(2)}) %all-to-all-start.1) | async-done | bytes 262176 | tf_op jit(solution)/shard_map/all_to_all | solution.py:438
  28.3 5.7 %all-to-all-start = ((f32[64,32,128]{2,1,0:T(8,128)}), f32[64,32,128]{2,1,0:T(8,128)S(1)}, u32[]{:S(2)}, u32[]{:S(2)}) async-start(f32[64,32,128]{2,1,0:T(8,128)} %bitcast.22), calls=%async_computation | async-start | bytes 2097152 | tf_op jit(solution)/shard_map/all_to_all | solution.py:471
  33.9 1.7 %collective-permute-start = (f32[512,128]{1,0:T(8,128)S(1)}, f32[512,128]{1,0:T(8,128)S(1)}, u32[]{:S(2)}, u32[]{:S(2)}) collective-permute-start(f32[512,128]{1,0:T(8,128)S(1)} %bitcast.17), channel_id=1, source_target_pairs={{0,1},{1,2},{2,3},{3,0},{4,5},{5,6},{6,7},{7,4},{8,9},{9,10},{10,1... | collective-permute-start | bytes 786440 | tf_op jit(solution)/shard_map/ppermute | solution.py:443
  35.6 2.9 %collective-permute-start.1 = (f32[512,128]{1,0:T(8,128)S(1)}, f32[512,128]{1,0:T(8,128)S(1)}, u32[]{:S(2)}, u32[]{:S(2)}) collective-permute-start(f32[512,128]{1,0:T(8,128)S(1)} %bitcast.18), channel_id=1, source_target_pairs={{0,2},{1,3},{2,0},{3,1},{4,6},{5,7},{6,4},{7,5},{8,10},{9,11},{10,... | collective-permute-start | bytes 786440 | tf_op jit(solution)/shard_map/ppermute | solution.py:443
  38.5 1.4 %collective-permute-start.2 = (f32[512,128]{1,0:T(8,128)S(1)}, f32[512,128]{1,0:T(8,128)S(1)}, u32[]{:S(2)}, u32[]{:S(2)}) collective-permute-start(f32[512,128]{1,0:T(8,128)S(1)} %bitcast.19), channel_id=1, source_target_pairs={{0,3},{1,0},{2,1},{3,2},{4,7},{5,4},{6,5},{7,6},{8,11},{9,8},{10,9... | collective-permute-start | bytes 786440 | tf_op jit(solution)/shard_map/ppermute | solution.py:443
  39.8 0.8 convert_multiply_fusion
  40.6 0.1 broadcast_in_dim_tile.3.scaled_ref
  40.7 3.0 %collective-permute-done.refs_1_ = f32[512,128]{1,0:T(8,128)S(1)} collective-permute-done((f32[512,128]{1,0:T(8,128)S(1)}, f32[512,128]{1,0:T(8,128)S(1)}, u32[]{:S(2)}, u32[]{:S(2)}) %collective-permute-start) | collective-permute-done | bytes 262176 | tf_op jit(solution)/shard_map/ppermute | solution.py:443
  43.6 6.8 %collective-permute-done.1.refs_2_ = f32[512,128]{1,0:T(8,128)S(1)} collective-permute-done((f32[512,128]{1,0:T(8,128)S(1)}, f32[512,128]{1,0:T(8,128)S(1)}, u32[]{:S(2)}, u32[]{:S(2)}) %collective-permute-start.1) | collective-permute-done | bytes 262176 | tf_op jit(solution)/shard_map/ppermute | solution.py:443
  50.4 0.0 collective-permute-done.2.refs_3_
  50.4 0.7 shard_map.79
  51.1 11.6 %all-to-all-done = f32[64,32,128]{2,1,0:T(8,128)S(1)} async-done(((f32[64,32,128]{2,1,0:T(8,128)}), f32[64,32,128]{2,1,0:T(8,128)S(1)}, u32[]{:S(2)}, u32[]{:S(2)}) %all-to-all-start) | async-done | bytes 1048608 | tf_op jit(solution)/shard_map/all_to_all | solution.py:471
  62.7 40.9 %shard_map.80 = f32[512,128]{1,0:T(8,128)} custom-call(f32[2048,128]{1,0:T(8,128)S(1)} %bitcast.16, f32[512,128]{1,0:T(8,128)S(1)} %get-tuple-element.8.child_ref, f32[576,256]{1,0:T(8,128)S(1)} %get-tuple-element.9.table_ref, s32[16,128]{1,0:T(8,128)S(1)} %get-tuple-element.10.topo_ref, f32[1,128]{1,0:T(1,128)S(1)} %broadcast_in_dim_tile.3.scaled_ref), custom_call_target="tpu_custom_call" | custom-call | tf_op jit(solution)/shard_map/pallas_call | solution.py:478
  103.6 5.7 %all-to-all-start.2 = ((f32[64,8,128]{2,1,0:T(8,128)}), f32[64,8,128]{2,1,0:T(8,128)S(1)}, u32[]{:S(2)}, u32[]{:S(2)}) async-start(f32[64,8,128]{2,1,0:T(8,128)} %bitcast.5), calls=%async_computation.2 | async-start | bytes 524288 | tf_op jit(solution)/shard_map/all_to_all | solution.py:496
  109.3 0.7 slice.27
  110.0 0.7 slice.28
  110.7 0.7 slice.29
  111.4 0.3 convert_reduce_fusion
  111.7 9.9 %all-to-all-done.2 = f32[64,8,128]{2,1,0:T(8,128)S(1)} async-done(((f32[64,8,128]{2,1,0:T(8,128)}), f32[64,8,128]{2,1,0:T(8,128)S(1)}, u32[]{:S(2)}, u32[]{:S(2)}) %all-to-all-start.2) | async-done | bytes 262176 | tf_op jit(solution)/shard_map/all_to_all | solution.py:496
  121.5 0.1 slice_reduce_fusion
  121.6 10.8 %psum.7 = f32[3,128]{1,0:T(4,128)S(1)} all-reduce(f32[3,128]{1,0:T(4,128)S(1)} %slice_reduce_fusion), channel_id=1, replica_groups=mesh['node'=64,'site'=4] {'site'}, use_global_device_ids=true, to_apply=%region_1.0 | all-reduce | flops 384 | bytes 3072 | tf_op jit(solution)/shard_map/psum | solution.py:499
  132.3 0.1 slice.25
  132.4 0.1 copy.12
  132.5 0.6 reshape.38
  133.1 0.2 select_reduce_fusion
  133.3 0.6 divide_multiply_fusion
  (3 shorter events, 0.0 us)
Async XLA Ops:
  4.0 24.2 %all-to-all-start.1 = ((f32[64,8,128]{2,1,0:T(8,128)}), f32[64,8,128]{2,1,0:T(8,128)S(1)}, u32[]{:S(2)}, u32[]{:S(2)}) async-start(f32[64,8,128]{2,1,0:T(8,128)} %bitcast.23), calls=%async_computation.1 | async-start | bytes 524288 | tf_op jit(solution)/shard_map/all_to_all | solution.py:438
  28.3 34.5 %all-to-all-start = ((f32[64,32,128]{2,1,0:T(8,128)}), f32[64,32,128]{2,1,0:T(8,128)S(1)}, u32[]{:S(2)}, u32[]{:S(2)}) async-start(f32[64,32,128]{2,1,0:T(8,128)} %bitcast.22), calls=%async_computation | async-start | bytes 2097152 | tf_op jit(solution)/shard_map/all_to_all | solution.py:471
  33.9 9.7 %collective-permute-start = (f32[512,128]{1,0:T(8,128)S(1)}, f32[512,128]{1,0:T(8,128)S(1)}, u32[]{:S(2)}, u32[]{:S(2)}) collective-permute-start(f32[512,128]{1,0:T(8,128)S(1)} %bitcast.17), channel_id=1, source_target_pairs={{0,1},{1,2},{2,3},{3,0},{4,5},{5,6},{6,7},{7,4},{8,9},{9,10},{10,1... | collective-permute-start | bytes 786440 | tf_op jit(solution)/shard_map/ppermute | solution.py:443
  35.6 14.8 %collective-permute-start.1 = (f32[512,128]{1,0:T(8,128)S(1)}, f32[512,128]{1,0:T(8,128)S(1)}, u32[]{:S(2)}, u32[]{:S(2)}) collective-permute-start(f32[512,128]{1,0:T(8,128)S(1)} %bitcast.18), channel_id=1, source_target_pairs={{0,2},{1,3},{2,0},{3,1},{4,6},{5,7},{6,4},{7,5},{8,10},{9,11},{10,... | collective-permute-start | bytes 786440 | tf_op jit(solution)/shard_map/ppermute | solution.py:443
  38.5 12.0 %collective-permute-start.2 = (f32[512,128]{1,0:T(8,128)S(1)}, f32[512,128]{1,0:T(8,128)S(1)}, u32[]{:S(2)}, u32[]{:S(2)}) collective-permute-start(f32[512,128]{1,0:T(8,128)S(1)} %bitcast.19), channel_id=1, source_target_pairs={{0,3},{1,0},{2,1},{3,2},{4,7},{5,4},{6,5},{7,6},{8,11},{9,8},{10,9... | collective-permute-start | bytes 786440 | tf_op jit(solution)/shard_map/ppermute | solution.py:443
  103.6 17.9 %all-to-all-start.2 = ((f32[64,8,128]{2,1,0:T(8,128)}), f32[64,8,128]{2,1,0:T(8,128)S(1)}, u32[]{:S(2)}, u32[]{:S(2)}) async-start(f32[64,8,128]{2,1,0:T(8,128)} %bitcast.5), calls=%async_computation.2 | async-start | bytes 524288 | tf_op jit(solution)/shard_map/all_to_all | solution.py:496

commit v9 on v7

--- a/solution.py
+++ b/solution.py
@@ -31,8 +31,8 @@
 
 
 def slot_kernel(
-    where_ref, dag_ref, weight_ref, length_ref, topo_ref, share_ref, slot_ref, meta_ref,
-    *, levels, owners, node_dev, fields, share_rows,
+    dag_ref, weight_ref, length_ref, topo_ref, meta_ref, slot_ref,
+    *, levels, owners, node_dev, fields,
 ):
     edges = weight_ref.shape[1]
     slots = 4 * owners
@@ -45,9 +45,9 @@
     meta_ref[...] = jnp.zeros(meta_ref.shape, F32)
     field_row = rows(8)
     for level in range(levels):
-        child = dag_ref[level : level + 1, :] - where_ref[0] * node_dev
-        parent = dag_ref[levels + level : levels + level + 1, :]
-        rotation = dag_ref[2 * levels + level : 2 * levels + level + 1, :]
+        child = dag_ref[0, level : level + 1, :] - lax.axis_index("node") * node_dev
+        parent = dag_ref[1, level : level + 1, :]
+        rotation = dag_ref[2, level : level + 1, :]
         owner_of = parent // node_dev
         code = rotation * node_dev + parent - owner_of * node_dev
         goes = (rows(owners) == owner_of).astype(F32)
@@ -80,27 +80,34 @@
                     field : field + 1, part * LANES : (part + 1) * LANES
                 ]
     row = fields * levels * 2
-    meta_ref[row : row + 1, : topo_ref.shape[1]] = topo_ref[...].astype(F32)
-    share = meta_ref[pl.ds(pl.multiple_of(where_ref[1] * share_rows, share_rows), share_rows), :]
-    for owner in range(owners):
-        share_ref[owner * share_rows : (owner + 1) * share_rows, :] = share
+    use = topo_ref.shape[1]
+    for topology in range(topo_ref.shape[0]):
+        meta_ref[row : row + 1, topology * use : (topology + 1) * use] = topo_ref[
+            topology : topology + 1, :
+        ].astype(F32)
 
 
 def table_kernel(
-    place_ref, *refs, levels, owners, fields, shares, share_rows, entries,
+    met_ref, child_ref, table_ref, topo_ref, meta_ref,
+    *, levels, owners, fields, meta_rows, entries, strides,
 ):
-    share_refs, (child_ref, table_ref, topo_ref, meta_ref) = refs[:shares], refs[shares:]
-    size = owners * share_rows
-    for step in range(shares):
-        origin = lax.rem(place_ref[0] + (shares - step), shares)
-        meta_ref[pl.ds(pl.multiple_of(origin * size, size), size), :] = share_refs[step][...]
+    device = lax.axis_index("node")
+    pitch = meta_ref.shape[0] // owners
+    child_rows = child_ref.shape[0] // owners
+    for place in range(owners):
+        origin = device
+        for bit, stride in enumerate(strides):
+            if place >> bit & 1:
+                origin = lax.bitwise_xor(origin, jnp.int32(stride))
+        block = met_ref[place * meta_rows : (place + 1) * meta_rows, :]
+        meta_ref[pl.ds(pl.multiple_of(origin * pitch, 8), meta_rows), :] = block
+        child_ref[pl.ds(pl.multiple_of(origin * child_rows, 8), child_rows), :] = block[
+            :child_rows
+        ]
 
     def rows_of(row):
-        return meta_ref[
-            pl.ds(row // share_rows * size + row % share_rows, owners, stride=share_rows), :
-        ]
-
-    child_ref[...] = meta_ref[:size, :]
+        return meta_ref[pl.ds(row, owners, stride=pitch), :]
+
     for level in range(levels):
         for field in range(1, fields):
             for part in range(2):
@@ -400,49 +407,25 @@
 
     halves = topo_dev // 2
     vmem = pl.BlockSpec(memory_space=pltpu.VMEM)
-    smem = pl.BlockSpec(memory_space=pltpu.SMEM)
-    shares = lax.axis_size("site")
-    share_rows = -(-(fields * levels * 2 + 1) // (8 * shares)) * 8
-    place = lax.axis_index("site")
-    share, slot = pl.pallas_call(
+    meta_rows = -(-(fields * levels * 2 + 1) // 8) * 8
+    met, slot = pl.pallas_call(
         functools.partial(
-            slot_kernel, levels=levels, owners=owners, node_dev=node_dev, fields=fields,
-            share_rows=share_rows,
+            slot_kernel, levels=levels, owners=owners, node_dev=node_dev, fields=fields
         ),
-        in_specs=[smem] + [vmem] * 4,
+        in_specs=[vmem] * 4,
         out_shape=[
-            jax.ShapeDtypeStruct((owners * share_rows, LANES), F32),
+            jax.ShapeDtypeStruct((meta_rows, LANES), F32),
             jax.ShapeDtypeStruct((levels, edge_dev), jnp.int32),
         ],
-        scratch_shapes=[pltpu.VMEM((share_rows * shares, LANES), F32)],
-    )(
-        jnp.stack([device, place]).astype(jnp.int32),
-        dag_edges.transpose(2, 0, 1).reshape(3 * levels, edge_dev), weights, lengths,
-        topo_nodes.reshape(1, -1),
-    )
-    share = lax.all_to_all(
-        share.reshape(owners, share_rows, LANES), "node",
-        split_axis=0, concat_axis=0, tiled=True,
-    ).reshape(owners * share_rows, LANES)
-    met = [share] + [
-        lax.ppermute(share, "site", [(k, (k + step) % shares) for k in range(shares)])
-        for step in range(1, shares)
-    ]
-    entries = use * halves
-    child_table, edge_table, topologies = pl.pallas_call(
-        functools.partial(
-            table_kernel, levels=levels, owners=owners, fields=fields, shares=shares,
-            share_rows=share_rows, entries=entries,
-        ),
-        in_specs=[smem] + [vmem] * shares,
-        out_shape=[
-            jax.ShapeDtypeStruct((owners * share_rows, LANES), F32),
-            jax.ShapeDtypeStruct((levels * (fields - 1) * owners, slots), F32),
-            jax.ShapeDtypeStruct((entries, LANES), jnp.int32),
-        ],
-        scratch_shapes=[pltpu.VMEM((owners * share_rows * shares, LANES), F32)],
-        compiler_params=pltpu.CompilerParams(vmem_limit_bytes=8 * 1024 * 1024),
-    )(place.astype(jnp.int32).reshape(1), *met)
+    )(dag_edges.transpose(2, 0, 1), weights, lengths, topo_nodes)
+
+    def exchange(tables, stride):
+        other = lax.ppermute(tables, "node", [(k, k ^ stride) for k in range(owners)])
+        return jnp.concatenate([tables, other], axis=0)
+
+    strides = [1 << bit for bit in reversed(range(owners.bit_length() - 1))]
+    for stride in strides[: len(strides) // 2]:
+        met = exchange(met, stride)
 
     chunk = states // 2 * site_own
     peers = LANES // site_own
@@ -453,9 +436,27 @@
         out_specs=pl.BlockSpec((peers * chunk, LANES), lambda step: (step, 0)),
         out_shape=jax.ShapeDtypeStruct((owners * chunk, LANES), F32),
     )(leaf_partials)
+    packed, met = lax.optimization_barrier((packed, met))
     received = lax.all_to_all(
         packed.reshape(owners, chunk, LANES), "node", split_axis=0, concat_axis=0, tiled=True
     ).reshape(owners * chunk, LANES)
+    for stride in strides[len(strides) // 2 :]:
+        met = exchange(met, stride)
+    entries = use * halves
+    child_table, edge_table, topologies = pl.pallas_call(
+        functools.partial(
+            table_kernel, levels=levels, owners=owners, fields=fields, meta_rows=meta_rows,
+            entries=entries, strides=strides,
+        ),
+        in_specs=[vmem],
+        out_shape=[
+            jax.ShapeDtypeStruct((owners * 8, LANES), F32),
+            jax.ShapeDtypeStruct((levels * (fields - 1) * owners, slots), F32),
+            jax.ShapeDtypeStruct((entries, LANES), jnp.int32),
+        ],
+        scratch_shapes=[pltpu.VMEM((owners * (meta_rows + 8), LANES), F32)],
+        compiler_params=pltpu.CompilerParams(vmem_limit_bytes=8 * 1024 * 1024),
+    )(met)
     own_counts = lax.dynamic_slice_in_dim(counts, device * site_own, site_own)
     scaled = jnp.tile(own_counts.astype(F32) / sites_all, LANES // site_own)[None, :]
 

time: 136 us -> 139 us (1.022)
  starting transfers between devices: 29.2 us -> 33.4 us
    ppermute x3 -> x6, waiting for transfers between devices: 9.75 us -> 22.1 us  [exchange(): lax.ppermute(tables, 'node', [(k, k ^ stride) for k in range(owners)])]
    all_to_all x1 -> x0, starting transfers between devices: 12 us -> none  [on_device(): lax.all_to_all(share.reshape(owners, share_rows, LANES), 'node', split_ax...]
    ppermute x3 -> x6, starting transfers between devices: 5.9 us -> 14.4 us  [exchange(): lax.ppermute(tables, 'node', [(k, k ^ stride) for k in range(owners)])]
    all_to_all x1 -> x0, waiting for transfers between devices: 6.57 us -> none  [on_device(): lax.all_to_all(share.reshape(owners, share_rows, LANES), 'node', split_ax...]
    all_to_all x1, waiting for transfers between devices: 11.6 us -> 5.67 us  [on_device(): lax.all_to_all(packed.reshape(owners, chunk, LANES), 'node', split_axis=0...]
    all_to_all x1, starting transfers between devices: 5.65 us -> 10.8 us  [on_device(): lax.all_to_all(packed.reshape(owners, chunk, LANES), 'node', split_axis=0...]
    all_to_all x1, starting transfers between devices: 5.65 us -> 8.3 us  [on_device(): lax.all_to_all(partial.reshape(owners, out_rows, LANES), 'node', split_ax...]
    reshape x2 -> x0, local copies, waits for them, and re-layouts: 1.91 us -> none  [the longest x1 1.3 us: on_device(): topo_nodes.reshape(1, -1)]
  transfers between devices with their start and end apart: 6 -> 8, of which waited for: 5 -> 7; matrix products, arithmetic and copies ran while one was open for 2% -> 2% of each run, Pallas kernels for 5% -> 5%
where the time goes in v9:
time: 139 us; the launch traced here: 138 us
  Pallas kernels  48.2 us (35%)
  waiting for transfers between devices  37.6 us (27%)
  starting transfers between devices  33.4 us (24%)
  blocking collectives  10.8 us (8%)
  local copies, waits for them, and re-layouts  4.24 us (3%)
  other arithmetic  3.47 us (2%)
    pallas_call x1, Pallas kernels, on_device(): pl.pallas_call(functools.partial(dag_kernel, levels=levels, owners=owners...  39.9 us
    ppermute x6, waiting for transfers between devices, exchange(): lax.ppermute(tables, 'node', [(k, k ^ stride) for k in range(owners)])  22.1 us
    ppermute x6, starting transfers between devices, exchange(): lax.ppermute(tables, 'node', [(k, k ^ stride) for k in range(owners)])  14.4 us
    psum x1, blocking collectives, on_device(): lax.psum(jnp.sum(shares[:, :slots // LANES + 1], axis=0), 'site')  10.8 us
    all_to_all x1, starting transfers between devices, on_device(): lax.all_to_all(packed.reshape(owners, chunk, LANES), 'node', split_axis=0...  10.8 us
    all_to_all x1, waiting for transfers between devices, on_device(): lax.all_to_all(partial.reshape(owners, out_rows, LANES), 'node', split_ax...  9.86 us
    all_to_all x1, starting transfers between devices, on_device(): lax.all_to_all(partial.reshape(owners, out_rows, LANES), 'node', split_ax...  8.3 us
    all_to_all x1, waiting for transfers between devices, on_device(): lax.all_to_all(packed.reshape(owners, chunk, LANES), 'node', split_axis=0...  5.67 us
  transfers between devices with their start and end apart: 8, of which 7 were waited for; matrix products, arithmetic and copies ran while one was open for 2% of the time, Pallas kernels for 5%

profile of v9, /device:TPU:2, one launch (start us, length us, event | category | flops | bytes accessed | tf_op | source)
XLA Modules:
  0.0 138.4 jit_solution(18166237480436686177)
XLA Ops:
  0.6 1.3 copy.14
  1.9 2.0 %shard_map.78 = (f32[32,128]{1,0:T(8,128)}, s32[3,192]{1,0:T(4,128)}) custom-call(s32[3,3,192]{2,1,0:T(4,128)} %bitcast.17, f32[3,192]{1,0:T(4,128)} %weight_ref.1, f32[3,192]{1,0:T(4,128)} %length_ref.1, s32[4,8]{1,0:T(4,128)} %topo_ref.1), custom_call_target="tpu_custom_call" | custom-call | tf_op jit(solution)/shard_map/pallas_call | solution.py:411
  3.9 7.2 %collective-permute-start = (f32[32,128]{1,0:T(8,128)}, f32[32,128]{1,0:T(8,128)S(1)}, u32[]{:S(2)}, u32[]{:S(2)}) collective-permute-start(f32[32,128]{1,0:T(8,128)} %get-tuple-element.9), channel_id=1, source_target_pairs={{0,128},{4,132},{8,136},{12,140},{16,144},{20,148},{24,152},{28,15... | collective-permute-start | bytes 49160 | tf_op jit(solution)/shard_map/ppermute | solution.py:423
  11.1 1.9 %collective-permute-done = f32[32,128]{1,0:T(8,128)S(1)} collective-permute-done((f32[32,128]{1,0:T(8,128)}, f32[32,128]{1,0:T(8,128)S(1)}, u32[]{:S(2)}, u32[]{:S(2)}) %collective-permute-start) | collective-permute-done | bytes 16416 | tf_op jit(solution)/shard_map/ppermute | solution.py:423
  13.0 0.7 pad_maximum_fusion.5
  13.7 2.0 %collective-permute-start.1 = (f32[64,128]{1,0:T(8,128)S(1)}, f32[64,128]{1,0:T(8,128)S(1)}, u32[]{:S(2)}, u32[]{:S(2)}) collective-permute-start(f32[64,128]{1,0:T(8,128)S(1)} %pad_maximum_fusion.5), channel_id=1, source_target_pairs={{0,64},{4,68},{8,72},{12,76},{16,80},{20,84},{24,88},{28,92},{32,9... | collective-permute-start | bytes 98312 | tf_op jit(solution)/shard_map/ppermute | solution.py:423
  15.7 2.8 %collective-permute-done.1 = f32[64,128]{1,0:T(8,128)S(1)} collective-permute-done((f32[64,128]{1,0:T(8,128)S(1)}, f32[64,128]{1,0:T(8,128)S(1)}, u32[]{:S(2)}, u32[]{:S(2)}) %collective-permute-start.1) | collective-permute-done | bytes 32800 | tf_op jit(solution)/shard_map/ppermute | solution.py:423
  18.5 0.7 pad_maximum_fusion.4
  19.3 1.0 collective-permute-start.2
  20.3 5.6 %shard_map.77 = f32[2048,128]{1,0:T(8,128)} custom-call(f32[64,4,1024]{2,1,0:T(4,128)} %leaf_ref.1), custom_call_target="tpu_custom_call" | custom-call | tf_op jit(solution)/shard_map/pallas_call | solution.py:432
  25.9 10.8 %all-to-all-start = ((f32[64,32,128]{2,1,0:T(8,128)}), f32[64,32,128]{2,1,0:T(8,128)S(1)}, u32[]{:S(2)}, u32[]{:S(2)}) async-start(f32[64,32,128]{2,1,0:T(8,128)} %bitcast.16), calls=%async_computation | async-start | bytes 2097152 | tf_op jit(solution)/shard_map/all_to_all | solution.py:440
  36.7 2.2 %collective-permute-start.3 = (f32[256,128]{1,0:T(8,128)S(1)}, f32[256,128]{1,0:T(8,128)S(1)}, u32[]{:S(2)}, u32[]{:S(2)}) collective-permute-start(f32[256,128]{1,0:T(8,128)S(1)} %pad_maximum_fusion.3), channel_id=1, source_target_pairs={{0,16},{4,20},{8,24},{12,28},{16,0},{20,4},{24,8},{28,12},{32,48},... | collective-permute-start | bytes 393224 | tf_op jit(solution)/shard_map/ppermute | solution.py:423
  38.9 7.2 %collective-permute-done.3 = f32[256,128]{1,0:T(8,128)S(1)} collective-permute-done((f32[256,128]{1,0:T(8,128)S(1)}, f32[256,128]{1,0:T(8,128)S(1)}, u32[]{:S(2)}, u32[]{:S(2)}) %collective-permute-start.3) | collective-permute-done | bytes 131104 | tf_op jit(solution)/shard_map/ppermute | solution.py:423
  46.1 1.7 %collective-permute-start.4 = (f32[512,128]{1,0:T(8,128)S(1)}, f32[512,128]{1,0:T(8,128)S(1)}, u32[]{:S(2)}, u32[]{:S(2)}) collective-permute-start(f32[512,128]{1,0:T(8,128)S(1)} %pad_maximum_fusion.2), channel_id=1, source_target_pairs={{0,8},{4,12},{8,0},{12,4},{16,24},{20,28},{24,16},{28,20},{32,40},... | collective-permute-start | bytes 786440 | tf_op jit(solution)/shard_map/ppermute | solution.py:423
  47.8 9.1 %collective-permute-done.4 = f32[512,128]{1,0:T(8,128)S(1)} collective-permute-done((f32[512,128]{1,0:T(8,128)S(1)}, f32[512,128]{1,0:T(8,128)S(1)}, u32[]{:S(2)}, u32[]{:S(2)}) %collective-permute-start.4) | collective-permute-done | bytes 262176 | tf_op jit(solution)/shard_map/ppermute | solution.py:423
  56.9 0.3 collective-permute-start.5
  57.2 0.8 convert_multiply_fusion
  58.1 1.0 collective-permute-done.5
  59.2 0.7 shard_map.79
  59.8 5.7 %all-to-all-done = f32[64,32,128]{2,1,0:T(8,128)S(1)} async-done(((f32[64,32,128]{2,1,0:T(8,128)}), f32[64,32,128]{2,1,0:T(8,128)S(1)}, u32[]{:S(2)}, u32[]{:S(2)}) %all-to-all-start) | async-done | bytes 1048608 | tf_op jit(solution)/shard_map/all_to_all | solution.py:440
  65.5 39.9 %shard_map.80 = f32[512,128]{1,0:T(8,128)} custom-call(f32[2048,128]{1,0:T(8,128)S(1)} %bitcast.14, f32[512,128]{1,0:T(8,128)S(1)} %get-tuple-element.12.child_ref, f32[576,256]{1,0:T(8,128)S(1)} %get-tuple-element.13.table_ref, s32[16,128]{1,0:T(8,128)S(1)} %get-tuple-element.14.topo_ref, f32[1,128]{1,0:T(1,128)S(1)} %broadcast_in_dim_tile.3.scaled_ref), custom_call_target="tpu_custom_call" | custom-call | tf_op jit(solution)/shard_map/pallas_call | solution.py:464
  105.4 8.3 %all-to-all-start.1 = ((f32[64,8,128]{2,1,0:T(8,128)}), f32[64,8,128]{2,1,0:T(8,128)S(1)}, u32[]{:S(2)}, u32[]{:S(2)}) async-start(f32[64,8,128]{2,1,0:T(8,128)} %bitcast.3), calls=%async_computation.1 | async-start | bytes 524288 | tf_op jit(solution)/shard_map/all_to_all | solution.py:482
  113.7 0.7 slice.27
  114.4 0.7 slice.28
  115.1 0.7 slice.29
  115.8 0.3 convert_reduce_fusion
  116.1 9.9 %all-to-all-done.1 = f32[64,8,128]{2,1,0:T(8,128)S(1)} async-done(((f32[64,8,128]{2,1,0:T(8,128)}), f32[64,8,128]{2,1,0:T(8,128)S(1)}, u32[]{:S(2)}, u32[]{:S(2)}) %all-to-all-start.1) | async-done | bytes 262176 | tf_op jit(solution)/shard_map/all_to_all | solution.py:482
  126.0 10.8 %psum.7 = f32[3,128]{1,0:T(4,128)S(1)} all-reduce(f32[3,128]{1,0:T(4,128)S(1)} %slice_reduce_fusion), channel_id=1, replica_groups=mesh['node'=64,'site'=4] {'site'}, use_global_device_ids=true, to_apply=%region_1.0 | all-reduce | flops 384 | bytes 3072 | tf_op jit(solution)/shard_map/psum | solution.py:485
  136.9 0.1 copy.12
  137.0 0.6 reshape.30
  137.6 0.2 select_reduce_fusion
  137.8 0.6 divide_multiply_fusion
  (13 shorter events, 0.4 us)
Async XLA Ops:
  3.9 9.1 %collective-permute-start = (f32[32,128]{1,0:T(8,128)}, f32[32,128]{1,0:T(8,128)S(1)}, u32[]{:S(2)}, u32[]{:S(2)}) collective-permute-start(f32[32,128]{1,0:T(8,128)} %get-tuple-element.9), channel_id=1, source_target_pairs={{0,128},{4,132},{8,136},{12,140},{16,144},{20,148},{24,152},{28,15... | collective-permute-start | bytes 49160 | tf_op jit(solution)/shard_map/ppermute | solution.py:423
  13.7 4.8 %collective-permute-start.1 = (f32[64,128]{1,0:T(8,128)S(1)}, f32[64,128]{1,0:T(8,128)S(1)}, u32[]{:S(2)}, u32[]{:S(2)}) collective-permute-start(f32[64,128]{1,0:T(8,128)S(1)} %pad_maximum_fusion.5), channel_id=1, source_target_pairs={{0,64},{4,68},{8,72},{12,76},{16,80},{20,84},{24,88},{28,92},{32,9... | collective-permute-start | bytes 98312 | tf_op jit(solution)/shard_map/ppermute | solution.py:423
  19.3 6.7 %copy-start = (f32[32,128]{1,0:T(8,128)S(1)}, f32[32,128]{1,0:T(8,128)}, u32[]{:S(2)}) copy-start(f32[32,128]{1,0:T(8,128)} %get-tuple-element.9) | copy-start | bytes 49156
  19.3 6.7 %collective-permute-start.2 = (f32[128,128]{1,0:T(8,128)S(1)}, f32[128,128]{1,0:T(8,128)S(1)}, u32[]{:S(2)}, u32[]{:S(2)}) collective-permute-start(f32[128,128]{1,0:T(8,128)S(1)} %pad_maximum_fusion.4), channel_id=1, source_target_pairs={{0,32},{4,36},{8,40},{12,44},{16,48},{20,52},{24,56},{28,60},{32,0... | collective-permute-start | bytes 196616 | tf_op jit(solution)/shard_map/ppermute | solution.py:423
  25.9 39.6 %all-to-all-start = ((f32[64,32,128]{2,1,0:T(8,128)}), f32[64,32,128]{2,1,0:T(8,128)S(1)}, u32[]{:S(2)}, u32[]{:S(2)}) async-start(f32[64,32,128]{2,1,0:T(8,128)} %bitcast.16), calls=%async_computation | async-start | bytes 2097152 | tf_op jit(solution)/shard_map/all_to_all | solution.py:440
  36.7 9.3 %collective-permute-start.3 = (f32[256,128]{1,0:T(8,128)S(1)}, f32[256,128]{1,0:T(8,128)S(1)}, u32[]{:S(2)}, u32[]{:S(2)}) collective-permute-start(f32[256,128]{1,0:T(8,128)S(1)} %pad_maximum_fusion.3), channel_id=1, source_target_pairs={{0,16},{4,20},{8,24},{12,28},{16,0},{20,4},{24,8},{28,12},{32,48},... | collective-permute-start | bytes 393224 | tf_op jit(solution)/shard_map/ppermute | solution.py:423
  46.1 10.8 %collective-permute-start.4 = (f32[512,128]{1,0:T(8,128)S(1)}, f32[512,128]{1,0:T(8,128)S(1)}, u32[]{:S(2)}, u32[]{:S(2)}) collective-permute-start(f32[512,128]{1,0:T(8,128)S(1)} %pad_maximum_fusion.2), channel_id=1, source_target_pairs={{0,8},{4,12},{8,0},{12,4},{16,24},{20,28},{24,16},{28,20},{32,40},... | collective-permute-start | bytes 786440 | tf_op jit(solution)/shard_map/ppermute | solution.py:423
  56.9 2.2 %collective-permute-start.5 = (f32[1024,128]{1,0:T(8,128)S(1)}, f32[1024,128]{1,0:T(8,128)S(1)}, u32[]{:S(2)}, u32[]{:S(2)}) collective-permute-start(f32[1024,128]{1,0:T(8,128)S(1)} %pad_maximum_fusion.1), channel_id=1, source_target_pairs={{0,4},{4,0},{8,12},{12,8},{16,20},{20,16},{24,28},{28,24},{32,36},... | collective-permute-start | bytes 1572872 | tf_op jit(solution)/shard_map/ppermute | solution.py:423
  105.4 20.5 %all-to-all-start.1 = ((f32[64,8,128]{2,1,0:T(8,128)}), f32[64,8,128]{2,1,0:T(8,128)S(1)}, u32[]{:S(2)}, u32[]{:S(2)}) async-start(f32[64,8,128]{2,1,0:T(8,128)} %bitcast.3), calls=%async_computation.1 | async-start | bytes 524288 | tf_op jit(solution)/shard_map/all_to_all | solution.py:482

commit v10 on v7

--- a/solution.py
+++ b/solution.py
@@ -9,12 +9,12 @@
 
 F32 = jnp.float32
 BF16 = jnp.bfloat16
-SPREAD_UNROLL = 8
-GATHER_UNROLL = 8
-FINISH_UNROLL = 4
-LAST_UNROLL = 4
-EDGE_UNROLL = 8
-LEAF_UNROLL = 4
+SPREAD_UNROLL = 16
+GATHER_UNROLL = 32
+FINISH_UNROLL = 8
+LAST_UNROLL = 8
+EDGE_UNROLL = 16
+LEAF_UNROLL = 8
 LANES = 128
 GROUP = 4
 
@@ -31,7 +31,7 @@
 
 
 def slot_kernel(
-    where_ref, dag_ref, weight_ref, length_ref, topo_ref, share_ref, slot_ref, meta_ref,
+    dag_ref, weight_ref, length_ref, topo_ref, share_ref, slot_ref, meta_ref,
     *, levels, owners, node_dev, fields, share_rows,
 ):
     edges = weight_ref.shape[1]
@@ -45,9 +45,9 @@
     meta_ref[...] = jnp.zeros(meta_ref.shape, F32)
     field_row = rows(8)
     for level in range(levels):
-        child = dag_ref[level : level + 1, :] - where_ref[0] * node_dev
-        parent = dag_ref[levels + level : levels + level + 1, :]
-        rotation = dag_ref[2 * levels + level : 2 * levels + level + 1, :]
+        child = dag_ref[0, level : level + 1, :] - lax.axis_index("node") * node_dev
+        parent = dag_ref[1, level : level + 1, :]
+        rotation = dag_ref[2, level : level + 1, :]
         owner_of = parent // node_dev
         code = rotation * node_dev + parent - owner_of * node_dev
         goes = (rows(owners) == owner_of).astype(F32)
@@ -80,19 +80,24 @@
                     field : field + 1, part * LANES : (part + 1) * LANES
                 ]
     row = fields * levels * 2
-    meta_ref[row : row + 1, : topo_ref.shape[1]] = topo_ref[...].astype(F32)
-    share = meta_ref[pl.ds(pl.multiple_of(where_ref[1] * share_rows, share_rows), share_rows), :]
+    use = topo_ref.shape[1]
+    for topology in range(topo_ref.shape[0]):
+        meta_ref[row : row + 1, topology * use : (topology + 1) * use] = topo_ref[
+            topology : topology + 1, :
+        ].astype(F32)
+    place = lax.axis_index("site")
+    share = meta_ref[pl.ds(pl.multiple_of(place * share_rows, share_rows), share_rows), :]
     for owner in range(owners):
         share_ref[owner * share_rows : (owner + 1) * share_rows, :] = share
 
 
 def table_kernel(
-    place_ref, *refs, levels, owners, fields, shares, share_rows, entries,
+    *refs, levels, owners, fields, shares, share_rows, entries,
 ):
     share_refs, (child_ref, table_ref, topo_ref, meta_ref) = refs[:shares], refs[shares:]
     size = owners * share_rows
     for step in range(shares):
-        origin = lax.rem(place_ref[0] + (shares - step), shares)
+        origin = lax.rem(lax.axis_index("site") + (shares - step), shares)
         meta_ref[pl.ds(pl.multiple_of(origin * size, size), size), :] = share_refs[step][...]
 
     def rows_of(row):
@@ -400,25 +405,21 @@
 
     halves = topo_dev // 2
     vmem = pl.BlockSpec(memory_space=pltpu.VMEM)
-    smem = pl.BlockSpec(memory_space=pltpu.SMEM)
     shares = lax.axis_size("site")
     share_rows = -(-(fields * levels * 2 + 1) // (8 * shares)) * 8
-    place = lax.axis_index("site")
     share, slot = pl.pallas_call(
         functools.partial(
             slot_kernel, levels=levels, owners=owners, node_dev=node_dev, fields=fields,
             share_rows=share_rows,
         ),
-        in_specs=[smem] + [vmem] * 4,
+        in_specs=[vmem] * 4,
         out_shape=[
             jax.ShapeDtypeStruct((owners * share_rows, LANES), F32),
             jax.ShapeDtypeStruct((levels, edge_dev), jnp.int32),
         ],
         scratch_shapes=[pltpu.VMEM((share_rows * shares, LANES), F32)],
     )(
-        jnp.stack([device, place]).astype(jnp.int32),
-        dag_edges.transpose(2, 0, 1).reshape(3 * levels, edge_dev), weights, lengths,
-        topo_nodes.reshape(1, -1),
+        dag_edges.transpose(2, 0, 1), weights, lengths, topo_nodes
     )
     share = lax.all_to_all(
         share.reshape(owners, share_rows, LANES), "node",
@@ -434,7 +435,7 @@
             table_kernel, levels=levels, owners=owners, fields=fields, shares=shares,
             share_rows=share_rows, entries=entries,
         ),
-        in_specs=[smem] + [vmem] * shares,
+        in_specs=[vmem] * shares,
         out_shape=[
             jax.ShapeDtypeStruct((owners * share_rows, LANES), F32),
             jax.ShapeDtypeStruct((levels * (fields - 1) * owners, slots), F32),
@@ -442,7 +443,7 @@
         ],
         scratch_shapes=[pltpu.VMEM((owners * share_rows * shares, LANES), F32)],
         compiler_params=pltpu.CompilerParams(vmem_limit_bytes=8 * 1024 * 1024),
-    )(place.astype(jnp.int32).reshape(1), *met)
+    )(*met)
 
     chunk = states // 2 * site_own
     peers = LANES // site_own

time: 136 us -> 125 us (0.919)
  Pallas kernels: 48.4 us -> 40.2 us
    pallas_call x1, Pallas kernels: 39.9 us -> 31.7 us  [on_device(): pl.pallas_call(functools.partial(dag_kernel, levels=levels, owners=owners...]
    reshape x2 -> x0, local copies, waits for them, and re-layouts: 1.91 us -> none  [the longest x1 1.3 us: on_device(): topo_nodes.reshape(1, -1)]
  transfers between devices with their start and end apart: 6 -> 6, of which waited for: 5 -> 5; matrix products, arithmetic and copies ran while one was open for 2% -> 3% of each run, Pallas kernels for 5% -> 5%
where the time goes in v10:
time: 125 us
  Pallas kernels  40.2 us (32%)
  waiting for transfers between devices  37.8 us (30%)
  starting transfers between devices  29.2 us (23%)
  blocking collectives  10.7 us (9%)
  local copies, waits for them, and re-layouts  4.23 us (3%)
  other arithmetic  1.89 us (2%)
    pallas_call x1, Pallas kernels, on_device(): pl.pallas_call(functools.partial(dag_kernel, levels=levels, owners=owners...  31.7 us
    all_to_all x1, starting transfers between devices, on_device(): lax.all_to_all(share.reshape(owners, share_rows, LANES), 'node', split_ax...  12 us
    all_to_all x1, waiting for transfers between devices, on_device(): lax.all_to_all(packed.reshape(owners, chunk, LANES), 'node', split_axis=0...  11.6 us
    psum x1, blocking collectives, on_device(): lax.psum(jnp.sum(shares[:, :slots // LANES + 1], axis=0), 'site')  10.7 us
    all_to_all x1, waiting for transfers between devices, on_device(): lax.all_to_all(partial.reshape(owners, out_rows, LANES), 'node', split_ax...  9.86 us
    ppermute x3, waiting for transfers between devices, on_device(): lax.ppermute(share, 'site', [(k, (k + step) % shares) for k in range(shar...  9.75 us
    all_to_all x1, waiting for transfers between devices, on_device(): lax.all_to_all(share.reshape(owners, share_rows, LANES), 'node', split_ax...  6.57 us
    ppermute x3, starting transfers between devices, on_device(): lax.ppermute(share, 'site', [(k, (k + step) % shares) for k in range(shar...  5.9 us
  transfers between devices with their start and end apart: 6, of which 5 were waited for; matrix products, arithmetic and copies ran while one was open for 3% of the time, Pallas kernels for 5%

profile of v10, /device:TPU:2, one launch (start us, length us, event | category | flops | bytes accessed | tf_op | source)
XLA Modules:
  0.0 124.7 jit_solution(14345757105365021714)
XLA Ops:
  0.6 1.3 %copy.14 = s32[3,192,3]{1,0,2:T(4,128)} copy(s32[3,192,3]{1,2,0:T(4,128)} %param.7) | data formatting | bytes 13824 | tf_op args[1]
  1.9 2.1 %shard_map.78 = (f32[512,128]{1,0:T(8,128)}, s32[3,192]{1,0:T(4,128)}) custom-call(s32[3,3,192]{2,1,0:T(4,128)} %bitcast.24, f32[3,192]{1,0:T(4,128)} %weight_ref.1, f32[3,192]{1,0:T(4,128)} %length_ref.1, s32[4,8]{1,0:T(4,128)} %topo_ref.1), custom_call_target="tpu_custom_call" | custom-call | tf_op jit(solution)/shard_map/pallas_call | solution.py:410
  4.0 12.0 %all-to-all-start.1 = ((f32[64,8,128]{2,1,0:T(8,128)}), f32[64,8,128]{2,1,0:T(8,128)S(1)}, u32[]{:S(2)}, u32[]{:S(2)}) async-start(f32[64,8,128]{2,1,0:T(8,128)} %bitcast.23), calls=%async_computation.1 | async-start | bytes 524288 | tf_op jit(solution)/shard_map/all_to_all | solution.py:424
  16.1 5.7 %shard_map.77 = f32[2048,128]{1,0:T(8,128)} custom-call(f32[64,4,1024]{2,1,0:T(4,128)} %leaf_ref.1), custom_call_target="tpu_custom_call" | custom-call | tf_op jit(solution)/shard_map/pallas_call | solution.py:450
  21.7 6.6 %all-to-all-done.1 = f32[64,8,128]{2,1,0:T(8,128)S(1)} async-done(((f32[64,8,128]{2,1,0:T(8,128)}), f32[64,8,128]{2,1,0:T(8,128)S(1)}, u32[]{:S(2)}, u32[]{:S(2)}) %all-to-all-start.1) | async-done | bytes 262176 | tf_op jit(solution)/shard_map/all_to_all | solution.py:424
  28.3 5.7 %all-to-all-start = ((f32[64,32,128]{2,1,0:T(8,128)}), f32[64,32,128]{2,1,0:T(8,128)S(1)}, u32[]{:S(2)}, u32[]{:S(2)}) async-start(f32[64,32,128]{2,1,0:T(8,128)} %bitcast.22), calls=%async_computation | async-start | bytes 2097152 | tf_op jit(solution)/shard_map/all_to_all | solution.py:457
  33.9 1.7 %collective-permute-start = (f32[512,128]{1,0:T(8,128)S(1)}, f32[512,128]{1,0:T(8,128)S(1)}, u32[]{:S(2)}, u32[]{:S(2)}) collective-permute-start(f32[512,128]{1,0:T(8,128)S(1)} %bitcast.17), channel_id=1, source_target_pairs={{0,1},{1,2},{2,3},{3,0},{4,5},{5,6},{6,7},{7,4},{8,9},{9,10},{10,1... | collective-permute-start | bytes 786440 | tf_op jit(solution)/shard_map/ppermute | solution.py:429
  35.6 2.9 %collective-permute-start.1 = (f32[512,128]{1,0:T(8,128)S(1)}, f32[512,128]{1,0:T(8,128)S(1)}, u32[]{:S(2)}, u32[]{:S(2)}) collective-permute-start(f32[512,128]{1,0:T(8,128)S(1)} %bitcast.18), channel_id=1, source_target_pairs={{0,2},{1,3},{2,0},{3,1},{4,6},{5,7},{6,4},{7,5},{8,10},{9,11},{10,... | collective-permute-start | bytes 786440 | tf_op jit(solution)/shard_map/ppermute | solution.py:429
  38.5 1.4 %collective-permute-start.2 = (f32[512,128]{1,0:T(8,128)S(1)}, f32[512,128]{1,0:T(8,128)S(1)}, u32[]{:S(2)}, u32[]{:S(2)}) collective-permute-start(f32[512,128]{1,0:T(8,128)S(1)} %bitcast.19), channel_id=1, source_target_pairs={{0,3},{1,0},{2,1},{3,2},{4,7},{5,4},{6,5},{7,6},{8,11},{9,8},{10,9... | collective-permute-start | bytes 786440 | tf_op jit(solution)/shard_map/ppermute | solution.py:429
  39.8 0.8 convert_multiply_fusion
  40.6 0.1 broadcast_in_dim_tile.3.scaled_ref
  40.7 3.0 %collective-permute-done.refs_1_ = f32[512,128]{1,0:T(8,128)S(1)} collective-permute-done((f32[512,128]{1,0:T(8,128)S(1)}, f32[512,128]{1,0:T(8,128)S(1)}, u32[]{:S(2)}, u32[]{:S(2)}) %collective-permute-start) | collective-permute-done | bytes 262176 | tf_op jit(solution)/shard_map/ppermute | solution.py:429
  43.6 6.8 %collective-permute-done.1.refs_2_ = f32[512,128]{1,0:T(8,128)S(1)} collective-permute-done((f32[512,128]{1,0:T(8,128)S(1)}, f32[512,128]{1,0:T(8,128)S(1)}, u32[]{:S(2)}, u32[]{:S(2)}) %collective-permute-start.1) | collective-permute-done | bytes 262176 | tf_op jit(solution)/shard_map/ppermute | solution.py:429
  50.4 0.0 collective-permute-done.2.refs_3_
  50.4 0.7 shard_map.79
  51.1 11.6 %all-to-all-done = f32[64,32,128]{2,1,0:T(8,128)S(1)} async-done(((f32[64,32,128]{2,1,0:T(8,128)}), f32[64,32,128]{2,1,0:T(8,128)S(1)}, u32[]{:S(2)}, u32[]{:S(2)}) %all-to-all-start) | async-done | bytes 1048608 | tf_op jit(solution)/shard_map/all_to_all | solution.py:457
  62.7 31.7 %shard_map.80 = f32[512,128]{1,0:T(8,128)} custom-call(f32[2048,128]{1,0:T(8,128)S(1)} %bitcast.16, f32[512,128]{1,0:T(8,128)S(1)} %get-tuple-element.8.child_ref, f32[576,256]{1,0:T(8,128)S(1)} %get-tuple-element.9.table_ref, s32[16,128]{1,0:T(8,128)S(1)} %get-tuple-element.10.topo_ref, f32[1,128]{1,0:T(1,128)S(1)} %broadcast_in_dim_tile.3.scaled_ref), custom_call_target="tpu_custom_call" | custom-call | tf_op jit(solution)/shard_map/pallas_call | solution.py:464
  94.5 5.7 %all-to-all-start.2 = ((f32[64,8,128]{2,1,0:T(8,128)}), f32[64,8,128]{2,1,0:T(8,128)S(1)}, u32[]{:S(2)}, u32[]{:S(2)}) async-start(f32[64,8,128]{2,1,0:T(8,128)} %bitcast.5), calls=%async_computation.2 | async-start | bytes 524288 | tf_op jit(solution)/shard_map/all_to_all | solution.py:482
  100.1 0.7 slice.27
  100.8 0.7 slice.28
  101.5 0.7 slice.29
  102.2 0.3 convert_reduce_fusion
  102.5 9.9 %all-to-all-done.2 = f32[64,8,128]{2,1,0:T(8,128)S(1)} async-done(((f32[64,8,128]{2,1,0:T(8,128)}), f32[64,8,128]{2,1,0:T(8,128)S(1)}, u32[]{:S(2)}, u32[]{:S(2)}) %all-to-all-start.2) | async-done | bytes 262176 | tf_op jit(solution)/shard_map/all_to_all | solution.py:482
  112.4 0.1 slice_reduce_fusion
  112.4 10.7 %psum.7 = f32[3,128]{1,0:T(4,128)S(1)} all-reduce(f32[3,128]{1,0:T(4,128)S(1)} %slice_reduce_fusion), channel_id=1, replica_groups=mesh['node'=64,'site'=4] {'site'}, use_global_device_ids=true, to_apply=%region_1.0 | all-reduce | flops 384 | bytes 3072 | tf_op jit(solution)/shard_map/psum | solution.py:485
  123.2 0.1 slice.25
  123.3 0.1 copy.12
  123.4 0.6 reshape.38
  124.0 0.2 select_reduce_fusion
  124.1 0.6 divide_multiply_fusion
  (3 shorter events, 0.0 us)
Async XLA Ops:
  4.0 24.2 %all-to-all-start.1 = ((f32[64,8,128]{2,1,0:T(8,128)}), f32[64,8,128]{2,1,0:T(8,128)S(1)}, u32[]{:S(2)}, u32[]{:S(2)}) async-start(f32[64,8,128]{2,1,0:T(8,128)} %bitcast.23), calls=%async_computation.1 | async-start | bytes 524288 | tf_op jit(solution)/shard_map/all_to_all | solution.py:424
  28.3 34.5 %all-to-all-start = ((f32[64,32,128]{2,1,0:T(8,128)}), f32[64,32,128]{2,1,0:T(8,128)S(1)}, u32[]{:S(2)}, u32[]{:S(2)}) async-start(f32[64,32,128]{2,1,0:T(8,128)} %bitcast.22), calls=%async_computation | async-start | bytes 2097152 | tf_op jit(solution)/shard_map/all_to_all | solution.py:457
  33.9 9.7 %collective-permute-start = (f32[512,128]{1,0:T(8,128)S(1)}, f32[512,128]{1,0:T(8,128)S(1)}, u32[]{:S(2)}, u32[]{:S(2)}) collective-permute-start(f32[512,128]{1,0:T(8,128)S(1)} %bitcast.17), channel_id=1, source_target_pairs={{0,1},{1,2},{2,3},{3,0},{4,5},{5,6},{6,7},{7,4},{8,9},{9,10},{10,1... | collective-permute-start | bytes 786440 | tf_op jit(solution)/shard_map/ppermute | solution.py:429
  35.6 14.8 %collective-permute-start.1 = (f32[512,128]{1,0:T(8,128)S(1)}, f32[512,128]{1,0:T(8,128)S(1)}, u32[]{:S(2)}, u32[]{:S(2)}) collective-permute-start(f32[512,128]{1,0:T(8,128)S(1)} %bitcast.18), channel_id=1, source_target_pairs={{0,2},{1,3},{2,0},{3,1},{4,6},{5,7},{6,4},{7,5},{8,10},{9,11},{10,... | collective-permute-start | bytes 786440 | tf_op jit(solution)/shard_map/ppermute | solution.py:429
  38.5 12.0 %collective-permute-start.2 = (f32[512,128]{1,0:T(8,128)S(1)}, f32[512,128]{1,0:T(8,128)S(1)}, u32[]{:S(2)}, u32[]{:S(2)}) collective-permute-start(f32[512,128]{1,0:T(8,128)S(1)} %bitcast.19), channel_id=1, source_target_pairs={{0,3},{1,0},{2,1},{3,2},{4,7},{5,4},{6,5},{7,6},{8,11},{9,8},{10,9... | collective-permute-start | bytes 786440 | tf_op jit(solution)/shard_map/ppermute | solution.py:429
  94.5 17.9 %all-to-all-start.2 = ((f32[64,8,128]{2,1,0:T(8,128)}), f32[64,8,128]{2,1,0:T(8,128)S(1)}, u32[]{:S(2)}, u32[]{:S(2)}) async-start(f32[64,8,128]{2,1,0:T(8,128)} %bitcast.5), calls=%async_computation.2 | async-start | bytes 524288 | tf_op jit(solution)/shard_map/all_to_all | solution.py:482

commit v11 on v10

--- a/solution.py
+++ b/solution.py
@@ -9,11 +9,11 @@
 
 F32 = jnp.float32
 BF16 = jnp.bfloat16
-SPREAD_UNROLL = 16
+SPREAD_UNROLL = 32
 GATHER_UNROLL = 32
 FINISH_UNROLL = 8
 LAST_UNROLL = 8
-EDGE_UNROLL = 16
+EDGE_UNROLL = 32
 LEAF_UNROLL = 8
 LANES = 128
 GROUP = 4
@@ -482,12 +482,20 @@
     shares = lax.all_to_all(
         partial.reshape(owners, out_rows, LANES), "node", split_axis=0, concat_axis=0, tiled=True
     )
-    mine = lax.psum(jnp.sum(shares[:, : slots // LANES + 1], axis=0), "site").reshape(-1)
+    mine = jnp.sum(shares[:, : slots // LANES + 1], axis=0)
+    sites = lax.axis_size("site")
+    for bit in range(sites.bit_length() - 1):
+        mine = mine + lax.ppermute(mine, "site", [(k, k ^ (1 << bit)) for k in range(sites)])
+    mine = mine.reshape(-1)
     multiplicity = jnp.sum(
         (topologies.reshape(-1)[None, :] == dag_edges[levels - 1, :, 1][:, None]).astype(F32), axis=1
     )
-    edge_gradient = multiplicity / weights[levels - 1] * jnp.sum(
-        jnp.where(slot[levels - 1][:, None] == jnp.arange(slots)[None, :], mine[None, :slots], 0.0),
+    scale = multiplicity / weights[levels - 1]
+    edge_gradient = jnp.sum(
+        jnp.where(
+            slot[levels - 1][:, None] == jnp.arange(slots)[None, :],
+            mine[None, :slots] * scale[:, None], 0.0,
+        ),
         axis=1,
     )
     topology = mine[slots : slots + 16].reshape(2, 8)[:, :halves].T.reshape(-1)

time: 125 us -> 122 us (0.976)
  waiting for transfers between devices: 37.8 us -> 29.7 us
  blocking collectives: 10.7 us -> 17.7 us
  Pallas kernels: 40.2 us -> 38.4 us
    all_to_all x0 -> x1, blocking collectives: none -> 17.7 us  [on_device(): lax.all_to_all(partial.reshape(owners, out_rows, LANES), 'node', split_ax...]
    psum x1 -> x0, blocking collectives: 10.7 us -> none  [on_device(): lax.psum(jnp.sum(shares[:, :slots // LANES + 1], axis=0), 'site')]
    all_to_all x1 -> x0, waiting for transfers between devices: 9.86 us -> none  [on_device(): lax.all_to_all(partial.reshape(owners, out_rows, LANES), 'node', split_ax...]
    all_to_all x1 -> x0, starting transfers between devices: 5.66 us -> none  [on_device(): lax.all_to_all(partial.reshape(owners, out_rows, LANES), 'node', split_ax...]
    ppermute x0 -> x2, starting transfers between devices: none -> 4.79 us  [on_device(): lax.ppermute(mine, 'site', [(k, k ^ 1 << bit) for k in range(sites)])]
    pallas_call x1, Pallas kernels: 31.7 us -> 29.9 us  [on_device(): pl.pallas_call(functools.partial(dag_kernel, levels=levels, owners=owners...]
    ppermute x0 -> x2, waiting for transfers between devices: none -> 1.74 us  [on_device(): lax.ppermute(mine, 'site', [(k, k ^ 1 << bit) for k in range(sites)])]
  transfers between devices with their start and end apart: 6 -> 7, of which waited for: 5 -> 5; matrix products, arithmetic and copies ran while one was open for 3% -> 3% of each run, Pallas kernels for 5% -> 5%
where the time goes in v11:
time: 122 us; the launch traced here: 121 us
  Pallas kernels  38.4 us (31%)
  waiting for transfers between devices  29.7 us (24%)
  starting transfers between devices  28.4 us (23%)
  blocking collectives  17.7 us (15%)
  local copies, waits for them, and re-layouts  4.24 us (3%)
  other arithmetic  1.92 us (2%)
    pallas_call x1, Pallas kernels, on_device(): pl.pallas_call(functools.partial(dag_kernel, levels=levels, owners=owners...  29.9 us
    all_to_all x1, blocking collectives, on_device(): lax.all_to_all(partial.reshape(owners, out_rows, LANES), 'node', split_ax...  17.7 us
    all_to_all x1, starting transfers between devices, on_device(): lax.all_to_all(share.reshape(owners, share_rows, LANES), 'node', split_ax...  12 us
    all_to_all x1, waiting for transfers between devices, on_device(): lax.all_to_all(packed.reshape(owners, chunk, LANES), 'node', split_axis=0...  11.6 us
    ppermute x3, waiting for transfers between devices, on_device(): lax.ppermute(share, 'site', [(k, (k + step) % shares) for k in range(shar...  9.75 us
    all_to_all x1, waiting for transfers between devices, on_device(): lax.all_to_all(share.reshape(owners, share_rows, LANES), 'node', split_ax...  6.56 us
    ppermute x3, starting transfers between devices, on_device(): lax.ppermute(share, 'site', [(k, (k + step) % shares) for k in range(shar...  5.9 us
    pallas_call x1, Pallas kernels, on_device(): pl.pallas_call(functools.partial(pack_kernel, site_own=site_own), grid=(s...  5.66 us
  transfers between devices with their start and end apart: 7, of which 5 were waited for; matrix products, arithmetic and copies ran while one was open for 3% of the time, Pallas kernels for 5%

profile of v11, /device:TPU:2, one launch (start us, length us, event | category | flops | bytes accessed | tf_op | source)
XLA Modules:
  0.0 120.9 jit_solution(11212813097539086120)
XLA Ops:
  0.6 1.3 %copy.14 = s32[3,192,3]{1,0,2:T(4,128)} copy(s32[3,192,3]{1,2,0:T(4,128)} %param.7) | data formatting | bytes 13824 | tf_op args[1]
  1.9 2.1 %shard_map.78 = (f32[512,128]{1,0:T(8,128)}, s32[3,192]{1,0:T(4,128)}) custom-call(s32[3,3,192]{2,1,0:T(4,128)} %bitcast.25, f32[3,192]{1,0:T(4,128)} %weight_ref.1, f32[3,192]{1,0:T(4,128)} %length_ref.1, s32[4,8]{1,0:T(4,128)} %topo_ref.1), custom_call_target="tpu_custom_call" | custom-call | tf_op jit(solution)/shard_map/pallas_call | solution.py:410
  4.0 12.0 %all-to-all-start.1 = ((f32[64,8,128]{2,1,0:T(8,128)}), f32[64,8,128]{2,1,0:T(8,128)S(1)}, u32[]{:S(2)}, u32[]{:S(2)}) async-start(f32[64,8,128]{2,1,0:T(8,128)} %bitcast.24), calls=%async_computation.1 | async-start | bytes 524288 | tf_op jit(solution)/shard_map/all_to_all | solution.py:424
  16.0 5.7 %shard_map.77 = f32[2048,128]{1,0:T(8,128)} custom-call(f32[64,4,1024]{2,1,0:T(4,128)} %leaf_ref.1), custom_call_target="tpu_custom_call" | custom-call | tf_op jit(solution)/shard_map/pallas_call | solution.py:450
  21.7 6.6 %all-to-all-done.1 = f32[64,8,128]{2,1,0:T(8,128)S(1)} async-done(((f32[64,8,128]{2,1,0:T(8,128)}), f32[64,8,128]{2,1,0:T(8,128)S(1)}, u32[]{:S(2)}, u32[]{:S(2)}) %all-to-all-start.1) | async-done | bytes 262176 | tf_op jit(solution)/shard_map/all_to_all | solution.py:424
  28.3 5.7 %all-to-all-start = ((f32[64,32,128]{2,1,0:T(8,128)}), f32[64,32,128]{2,1,0:T(8,128)S(1)}, u32[]{:S(2)}, u32[]{:S(2)}) async-start(f32[64,32,128]{2,1,0:T(8,128)} %bitcast.23), calls=%async_computation | async-start | bytes 2097152 | tf_op jit(solution)/shard_map/all_to_all | solution.py:457
  33.9 1.7 %collective-permute-start = (f32[512,128]{1,0:T(8,128)S(1)}, f32[512,128]{1,0:T(8,128)S(1)}, u32[]{:S(2)}, u32[]{:S(2)}) collective-permute-start(f32[512,128]{1,0:T(8,128)S(1)} %bitcast.18), channel_id=1, source_target_pairs={{0,1},{1,2},{2,3},{3,0},{4,5},{5,6},{6,7},{7,4},{8,9},{9,10},{10,1... | collective-permute-start | bytes 786440 | tf_op jit(solution)/shard_map/ppermute | solution.py:429
  35.6 2.9 %collective-permute-start.1 = (f32[512,128]{1,0:T(8,128)S(1)}, f32[512,128]{1,0:T(8,128)S(1)}, u32[]{:S(2)}, u32[]{:S(2)}) collective-permute-start(f32[512,128]{1,0:T(8,128)S(1)} %bitcast.19), channel_id=1, source_target_pairs={{0,2},{1,3},{2,0},{3,1},{4,6},{5,7},{6,4},{7,5},{8,10},{9,11},{10,... | collective-permute-start | bytes 786440 | tf_op jit(solution)/shard_map/ppermute | solution.py:429
  38.5 1.4 %collective-permute-start.2 = (f32[512,128]{1,0:T(8,128)S(1)}, f32[512,128]{1,0:T(8,128)S(1)}, u32[]{:S(2)}, u32[]{:S(2)}) collective-permute-start(f32[512,128]{1,0:T(8,128)S(1)} %bitcast.20), channel_id=1, source_target_pairs={{0,3},{1,0},{2,1},{3,2},{4,7},{5,4},{6,5},{7,6},{8,11},{9,8},{10,9... | collective-permute-start | bytes 786440 | tf_op jit(solution)/shard_map/ppermute | solution.py:429
  39.8 0.8 convert_multiply_fusion
  40.6 0.1 broadcast_in_dim_tile.3.scaled_ref
  40.7 3.0 %collective-permute-done.refs_1_ = f32[512,128]{1,0:T(8,128)S(1)} collective-permute-done((f32[512,128]{1,0:T(8,128)S(1)}, f32[512,128]{1,0:T(8,128)S(1)}, u32[]{:S(2)}, u32[]{:S(2)}) %collective-permute-start) | collective-permute-done | bytes 262176 | tf_op jit(solution)/shard_map/ppermute | solution.py:429
  43.6 6.8 %collective-permute-done.1.refs_2_ = f32[512,128]{1,0:T(8,128)S(1)} collective-permute-done((f32[512,128]{1,0:T(8,128)S(1)}, f32[512,128]{1,0:T(8,128)S(1)}, u32[]{:S(2)}, u32[]{:S(2)}) %collective-permute-start.1) | collective-permute-done | bytes 262176 | tf_op jit(solution)/shard_map/ppermute | solution.py:429
  50.4 0.0 collective-permute-done.2.refs_3_
  50.4 0.7 shard_map.79
  51.1 11.6 %all-to-all-done = f32[64,32,128]{2,1,0:T(8,128)S(1)} async-done(((f32[64,32,128]{2,1,0:T(8,128)}), f32[64,32,128]{2,1,0:T(8,128)S(1)}, u32[]{:S(2)}, u32[]{:S(2)}) %all-to-all-start) | async-done | bytes 1048608 | tf_op jit(solution)/shard_map/all_to_all | solution.py:457
  62.7 29.9 %shard_map.80 = f32[512,128]{1,0:T(8,128)S(1)} custom-call(f32[2048,128]{1,0:T(8,128)S(1)} %bitcast.16, f32[512,128]{1,0:T(8,128)S(1)} %get-tuple-element.8.child_ref, f32[576,256]{1,0:T(8,128)S(1)} %get-tuple-element.9.table_ref, s32[16,128]{1,0:T(8,128)S(1)} %get-tuple-element.10.topo_ref, f32[1,128]{1,0:T(1,128)S(1)} %broadcast_in_dim_tile.3.scaled_ref), custom_call_target="tpu_custom_call" | custom-call | tf_op jit(solution)/shard_map/pallas_call | solution.py:464
  92.7 17.7 %all_to_all.15 = f32[64,8,128]{2,1,0:T(8,128)S(1)} all-to-all(f32[64,8,128]{2,1,0:T(8,128)S(1)} %bitcast.17), channel_id=1, replica_groups=mesh['node'=64,'site'=4] {'node'}, dimensions={0} | all-to-all | bytes 524288 | tf_op jit(solution)/shard_map/all_to_all | solution.py:482
  110.3 0.1 slice_reduce_fusion
  110.4 1.7 %collective-permute-start.3 = (f32[3,128]{1,0:T(4,128)S(1)}, f32[3,128]{1,0:T(4,128)S(1)}, u32[]{:S(2)}, u32[]{:S(2)}) collective-permute-start(f32[3,128]{1,0:T(4,128)S(1)} %slice_reduce_fusion), channel_id=1, source_target_pairs={{0,1},{1,0},{2,3},{3,2},{4,5},{5,4},{6,7},{7,6},{8,9},{9,8},{10,11... | collective-permute-start | bytes 4616 | tf_op jit(solution)/shard_map/ppermute | solution.py:488
  112.1 0.7 slice.29
  112.8 0.7 slice.30
  113.4 0.7 slice.27
  114.1 0.0 collective-permute-done.3
  114.1 3.1 %collective-permute-start.4 = (f32[3,128]{1,0:T(4,128)S(1)}, f32[3,128]{1,0:T(4,128)S(1)}, u32[]{:S(2)}, u32[]{:S(2)}) collective-permute-start(f32[3,128]{1,0:T(4,128)S(1)} %add.10), channel_id=1, source_target_pairs={{0,2},{1,3},{2,0},{3,1},{4,6},{5,7},{6,4},{7,5},{8,10},{9,11},{10,... | collective-permute-start | bytes 4616 | tf_op jit(solution)/shard_map/ppermute | solution.py:488
  117.3 0.3 convert_reduce_fusion
  117.6 1.7 %collective-permute-done.4 = f32[3,128]{1,0:T(4,128)S(1)} collective-permute-done((f32[3,128]{1,0:T(4,128)S(1)}, f32[3,128]{1,0:T(4,128)S(1)}, u32[]{:S(2)}, u32[]{:S(2)}) %collective-permute-start.4) | collective-permute-done | bytes 1568 | tf_op jit(solution)/shard_map/ppermute | solution.py:488
  119.3 0.1 slice.25
  119.4 0.1 copy.12
  119.5 0.6 reshape.45
  120.1 0.8 select_reduce_fusion
  (6 shorter events, 0.0 us)
Async XLA Ops:
  4.0 24.2 %all-to-all-start.1 = ((f32[64,8,128]{2,1,0:T(8,128)}), f32[64,8,128]{2,1,0:T(8,128)S(1)}, u32[]{:S(2)}, u32[]{:S(2)}) async-start(f32[64,8,128]{2,1,0:T(8,128)} %bitcast.24), calls=%async_computation.1 | async-start | bytes 524288 | tf_op jit(solution)/shard_map/all_to_all | solution.py:424
  28.3 34.5 %all-to-all-start = ((f32[64,32,128]{2,1,0:T(8,128)}), f32[64,32,128]{2,1,0:T(8,128)S(1)}, u32[]{:S(2)}, u32[]{:S(2)}) async-start(f32[64,32,128]{2,1,0:T(8,128)} %bitcast.23), calls=%async_computation | async-start | bytes 2097152 | tf_op jit(solution)/shard_map/all_to_all | solution.py:457
  33.9 9.7 %collective-permute-start = (f32[512,128]{1,0:T(8,128)S(1)}, f32[512,128]{1,0:T(8,128)S(1)}, u32[]{:S(2)}, u32[]{:S(2)}) collective-permute-start(f32[512,128]{1,0:T(8,128)S(1)} %bitcast.18), channel_id=1, source_target_pairs={{0,1},{1,2},{2,3},{3,0},{4,5},{5,6},{6,7},{7,4},{8,9},{9,10},{10,1... | collective-permute-start | bytes 786440 | tf_op jit(solution)/shard_map/ppermute | solution.py:429
  35.6 14.8 %collective-permute-start.1 = (f32[512,128]{1,0:T(8,128)S(1)}, f32[512,128]{1,0:T(8,128)S(1)}, u32[]{:S(2)}, u32[]{:S(2)}) collective-permute-start(f32[512,128]{1,0:T(8,128)S(1)} %bitcast.19), channel_id=1, source_target_pairs={{0,2},{1,3},{2,0},{3,1},{4,6},{5,7},{6,4},{7,5},{8,10},{9,11},{10,... | collective-permute-start | bytes 786440 | tf_op jit(solution)/shard_map/ppermute | solution.py:429
  38.5 12.0 %collective-permute-start.2 = (f32[512,128]{1,0:T(8,128)S(1)}, f32[512,128]{1,0:T(8,128)S(1)}, u32[]{:S(2)}, u32[]{:S(2)}) collective-permute-start(f32[512,128]{1,0:T(8,128)S(1)} %bitcast.20), channel_id=1, source_target_pairs={{0,3},{1,0},{2,1},{3,2},{4,7},{5,4},{6,5},{7,6},{8,11},{9,8},{10,9... | collective-permute-start | bytes 786440 | tf_op jit(solution)/shard_map/ppermute | solution.py:429
  110.4 3.7 %collective-permute-start.3 = (f32[3,128]{1,0:T(4,128)S(1)}, f32[3,128]{1,0:T(4,128)S(1)}, u32[]{:S(2)}, u32[]{:S(2)}) collective-permute-start(f32[3,128]{1,0:T(4,128)S(1)} %slice_reduce_fusion), channel_id=1, source_target_pairs={{0,1},{1,0},{2,3},{3,2},{4,5},{5,4},{6,7},{7,6},{8,9},{9,8},{10,11... | collective-permute-start | bytes 4616 | tf_op jit(solution)/shard_map/ppermute | solution.py:488
  114.1 5.2 %collective-permute-start.4 = (f32[3,128]{1,0:T(4,128)S(1)}, f32[3,128]{1,0:T(4,128)S(1)}, u32[]{:S(2)}, u32[]{:S(2)}) collective-permute-start(f32[3,128]{1,0:T(4,128)S(1)} %add.10), channel_id=1, source_target_pairs={{0,2},{1,3},{2,0},{3,1},{4,6},{5,7},{6,4},{7,5},{8,10},{9,11},{10,... | collective-permute-start | bytes 4616 | tf_op jit(solution)/shard_map/ppermute | solution.py:488
